TPU v7x, 128 devices: a whole 4x4x4 slice. The times are simulated.
128 devices in a mesh: dp: 16 (over y_lo, x, core), seq: 8 (over z, y_hi).
Axes of the slice: x: 4, y: 4 (y_hi: 2, y_lo: 2; y = y_hi * 2 + y_lo), z: 4, core: 2. Of those that a mesh axis runs over, the one named last changes fastest.
Arguments:
- query_input: bfloat16 [16, 1024, 2048], P('dp', 'seq'), may hold values from -6 to 6
- key_input: bfloat16 [16, 1024, 2048], P('dp', 'seq'), may hold values from -6 to 6
- value_input: bfloat16 [16, 1024, 2048], P('dp', 'seq'), may hold values from -6 to 6
- out_weight: bfloat16 [2048, 4096], P(None, 'dp'), may hold values from -0.125 to 0.125
- grad_out: bfloat16 [16, 1024, 4096], P('dp', 'seq'), may hold values from -6 to 6
Outputs:
- projected: bfloat16 [16, 1024, 4096], P('dp', 'seq')
- grad_query: bfloat16 [16, 1024, 2048], P('dp', None, 'seq')
- grad_key: bfloat16 [16, 1024, 2048], P('dp', None, 'seq')
- grad_value: bfloat16 [16, 1024, 2048], P('dp', None, 'seq')
- grad_weight: float32 [2048, 4096], P('seq', 'dp')
All inputs are finite; a program needn't handle non-finite values.
Results may differ from a plain program's by a relative error of at most 0.022.
Values may be sent and summed in bfloat16 or wider, within the bound.
No kernel may reach another device: no remote copies, remote signals or barrier semaphores. Data moves between devices by JAX's collectives and lax.ppermute only.
A program may use at most 128 MiB of HBM per device.

v0:
```python
import jax
import jax.numpy as jnp
from jax import lax
from jax.experimental import pallas as pl
from jax.experimental.pallas import tpu as pltpu
from jax.sharding import PartitionSpec as P

HEAD = 128
X = 4
BLOCK = 256
SCALE = HEAD ** (-0.5)
MIB = 1 << 20


def params(mib):
    return pltpu.CompilerParams(vmem_limit_bytes=mib * MIB)


def cost(flops, size, trans=0):
    return pl.CostEstimate(flops=flops, bytes_accessed=size, transcendentals=trans)


def nt(a, b):
    return lax.dot_general(a, b, (((1,), (1,)), ((), ())), preferred_element_type=jnp.float32)


def tn(a, b):
    return lax.dot_general(a, b, (((0,), (0,)), ((), ())), preferred_element_type=jnp.float32)


def run_copies(pairs, sems):
    copies = [pltpu.make_async_copy(a, b, sems.at[i]) for i, (a, b) in enumerate(pairs)]
    for copy in copies:
        copy.start()
    for copy in copies:
        copy.wait()


ANY = pl.BlockSpec(memory_space=pl.ANY)


def place():
    me = lax.axis_index("dp")
    return me // (2 * X), (me // 2) % X, me % 2


def column_of(yl, x, core, j):
    other_y, other_core = j // 2, j % 2
    yy = yl + other_y - 2 * yl * other_y
    cc = core + other_core - 2 * core * other_core
    return pl.multiple_of(((yy * X + x) * 2 + cc) * BLOCK, BLOCK)


def pack_qkv(query, key, value):
    tok, feat = query.shape
    groups = feat // BLOCK

    def body(q, k, v, out, sems):
        run_copies(
            [
                (src.at[:, pl.ds(g * BLOCK, BLOCK)], out.at[g, i])
                for g in range(groups)
                for i, src in enumerate((q, k, v))
            ],
            sems,
        )

    return pl.pallas_call(
        body,
        out_shape=jax.ShapeDtypeStruct((groups, 3, tok, BLOCK), query.dtype),
        in_specs=[ANY] * 3,
        out_specs=ANY,
        scratch_shapes=[pltpu.SemaphoreType.DMA((groups * 3,))],
        cost_estimate=cost(0, 3 * 2 * 2 * tok * feat),
        name="pack_qkv",
    )(query, key, value)


def pack_grad(grad):
    tok, cols = grad.shape

    def body(src, *rest):
        outs, sems = rest[:X], rest[X]
        yl, x, core = place()
        run_copies(
            [
                (
                    src.at[:, pl.ds(column_of(yl, (x + s) % X, core, j), BLOCK)],
                    outs[s].at[:, pl.ds(j * BLOCK, BLOCK)],
                )
                for s in range(X)
                for j in range(4)
            ],
            sems,
        )

    return pl.pallas_call(
        body,
        out_shape=[jax.ShapeDtypeStruct((tok, 4 * BLOCK), grad.dtype)] * X,
        in_specs=[ANY],
        out_specs=[ANY] * X,
        scratch_shapes=[pltpu.SemaphoreType.DMA((16,))],
        cost_estimate=cost(0, 4 * tok * cols),
        name="pack_grad",
    )(grad)


def place_projected(parts, cols):
    tok = parts[0].shape[0]

    def body(*refs):
        srcs, out, sems = refs[:X], refs[X], refs[X + 1]
        yl, x, core = place()
        run_copies(
            [
                (
                    srcs[s].at[:, pl.ds(j * BLOCK, BLOCK)],
                    out.at[:, pl.ds(column_of(yl, (x + s) % X, core, j), BLOCK)],
                )
                for s in range(X)
                for j in range(4)
            ],
            sems,
        )

    return pl.pallas_call(
        body,
        out_shape=jax.ShapeDtypeStruct((tok, cols), parts[0].dtype),
        in_specs=[ANY] * X,
        out_specs=ANY,
        scratch_shapes=[pltpu.SemaphoreType.DMA((16,))],
        cost_estimate=cost(0, 4 * tok * cols),
        name="place_projected",
    )(*parts)


def head_spec(groups, tok, i):
    return pl.BlockSpec((groups, pl.squeezed, tok, HEAD), lambda h: (0, i, 0, h))


def attend(qkv):
    groups, _, tok, width = qkv.shape
    heads, length = width // HEAD, groups * tok
    rows = 256

    def body(q_ref, k_ref, v_ref, o_ref, lse_ref):
        keys = k_ref[...].reshape(length, HEAD)
        values = v_ref[...].reshape(length, HEAD)
        for b in range(length // rows):
            per = rows // tok
            query = q_ref[b * per : (b + 1) * per].reshape(rows, HEAD)
            scores = nt(keys, query) * SCALE
            peak = jnp.max(scores, axis=0, keepdims=True)
            shifted = jnp.exp(scores - peak)
            total = jnp.sum(shifted, axis=0, keepdims=True)
            out = tn(values, shifted.astype(jnp.bfloat16)) / total
            o_ref[b * per : (b + 1) * per] = out.T.astype(jnp.bfloat16).reshape(per, tok, HEAD)
            lse_ref[:, b * rows : (b + 1) * rows] = peak + jnp.log(total)

    return pl.pallas_call(
        body,
        grid=(heads,),
        out_shape=[
            jax.ShapeDtypeStruct((groups, tok, width), jnp.bfloat16),
            jax.ShapeDtypeStruct((heads, 1, length), jnp.float32),
        ],
        in_specs=[head_spec(groups, tok, i) for i in range(3)],
        out_specs=[
            pl.BlockSpec((groups, tok, HEAD), lambda h: (0, 0, h)),
            pl.BlockSpec((pl.squeezed, 1, length), lambda h: (h, 0, 0)),
        ],
        compiler_params=params(32),
        cost_estimate=cost(8 * heads * length * length * HEAD, 8 * length * width, heads * length * length),
        name="attend",
    )(qkv, qkv, qkv)


def attend_back(qkv, lse, grad):
    groups, _, tok, width = qkv.shape
    heads, length = width // HEAD, groups * tok
    rows = 256

    def body(q_ref, k_ref, v_ref, lse_ref, g_ref, dq_ref, dk_ref, dv_ref, k_acc, v_acc):
        keys = k_ref[...].reshape(length, HEAD)
        values = v_ref[...].reshape(length, HEAD)
        for b in range(length // rows):
            per = rows // tok
            query = q_ref[b * per : (b + 1) * per].reshape(rows, HEAD)
            grad_rows = g_ref[b * per : (b + 1) * per].reshape(rows, HEAD)
            scores = nt(keys, query) * SCALE
            probs = jnp.exp(scores - lse_ref[:, b * rows : (b + 1) * rows])
            grad_probs = nt(values, grad_rows)
            delta = jnp.sum(probs * grad_probs, axis=0, keepdims=True)
            grad_scores = (probs * (grad_probs - delta)).astype(jnp.bfloat16)
            dv = jnp.dot(probs.astype(jnp.bfloat16), grad_rows, preferred_element_type=jnp.float32)
            dk = jnp.dot(grad_scores, query, preferred_element_type=jnp.float32)
            if b == 0:
                v_acc[...] = dv
                k_acc[...] = dk
            else:
                v_acc[...] += dv
                k_acc[...] += dk
            dq = tn(keys, grad_scores) * SCALE
            dq_ref[b * rows : (b + 1) * rows, :] = dq.T.astype(jnp.bfloat16)
        dk_ref[...] = (k_acc[...] * SCALE).astype(jnp.bfloat16)
        dv_ref[...] = v_acc[...].astype(jnp.bfloat16)

    out = jax.ShapeDtypeStruct((length, width), jnp.bfloat16)
    return pl.pallas_call(
        body,
        grid=(heads,),
        out_shape=[out] * 3,
        in_specs=[head_spec(groups, tok, i) for i in range(3)]
        + [
            pl.BlockSpec((pl.squeezed, 1, length), lambda h: (h, 0, 0)),
            pl.BlockSpec((groups, tok, HEAD), lambda h: (0, 0, h)),
        ],
        out_specs=[pl.BlockSpec((length, HEAD), lambda h: (0, h))] * 3,
        scratch_shapes=[pltpu.VMEM((length, HEAD), jnp.float32)] * 2,
        compiler_params=params(40),
        cost_estimate=cost(20 * heads * length * length * HEAD, 14 * length * width, heads * length * length),
        name="attend_back",
    )(qkv, qkv, qkv, lse, grad)


def grad_attended_parts(grads, weights):
    tok, width = grads[0].shape
    feat, block = weights[0].shape
    groups = feat // BLOCK

    def body(*refs):
        g_refs, w_refs, outs = refs[:X], refs[X : X + 4], refs[X + 4 :]
        total = None
        for j in range(4):
            cols = jnp.concatenate([g[:, j * block : (j + 1) * block] for g in g_refs], axis=0)
            term = nt(cols, w_refs[j][...])
            total = term if total is None else total + term
        total = total.astype(jnp.bfloat16)
        for s in range(X):
            outs[s][...] = total[s * tok : (s + 1) * tok]

    return pl.pallas_call(
        body,
        grid=(groups,),
        out_shape=[jax.ShapeDtypeStruct((groups, tok, BLOCK), jnp.bfloat16)] * X,
        in_specs=[pl.BlockSpec((tok, width), lambda n: (0, 0))] * X
        + [pl.BlockSpec((BLOCK, block), lambda n: (n, 0))] * 4,
        out_specs=[pl.BlockSpec((pl.squeezed, tok, BLOCK), lambda n: (n, 0, 0))] * X,
        compiler_params=params(32),
        cost_estimate=cost(2 * X * tok * width * feat, 2 * feat * width + 4 * X * tok * width),
        name="grad_attended",
    )(*grads, *weights)


def project(attended, grads, weights):
    groups, tok, block = attended[0].shape
    width = grads[0].shape[1]

    def body(*refs):
        a_refs, g_refs, w_refs = refs[:X], refs[X : 2 * X], refs[2 * X : 2 * X + 4]
        outs, near, far, acc = refs[2 * X + 4 : 3 * X + 4], *refs[3 * X + 4 :]
        n = pl.program_id(0)
        rows = jnp.concatenate([a[...] for a in a_refs], axis=0)
        for j in range(4):
            cols = slice(j * block, (j + 1) * block)
            term = jnp.dot(rows, w_refs[j][...], preferred_element_type=jnp.float32)

            @pl.when(n == 0)
            def _():
                acc[:, cols] = term

            @pl.when(n > 0)
            def _():
                acc[:, cols] += term

            grad_cols = jnp.concatenate([g[:, cols] for g in g_refs], axis=0)
            piece = tn(rows, grad_cols).astype(jnp.bfloat16)
            (near, far)[j % 2][j // 2] = piece

        @pl.when(n == groups - 1)
        def _():
            for s in range(X):
                outs[s][...] = acc[s * tok : (s + 1) * tok].astype(jnp.bfloat16)

    return pl.pallas_call(
        body,
        grid=(groups,),
        out_shape=[jax.ShapeDtypeStruct((tok, width), jnp.bfloat16)] * X
        + [jax.ShapeDtypeStruct((groups, 2, block, block), jnp.bfloat16)] * 2,
        in_specs=[pl.BlockSpec((pl.squeezed, tok, block), lambda n: (n, 0, 0))] * X
        + [pl.BlockSpec((tok, width), lambda n: (0, 0))] * X
        + [pl.BlockSpec((block, block), lambda n: (n, 0))] * 4,
        out_specs=[pl.BlockSpec((tok, width), lambda n: (0, 0))] * X
        + [pl.BlockSpec((pl.squeezed, 2, block, block), lambda n: (n, 0, 0, 0))] * 2,
        scratch_shapes=[pltpu.VMEM((X * tok, width), jnp.float32)],
        compiler_params=params(32),
        cost_estimate=cost(4 * X * tok * width * groups * block, 12 * MIB),
        name="project",
    )(*attended, *grads, *weights)


def shift_x(array, shift, count):
    pairs = []
    for d in range(count):
        x = (d // 2) % X
        pairs.append((d, d + 2 * ((x + shift) % X - x)))
    return lax.ppermute(array, "dp", pairs)


def swap(array, bit, count):
    return lax.ppermute(array, "dp", [(d, d ^ bit) for d in range(count)])


def exchange(array):
    return lax.all_to_all(array, "seq", 0, 0, tiled=False)


def f32_sum(*arrays):
    total = arrays[0].astype(jnp.float32)
    for array in arrays[1:]:
        total = total + array.astype(jnp.float32)
    return total


def shards(query_input, key_input, value_input, out_weight, grad_out):
    dp = lax.axis_size("dp")
    cols = grad_out.shape[2]
    qkv = exchange(pack_qkv(query_input[0], key_input[0], value_input[0]))

    mine = pack_grad(grad_out[0])
    grads = [mine[0]] + [shift_x(mine[s], s, dp) for s in range(1, X)]
    far_weight = swap(out_weight, 2 * X, dp)
    weights = [out_weight, swap(out_weight, 1, dp), far_weight, swap(far_weight, 1, dp)]

    parts = grad_attended_parts(grads, weights)
    parts = [parts[0]] + [shift_x(parts[s], -s, dp) for s in range(1, X)]
    grad_attended = exchange(f32_sum(*parts).astype(jnp.bfloat16))

    attended, lse = attend(qkv)
    attended = exchange(attended)
    rows = [attended] + [shift_x(attended, s, dp) for s in range(1, X)]
    *projected, near, far = project(rows, grads, weights)
    projected = [projected[0]] + [shift_x(projected[s], -s, dp) for s in range(1, X)]
    projected = place_projected(projected, cols)[None]

    weight_sum = f32_sum(near, swap(far, 1, dp)).astype(jnp.bfloat16)
    weight_sum = jnp.sum(exchange(weight_sum).astype(jnp.float32), axis=0)
    grad_weight = weight_sum[0] + swap(weight_sum[1].astype(jnp.bfloat16), 2 * X, dp).astype(
        jnp.float32
    )

    grads_in = attend_back(qkv, lse, grad_attended)
    return (projected, *[g[None] for g in grads_in], grad_weight)


def solution(mesh):
    return jax.shard_map(
        shards,
        mesh=mesh,
        in_specs=(
            P("dp", "seq", None),
            P("dp", "seq", None),
            P("dp", "seq", None),
            P(None, "dp"),
            P("dp", "seq", None),
        ),
        out_specs=(
            P("dp", "seq", None),
            P("dp", None, "seq"),
            P("dp", None, "seq"),
            P("dp", None, "seq"),
            P("seq", "dp"),
        ),
        check_vma=False,
    )
```

profile of v0, /device:TPU:0, one launch (start us, length us, event | category | flops | bytes accessed | tf_op | source)
XLA Modules:
  0.0 311.0 jit_solution(3388479527761777362)
XLA Ops:
  0.6 49.0 %pack_qkv.1 = bf16[8,3,128,256]{3,2,1,0:T(8,128)(2,1)} custom-call(bf16[128,2048]{1,0:T(8,128)(2,1)} %bitcast.16, bf16[128,2048]{1,0:T(8,128)(2,1)} %bitcast.17, bf16[128,2048]{1,0:T(8,128)(2,1)} %bitcast.18), custom_call_target="tpu_custom_call" | custom-call | bytes 3145728 | tf_op jit(solution)/shard_map/pack_qkv/pallas_call | solution.py:68
  49.6 8.2 %all-to-all-start = ((bf16[8,3,128,256]{3,2,1,0:T(8,128)(2,1)}), bf16[8,3,128,256]{3,2,1,0:T(8,128)(2,1)S(1)}, u32[]{:S(2)}, u32[]{:S(2)}) async-start(bf16[8,3,128,256]{3,2,1,0:T(8,128)(2,1)} %pack_qkv.1), calls=%async_computation | async-start | bytes 3145728 | tf_op jit(solution)/shard_map/all_to_all | solution.py:315
  57.8 0.8 collective-permute-start.7
  58.6 40.0 %collective-permute-done.7.refs_10_.refs_6_ = bf16[2048,256]{1,0:T(8,128)(2,1)} collective-permute-done((bf16[2048,256]{1,0:T(8,128)(2,1)S(1)}, bf16[2048,256]{1,0:T(8,128)(2,1)}, u32[]{:S(2)}, u32[]{:S(2)}) %collective-permute-start.7) | collective-permute-done | bytes 1048608 | tf_op jit(solution)/shard_map/ppermute | solution.py:311
  98.5 6.9 %attend.1 = (bf16[8,128,256]{2,1,0:T(8,128)(2,1)}, f32[2,1,1024]{2,1,0:T(1,128)S(1)}) custom-call(bf16[8,3,128,256]{3,2,1,0:T(8,128)(2,1)S(1)} %all-to-all-done.q_ref.k_ref.v_ref, bf16[8,3,128,256]{3,2,1,0:T(8,128)(2,1)S(1)} %all-to-all-done.q_ref.k_ref.v_ref, bf16[8,3,128,256]{3,2,1,0:T(8,128)(2,1)S(1)} %all-to-all-done.q_ref.k_ref.v_ref), custom_call_target="tpu_custom_call" | custom-call | flops 2147483648 | bytes 2097152 | tf_op jit(solution)/shard_map/attend/pallas_call | solution.py:160
  105.4 8.0 %all-to-all-start.1 = ((bf16[8,128,256]{2,1,0:T(8,128)(2,1)}), bf16[8,128,256]{2,1,0:T(8,128)(2,1)S(1)}, u32[]{:S(2)}, u32[]{:S(2)}) async-start(bf16[8,128,256]{2,1,0:T(8,128)(2,1)} %get-tuple-element.24), calls=%async_computation.1 | async-start | bytes 1048576 | tf_op jit(solution)/shard_map/all_to_all | solution.py:315
  113.3 33.0 %pack_grad.1 = (bf16[128,1024]{1,0:T(8,128)(2,1)}, bf16[128,1024]{1,0:T(8,128)(2,1)}, bf16[128,1024]{1,0:T(8,128)(2,1)}, bf16[128,1024]{1,0:T(8,128)(2,1)}) custom-call(bf16[128,4096]{1,0:T(8,128)(2,1)} %bitcast.14), custom_call_target="tpu_custom_call" | custom-call | bytes 2097152 | tf_op jit(solution)/shard_map/pack_grad/pallas_call | solution.py:97
  146.4 1.6 collective-permute-start.3
  147.9 2.7 collective-permute-start.4
  150.6 1.4 collective-permute-start.5
  152.1 4.2 %collective-permute-done.3.refs_5_.refs_1_ = bf16[128,1024]{1,0:T(8,128)(2,1)S(1)} collective-permute-done((bf16[128,1024]{1,0:T(8,128)(2,1)}, bf16[128,1024]{1,0:T(8,128)(2,1)S(1)}, u32[]{:S(2)}, u32[]{:S(2)}) %collective-permute-start.3) | collective-permute-done | bytes 262176 | tf_op jit(solution)/shard_map/ppermute | solution.py:307
  156.3 0.7 copy-done.4
  157.0 1.0 collective-permute-start
  158.0 5.7 %collective-permute-done.4.refs_6_.refs_2_ = bf16[128,1024]{1,0:T(8,128)(2,1)S(1)} collective-permute-done((bf16[128,1024]{1,0:T(8,128)(2,1)}, bf16[128,1024]{1,0:T(8,128)(2,1)S(1)}, u32[]{:S(2)}, u32[]{:S(2)}) %collective-permute-start.4) | collective-permute-done | bytes 262176 | tf_op jit(solution)/shard_map/ppermute | solution.py:307
  163.6 0.7 copy-done.7
  164.3 0.8 collective-permute-start.1
  165.1 1.1 collective-permute-start.2
  166.2 8.5 %collective-permute-done.refs_1_ = bf16[8,128,256]{2,1,0:T(8,128)(2,1)S(1)} collective-permute-done((bf16[8,128,256]{2,1,0:T(8,128)(2,1)S(1)}, bf16[8,128,256]{2,1,0:T(8,128)(2,1)S(1)}, u32[]{:S(2)}, u32[]{:S(2)}) %collective-permute-start) | collective-permute-done | bytes 524320 | tf_op jit(solution)/shard_map/ppermute | solution.py:307
  174.8 10.6 %collective-permute-done.1.refs_2_ = bf16[8,128,256]{2,1,0:T(8,128)(2,1)S(1)} collective-permute-done((bf16[8,128,256]{2,1,0:T(8,128)(2,1)S(1)}, bf16[8,128,256]{2,1,0:T(8,128)(2,1)S(1)}, u32[]{:S(2)}, u32[]{:S(2)}) %collective-permute-start.1) | collective-permute-done | bytes 524320 | tf_op jit(solution)/shard_map/ppermute | solution.py:307
  185.4 0.9 copy-done.2
  186.4 0.9 copy-done.5
  187.3 0.9 copy-done.8
  188.3 16.5 %project.1 = (bf16[128,1024]{1,0:T(8,128)(2,1)S(1)}, bf16[128,1024]{1,0:T(8,128)(2,1)}, bf16[128,1024]{1,0:T(8,128)(2,1)}, bf16[128,1024]{1,0:T(8,128)(2,1)S(1)}...) custom-call(bf16[8,128,256]{2,1,0:T(8,128)(2,1)S(1)} %all-to-all-done.1.refs_0_, ...), custom_call_target="tpu_custom_call" | custom-call | flops 4294967296 | bytes 12582912 | tf_op jit(solution)/shard_map/project/pallas_call | solution.py:285
  204.7 0.7 copy-done
  205.4 4.2 %collective-permute-done.15 = bf16[8,2,256,256]{3,2,1,0:T(8,128)(2,1)S(1)} collective-permute-done((bf16[8,2,256,256]{3,2,1,0:T(8,128)(2,1)S(1)}, bf16[8,2,256,256]{3,2,1,0:T(8,128)(2,1)S(1)}, u32[]{:S(2)}, u32[]{:S(2)}) %collective-permute-start.15) | collective-permute-done | bytes 2097184 | tf_op jit(solution)/shard_map/ppermute | solution.py:311
  209.6 2.0 add_convert_fusion
  211.6 6.9 %all-to-all-start.3 = ((bf16[8,2,256,256]{3,2,1,0:T(8,128)(2,1)}), bf16[8,2,256,256]{3,2,1,0:T(8,128)(2,1)}, u32[]{:S(2)}, u32[]{:S(2)}) async-start(bf16[8,2,256,256]{3,2,1,0:T(8,128)(2,1)} %add_convert_fusion), calls=%async_computation.3 | async-start | bytes 4194304 | tf_op jit(solution)/shard_map/all_to_all | solution.py:315
  218.6 0.9 copy-done.3
  219.5 0.9 copy-done.6
  220.5 0.9 copy-done.9
  221.4 6.8 %grad_attended.1 = (bf16[8,128,256]{2,1,0:T(8,128)(2,1)S(1)}, bf16[8,128,256]{2,1,0:T(8,128)(2,1)S(1)}, bf16[8,128,256]{2,1,0:T(8,128)(2,1)S(1)}, bf16[8,128,256]{2,1,0:T(8,128)(2,1)S(1)}) custom-call(bf16[128,1024]{1,0:T(8,128)(2,1)S(1)} %copy-done.3, bf16[128,1024]{1,0:T(8,128)(2,1)S(1)} %copy-done.6, bf16[128,1024]{1,0:T(8,128)(2,1)S(1)} %copy-done.9, ...), custom_call_target="tpu_custom_call" | custom-call | flops 2147483648 | bytes 6291456 | tf_op jit(solution)/shard_map/grad_attended/pallas_call | solution.py:242
  228.2 2.1 collective-permute-start.14
  230.3 1.7 collective-permute-start.13
  232.0 1.6 collective-permute-start.12
  233.6 0.8 collective-permute-start.9
  234.4 1.7 collective-permute-start.10
  236.1 7.7 %collective-permute-done.14 = bf16[8,128,256]{2,1,0:T(8,128)(2,1)S(1)} collective-permute-done((bf16[8,128,256]{2,1,0:T(8,128)(2,1)S(1)}, bf16[8,128,256]{2,1,0:T(8,128)(2,1)S(1)}, u32[]{:S(2)}, u32[]{:S(2)}) %collective-permute-start.14) | collective-permute-done | bytes 524320 | tf_op jit(solution)/shard_map/ppermute | solution.py:307
  243.9 1.3 collective-permute-start.11
  245.1 11.0 %collective-permute-done.13 = bf16[8,128,256]{2,1,0:T(8,128)(2,1)S(1)} collective-permute-done((bf16[8,128,256]{2,1,0:T(8,128)(2,1)S(1)}, bf16[8,128,256]{2,1,0:T(8,128)(2,1)S(1)}, u32[]{:S(2)}, u32[]{:S(2)}) %collective-permute-start.13) | collective-permute-done | bytes 524320 | tf_op jit(solution)/shard_map/ppermute | solution.py:307
  256.1 0.4 collective-permute-done.12
  256.5 1.1 add_convert_fusion.1
  257.6 7.2 %all-to-all-start.2 = ((bf16[8,128,256]{2,1,0:T(8,128)(2,1)}), bf16[8,128,256]{2,1,0:T(8,128)(2,1)S(1)}, u32[]{:S(2)}, u32[]{:S(2)}) async-start(bf16[8,128,256]{2,1,0:T(8,128)(2,1)} %add_convert_fusion.1), calls=%async_computation.2 | async-start | bytes 1048576 | tf_op jit(solution)/shard_map/all_to_all | solution.py:315
  264.9 1.3 collective-permute-done.11.refs_3_
  266.2 0.7 copy-done.12
  266.9 33.0 %place_projected.1 = bf16[128,4096]{1,0:T(8,128)(2,1)} custom-call(bf16[128,1024]{1,0:T(8,128)(2,1)} %copy-done, bf16[128,1024]{1,0:T(8,128)(2,1)} %copy-done.10, bf16[128,1024]{1,0:T(8,128)(2,1)} %copy-done.11, bf16[128,1024]{1,0:T(8,128)(2,1)} %copy-done.12), custom_call_target="tpu_custom_call" | custom-call | bytes 2097152 | tf_op jit(solution)/shard_map/place_projected/pallas_call | solution.py:126
  299.9 1.9 convert_reduce_fusion
  301.9 8.3 %attend_back.1 = (bf16[1024,256]{1,0:T(8,128)(2,1)}, bf16[1024,256]{1,0:T(8,128)(2,1)}, bf16[1024,256]{1,0:T(8,128)(2,1)}) custom-call(bf16[8,3,128,256]{3,2,1,0:T(8,128)(2,1)S(1)} %all-to-all-done.q_ref.k_ref.v_ref, bf16[8,3,128,256]{3,2,1,0:T(8,128)(2,1)S(1)} %all-to-all-done.q_ref.k_ref.v_ref, ...), custom_call_target="tpu_custom_call" | custom-call | flops 5368709120 | bytes 3670016 | tf_op jit(solution)/shard_map/attend_back/pallas_call | solution.py:209
  310.3 0.7 fusion
  (32 shorter events, 0.2 us)
Async XLA Ops:
  49.6 8.2 %copy-start.1 = (bf16[2048,256]{1,0:T(8,128)(2,1)S(1)}, bf16[2048,256]{1,0:T(8,128)(2,1)}, u32[]{:S(2)}) copy-start(bf16[2048,256]{1,0:T(8,128)(2,1)} %refs_4_.1) | copy-start | bytes 3145732
  49.6 48.9 %all-to-all-start = ((bf16[8,3,128,256]{3,2,1,0:T(8,128)(2,1)}), bf16[8,3,128,256]{3,2,1,0:T(8,128)(2,1)S(1)}, u32[]{:S(2)}, u32[]{:S(2)}) async-start(bf16[8,3,128,256]{3,2,1,0:T(8,128)(2,1)} %pack_qkv.1), calls=%async_computation | async-start | bytes 3145728 | tf_op jit(solution)/shard_map/all_to_all | solution.py:315
  57.8 40.7 %collective-permute-start.7 = (bf16[2048,256]{1,0:T(8,128)(2,1)S(1)}, bf16[2048,256]{1,0:T(8,128)(2,1)}, u32[]{:S(2)}, u32[]{:S(2)}) collective-permute-start(bf16[2048,256]{1,0:T(8,128)(2,1)S(1)} %copy-done.1), channel_id=1, source_target_pairs={{0,64},{8,72},{16,80},{24,88},{32,96},{40,104},{48,112},{56,120},{... | collective-permute-start | bytes 3145736 | tf_op jit(solution)/shard_map/ppermute | solution.py:311
  58.5 107.7 %collective-permute-start.6 = (bf16[2048,256]{1,0:T(8,128)(2,1)S(1)}, bf16[2048,256]{1,0:T(8,128)(2,1)}, u32[]{:S(2)}, u32[]{:S(2)}) collective-permute-start(bf16[2048,256]{1,0:T(8,128)(2,1)S(1)} %copy-done.1), channel_id=1, source_target_pairs={{0,8},{8,0},{16,24},{24,16},{32,40},{40,32},{48,56},{56,48},{64,72... | collective-permute-start | bytes 3145736 | tf_op jit(solution)/shard_map/ppermute | solution.py:311
  98.5 67.7 %collective-permute-start.8 = (bf16[2048,256]{1,0:T(8,128)(2,1)}, bf16[2048,256]{1,0:T(8,128)(2,1)}, u32[]{:S(2)}, u32[]{:S(2)}) collective-permute-start(bf16[2048,256]{1,0:T(8,128)(2,1)} %collective-permute-done.7.refs_10_.refs_6_), channel_id=1, source_target_pairs={{0,8},{8,0},{16,24},{24,16},{32,40},{40,32},{48,56},{56,48},{64,72... | collective-permute-start | bytes 3145736 | tf_op jit(solution)/shard_map/ppermute | solution.py:311
  105.4 51.6 %all-to-all-start.1 = ((bf16[8,128,256]{2,1,0:T(8,128)(2,1)}), bf16[8,128,256]{2,1,0:T(8,128)(2,1)S(1)}, u32[]{:S(2)}, u32[]{:S(2)}) async-start(bf16[8,128,256]{2,1,0:T(8,128)(2,1)} %get-tuple-element.24), calls=%async_computation.1 | async-start | bytes 1048576 | tf_op jit(solution)/shard_map/all_to_all | solution.py:315
  146.4 9.9 %collective-permute-start.3 = (bf16[128,1024]{1,0:T(8,128)(2,1)}, bf16[128,1024]{1,0:T(8,128)(2,1)S(1)}, u32[]{:S(2)}, u32[]{:S(2)}) collective-permute-start(bf16[128,1024]{1,0:T(8,128)(2,1)} %get-tuple-element.26), channel_id=1, source_target_pairs={{0,16},{8,24},{16,32},{24,40},{32,48},{40,56},{48,0},{56,8},{64,80... | collective-permute-start | bytes 786440 | tf_op jit(solution)/shard_map/ppermute | solution.py:307
  147.9 15.7 %collective-permute-start.4 = (bf16[128,1024]{1,0:T(8,128)(2,1)}, bf16[128,1024]{1,0:T(8,128)(2,1)S(1)}, u32[]{:S(2)}, u32[]{:S(2)}) collective-permute-start(bf16[128,1024]{1,0:T(8,128)(2,1)} %get-tuple-element.27), channel_id=1, source_target_pairs={{0,32},{8,40},{16,48},{24,56},{32,0},{40,8},{48,16},{56,24},{64,96... | collective-permute-start | bytes 786440 | tf_op jit(solution)/shard_map/ppermute | solution.py:307
  150.6 14.5 %collective-permute-start.5 = (bf16[128,1024]{1,0:T(8,128)(2,1)}, bf16[128,1024]{1,0:T(8,128)(2,1)}, u32[]{:S(2)}, u32[]{:S(2)}) collective-permute-start(bf16[128,1024]{1,0:T(8,128)(2,1)} %get-tuple-element.28), channel_id=1, source_target_pairs={{0,48},{8,56},{16,0},{24,8},{32,16},{40,24},{48,32},{56,40},{64,11... | collective-permute-start | bytes 786440 | tf_op jit(solution)/shard_map/ppermute | solution.py:307
  156.3 0.7 copy-start.4
  157.0 17.8 %collective-permute-start = (bf16[8,128,256]{2,1,0:T(8,128)(2,1)S(1)}, bf16[8,128,256]{2,1,0:T(8,128)(2,1)S(1)}, u32[]{:S(2)}, u32[]{:S(2)}) collective-permute-start(bf16[8,128,256]{2,1,0:T(8,128)(2,1)S(1)} %all-to-all-done.1.refs_0_), channel_id=1, source_target_pairs={{0,16},{8,24},{16,32},{24,40},{32,48},{40,56},{48,0},{56,8},{64,80... | collective-permute-start | bytes 1572872 | tf_op jit(solution)/shard_map/ppermute | solution.py:307
  163.6 0.7 copy-start.7
  164.3 21.1 %collective-permute-start.1 = (bf16[8,128,256]{2,1,0:T(8,128)(2,1)S(1)}, bf16[8,128,256]{2,1,0:T(8,128)(2,1)S(1)}, u32[]{:S(2)}, u32[]{:S(2)}) collective-permute-start(bf16[8,128,256]{2,1,0:T(8,128)(2,1)S(1)} %all-to-all-done.1.refs_0_), channel_id=1, source_target_pairs={{0,32},{8,40},{16,48},{24,56},{32,0},{40,8},{48,16},{56,24},{64,96... | collective-permute-start | bytes 1572872 | tf_op jit(solution)/shard_map/ppermute | solution.py:307
  165.1 20.3 %collective-permute-start.2 = (bf16[8,128,256]{2,1,0:T(8,128)(2,1)S(1)}, bf16[8,128,256]{2,1,0:T(8,128)(2,1)S(1)}, u32[]{:S(2)}, u32[]{:S(2)}) collective-permute-start(bf16[8,128,256]{2,1,0:T(8,128)(2,1)S(1)} %all-to-all-done.1.refs_0_), channel_id=1, source_target_pairs={{0,48},{8,56},{16,0},{24,8},{32,16},{40,24},{48,32},{56,40},{64,11... | collective-permute-start | bytes 1572872 | tf_op jit(solution)/shard_map/ppermute | solution.py:307
  185.4 1.0 copy-start.2
  186.4 0.9 copy-start.5
  187.3 0.9 copy-start.8
  204.7 0.7 copy-start
  205.4 4.2 %collective-permute-start.15 = (bf16[8,2,256,256]{3,2,1,0:T(8,128)(2,1)S(1)}, bf16[8,2,256,256]{3,2,1,0:T(8,128)(2,1)S(1)}, u32[]{:S(2)}, u32[]{:S(2)}) collective-permute-start(bf16[8,2,256,256]{3,2,1,0:T(8,128)(2,1)S(1)} %get-tuple-element.42), channel_id=1, source_target_pairs={{0,8},{8,0},{16,24},{24,16},{32,40},{40,32},{48,56},{56,48},{64,72... | collective-permute-start | bytes 6291464 | tf_op jit(solution)/shard_map/ppermute | solution.py:311
  211.6 46.0 %all-to-all-start.3 = ((bf16[8,2,256,256]{3,2,1,0:T(8,128)(2,1)}), bf16[8,2,256,256]{3,2,1,0:T(8,128)(2,1)}, u32[]{:S(2)}, u32[]{:S(2)}) async-start(bf16[8,2,256,256]{3,2,1,0:T(8,128)(2,1)} %add_convert_fusion), calls=%async_computation.3 | async-start | bytes 4194304 | tf_op jit(solution)/shard_map/all_to_all | solution.py:315
  218.6 0.9 copy-start.3
  219.5 0.9 copy-start.6
  220.5 0.9 copy-start.9
  228.2 15.6 %collective-permute-start.14 = (bf16[8,128,256]{2,1,0:T(8,128)(2,1)S(1)}, bf16[8,128,256]{2,1,0:T(8,128)(2,1)S(1)}, u32[]{:S(2)}, u32[]{:S(2)}) collective-permute-start(bf16[8,128,256]{2,1,0:T(8,128)(2,1)S(1)} %get-tuple-element.37), channel_id=1, source_target_pairs={{0,16},{8,24},{16,32},{24,40},{32,48},{40,56},{48,0},{56,8},{64,80... | collective-permute-start | bytes 1572872 | tf_op jit(solution)/shard_map/ppermute | solution.py:307
  230.3 25.8 %collective-permute-start.13 = (bf16[8,128,256]{2,1,0:T(8,128)(2,1)S(1)}, bf16[8,128,256]{2,1,0:T(8,128)(2,1)S(1)}, u32[]{:S(2)}, u32[]{:S(2)}) collective-permute-start(bf16[8,128,256]{2,1,0:T(8,128)(2,1)S(1)} %get-tuple-element.36), channel_id=1, source_target_pairs={{0,32},{8,40},{16,48},{24,56},{32,0},{40,8},{48,16},{56,24},{64,96... | collective-permute-start | bytes 1572872 | tf_op jit(solution)/shard_map/ppermute | solution.py:307
  232.0 24.5 %collective-permute-start.12 = (bf16[8,128,256]{2,1,0:T(8,128)(2,1)S(1)}, bf16[8,128,256]{2,1,0:T(8,128)(2,1)S(1)}, u32[]{:S(2)}, u32[]{:S(2)}) collective-permute-start(bf16[8,128,256]{2,1,0:T(8,128)(2,1)S(1)} %get-tuple-element.35), channel_id=1, source_target_pairs={{0,48},{8,56},{16,0},{24,8},{32,16},{40,24},{48,32},{56,40},{64,11... | collective-permute-start | bytes 1572872 | tf_op jit(solution)/shard_map/ppermute | solution.py:307
  233.6 31.2 %collective-permute-start.9 = (bf16[128,1024]{1,0:T(8,128)(2,1)}, bf16[128,1024]{1,0:T(8,128)(2,1)S(1)}, u32[]{:S(2)}, u32[]{:S(2)}) collective-permute-start(bf16[128,1024]{1,0:T(8,128)(2,1)} %get-tuple-element.30), channel_id=1, source_target_pairs={{0,48},{8,56},{16,0},{24,8},{32,16},{40,24},{48,32},{56,40},{64,11... | collective-permute-start | bytes 786440 | tf_op jit(solution)/shard_map/ppermute | solution.py:307
  234.4 30.4 %collective-permute-start.10 = (bf16[128,1024]{1,0:T(8,128)(2,1)}, bf16[128,1024]{1,0:T(8,128)(2,1)S(1)}, u32[]{:S(2)}, u32[]{:S(2)}) collective-permute-start(bf16[128,1024]{1,0:T(8,128)(2,1)} %get-tuple-element.31), channel_id=1, source_target_pairs={{0,32},{8,40},{16,48},{24,56},{32,0},{40,8},{48,16},{56,24},{64,96... | collective-permute-start | bytes 786440 | tf_op jit(solution)/shard_map/ppermute | solution.py:307
  243.9 22.3 %collective-permute-start.11 = (bf16[128,1024]{1,0:T(8,128)(2,1)S(1)}, bf16[128,1024]{1,0:T(8,128)(2,1)S(1)}, u32[]{:S(2)}, u32[]{:S(2)}) collective-permute-start(bf16[128,1024]{1,0:T(8,128)(2,1)S(1)} %get-tuple-element.32), channel_id=1, source_target_pairs={{0,16},{8,24},{16,32},{24,40},{32,48},{40,56},{48,0},{56,8},{64,80... | collective-permute-start | bytes 786440 | tf_op jit(solution)/shard_map/ppermute | solution.py:307
  257.6 44.3 %all-to-all-start.2 = ((bf16[8,128,256]{2,1,0:T(8,128)(2,1)}), bf16[8,128,256]{2,1,0:T(8,128)(2,1)S(1)}, u32[]{:S(2)}, u32[]{:S(2)}) async-start(bf16[8,128,256]{2,1,0:T(8,128)(2,1)} %add_convert_fusion.1), calls=%async_computation.2 | async-start | bytes 1048576 | tf_op jit(solution)/shard_map/all_to_all | solution.py:315
  264.8 1.3 copy-start.10
  264.9 1.3 copy-start.11
  266.2 0.7 copy-start.12
  301.8 8.4 %collective-permute-start.16 = (bf16[256,256]{1,0:T(8,128)(2,1)S(1)}, bf16[256,256]{1,0:T(8,128)(2,1)S(1)}, u32[]{:S(2)}, u32[]{:S(2)}) collective-permute-start(bf16[256,256]{1,0:T(8,128)(2,1)S(1)} %fusion.1), channel_id=1, source_target_pairs={{0,64},{8,72},{16,80},{24,88},{32,96},{40,104},{48,112},{56,120},{... | collective-permute-start | bytes 393224 | tf_op jit(solution)/shard_map/ppermute | solution.py:311
where the time goes:
time: 313 us; the launch traced here: 311 us
  Pallas kernels  153 us (49%)
  waiting for transfers between devices  93.6 us (30%)
  starting transfers between devices  48.9 us (16%)
  local copies, waits for them, and re-layouts  8.53 us (3%)
  other arithmetic  5.79 us (2%)
    ppermute x12, waiting for transfers between devices, shift_x(): return lax.ppermute(array, 'dp', pairs)  49.4 us
    pallas_call x1, Pallas kernels, pack_qkv(): pl.pallas_call(body, out_shape=jax.ShapeDtypeStruct((groups, 3, tok, BLOC...  49 us
    ppermute x5, waiting for transfers between devices, swap(): return lax.ppermute(array, 'dp', [(d, d ^ bit) for d in range(count)])  44.1 us
    pallas_call x1, Pallas kernels, place_projected(): pl.pallas_call(body, out_shape=jax.ShapeDtypeStruct((tok, cols), parts[0]...  33 us
    pallas_call x1, Pallas kernels, pack_grad(): pl.pallas_call(body, out_shape=[jax.ShapeDtypeStruct((tok, 4 * BLOCK), gr...  33 us
    all_to_all x4, starting transfers between devices, exchange(): return lax.all_to_all(array, 'seq', 0, 0, tiled=False)  30.3 us
    ppermute x12, starting transfers between devices, shift_x(): return lax.ppermute(array, 'dp', pairs)  17.8 us
    pallas_call x1, Pallas kernels, project(): pl.pallas_call(body, grid=(groups,), out_shape=[jax.ShapeDtypeStruct((tok...  16.5 us
  transfers between devices with their start and end apart: 21, of which 10 were waited for; matrix products, arithmetic and copies ran while one was open for 1% of the time, Pallas kernels for 28%

commit v1 on v0

v1 whole, which is shorter than its diff:
```python
import jax
import jax.numpy as jnp
from jax import lax
from jax.experimental import pallas as pl
from jax.experimental.pallas import tpu as pltpu
from jax.sharding import Mesh
from jax.sharding import PartitionSpec as P

HEAD = 128
X = 4
DP = ("yl", "x", "core")
SEQ = ("z", "yh")
BLOCK = 256
SCALE = HEAD ** (-0.5)
MIB = 1 << 20


def params(mib):
    return pltpu.CompilerParams(vmem_limit_bytes=mib * MIB)


def cost(flops, size, trans=0):
    return pl.CostEstimate(flops=flops, bytes_accessed=size, transcendentals=trans)


def nt(a, b):
    return lax.dot_general(a, b, (((1,), (1,)), ((), ())), preferred_element_type=jnp.float32)


def tn(a, b):
    return lax.dot_general(a, b, (((0,), (0,)), ((), ())), preferred_element_type=jnp.float32)


def place():
    return tuple(lax.axis_index(name) for name in DP)


def column_of(yl, x, core, j):
    other_y, other_core = j // 2, j % 2
    yy = yl + other_y - 2 * yl * other_y
    cc = core + other_core - 2 * core * other_core
    return pl.multiple_of(((yy * X + x) * 2 + cc) * BLOCK, BLOCK)


def pack_qkv(query, key, value):
    tok, feat = query.shape
    groups = feat // BLOCK

    def body(q, k, v, out):
        for g in range(groups):
            for i, src in enumerate((q, k, v)):
                out[g, i] = src[:, g * BLOCK : (g + 1) * BLOCK]

    return pl.pallas_call(
        body,
        out_shape=jax.ShapeDtypeStruct((groups, 3, tok, BLOCK), query.dtype),
        compiler_params=params(16),
        cost_estimate=cost(0, 3 * 2 * 2 * tok * feat),
        name="pack_qkv",
    )(query, key, value)


def pack_grad(grad):
    tok, cols = grad.shape

    def body(src, *outs):
        yl, x, core = place()
        for s in range(X):
            for j in range(4):
                outs[s][:, j * BLOCK : (j + 1) * BLOCK] = src[
                    :, pl.ds(column_of(yl, (x + s) % X, core, j), BLOCK)
                ]

    return pl.pallas_call(
        body,
        out_shape=[jax.ShapeDtypeStruct((tok, 4 * BLOCK), grad.dtype)] * X,
        compiler_params=params(16),
        cost_estimate=cost(0, 4 * tok * cols),
        name="pack_grad",
    )(grad)


def place_projected(parts, cols):
    tok = parts[0].shape[0]

    def body(*refs):
        srcs, out = refs[:X], refs[X]
        yl, x, core = place()
        for s in range(X):
            for j in range(4):
                out[:, pl.ds(column_of(yl, (x + s) % X, core, j), BLOCK)] = srcs[s][
                    :, j * BLOCK : (j + 1) * BLOCK
                ]

    return pl.pallas_call(
        body,
        out_shape=jax.ShapeDtypeStruct((tok, cols), parts[0].dtype),
        compiler_params=params(16),
        cost_estimate=cost(0, 4 * tok * cols),
        name="place_projected",
    )(*parts)


def head_spec(groups, tok, i):
    return pl.BlockSpec((groups, pl.squeezed, tok, HEAD), lambda h: (0, i, 0, h))


def attend(qkv):
    groups, _, tok, width = qkv.shape
    heads, length = width // HEAD, groups * tok
    rows = 256

    def body(q_ref, k_ref, v_ref, o_ref, lse_ref):
        keys = k_ref[...].reshape(length, HEAD)
        values = v_ref[...].reshape(length, HEAD)
        for b in range(length // rows):
            per = rows // tok
            query = q_ref[b * per : (b + 1) * per].reshape(rows, HEAD)
            scores = nt(keys, query) * SCALE
            peak = jnp.max(scores, axis=0, keepdims=True)
            shifted = jnp.exp(scores - peak)
            total = jnp.sum(shifted, axis=0, keepdims=True)
            out = tn(values, shifted.astype(jnp.bfloat16)) / total
            o_ref[b * per : (b + 1) * per] = out.T.astype(jnp.bfloat16).reshape(per, tok, HEAD)
            lse_ref[:, b * rows : (b + 1) * rows] = peak + jnp.log(total)

    return pl.pallas_call(
        body,
        grid=(heads,),
        out_shape=[
            jax.ShapeDtypeStruct((groups, tok, width), jnp.bfloat16),
            jax.ShapeDtypeStruct((heads, 1, length), jnp.float32),
        ],
        in_specs=[head_spec(groups, tok, i) for i in range(3)],
        out_specs=[
            pl.BlockSpec((groups, tok, HEAD), lambda h: (0, 0, h)),
            pl.BlockSpec((pl.squeezed, 1, length), lambda h: (h, 0, 0)),
        ],
        compiler_params=params(32),
        cost_estimate=cost(8 * heads * length * length * HEAD, 8 * length * width, heads * length * length),
        name="attend",
    )(qkv, qkv, qkv)


def attend_back(qkv, lse, grad):
    groups, _, tok, width = qkv.shape
    heads, length = width // HEAD, groups * tok
    rows = 256

    def body(q_ref, k_ref, v_ref, lse_ref, g_ref, dq_ref, dk_ref, dv_ref, k_acc, v_acc):
        keys = k_ref[...].reshape(length, HEAD)
        values = v_ref[...].reshape(length, HEAD)
        for b in range(length // rows):
            per = rows // tok
            query = q_ref[b * per : (b + 1) * per].reshape(rows, HEAD)
            grad_rows = g_ref[b * per : (b + 1) * per].reshape(rows, HEAD)
            scores = nt(keys, query) * SCALE
            probs = jnp.exp(scores - lse_ref[:, b * rows : (b + 1) * rows])
            grad_probs = nt(values, grad_rows)
            delta = jnp.sum(probs * grad_probs, axis=0, keepdims=True)
            grad_scores = (probs * (grad_probs - delta)).astype(jnp.bfloat16)
            dv = jnp.dot(probs.astype(jnp.bfloat16), grad_rows, preferred_element_type=jnp.float32)
            dk = jnp.dot(grad_scores, query, preferred_element_type=jnp.float32)
            if b == 0:
                v_acc[...] = dv
                k_acc[...] = dk
            else:
                v_acc[...] += dv
                k_acc[...] += dk
            dq = tn(keys, grad_scores) * SCALE
            dq_ref[b * rows : (b + 1) * rows, :] = dq.T.astype(jnp.bfloat16)
        dk_ref[...] = (k_acc[...] * SCALE).astype(jnp.bfloat16)
        dv_ref[...] = v_acc[...].astype(jnp.bfloat16)

    out = jax.ShapeDtypeStruct((length, width), jnp.bfloat16)
    return pl.pallas_call(
        body,
        grid=(heads,),
        out_shape=[out] * 3,
        in_specs=[head_spec(groups, tok, i) for i in range(3)]
        + [
            pl.BlockSpec((pl.squeezed, 1, length), lambda h: (h, 0, 0)),
            pl.BlockSpec((groups, tok, HEAD), lambda h: (0, 0, h)),
        ],
        out_specs=[pl.BlockSpec((length, HEAD), lambda h: (0, h))] * 3,
        scratch_shapes=[pltpu.VMEM((length, HEAD), jnp.float32)] * 2,
        compiler_params=params(40),
        cost_estimate=cost(20 * heads * length * length * HEAD, 14 * length * width, heads * length * length),
        name="attend_back",
    )(qkv, qkv, qkv, lse, grad)


def grad_attended_parts(grads, weights):
    rows, width = grads.shape
    tok = rows // X
    _, feat, block = weights.shape
    groups = feat // BLOCK

    def body(g_ref, w_ref, *outs):
        total = None
        for j in range(4):
            term = nt(g_ref[:, j * block : (j + 1) * block], w_ref[j])
            total = term if total is None else total + term
        total = total.astype(jnp.bfloat16)
        for s in range(X):
            outs[s][...] = total[s * tok : (s + 1) * tok]

    return pl.pallas_call(
        body,
        grid=(groups,),
        out_shape=[jax.ShapeDtypeStruct((groups, tok, BLOCK), jnp.bfloat16)] * X,
        in_specs=[
            pl.BlockSpec((rows, width), lambda n: (0, 0)),
            pl.BlockSpec((4, BLOCK, block), lambda n: (0, n, 0)),
        ],
        out_specs=[pl.BlockSpec((pl.squeezed, tok, BLOCK), lambda n: (n, 0, 0))] * X,
        compiler_params=params(32),
        cost_estimate=cost(2 * rows * width * feat, 2 * feat * width + 4 * rows * width),
        name="grad_attended",
    )(grads, weights)


def weight_parts(attended, grads, core):
    groups, tok, block = attended[0].shape
    rows = X * tok

    def body(*refs):
        a_refs, g_ref, out, cols = refs[:X], refs[X], refs[X + 1], refs[X + 2]

        @pl.when(pl.program_id(0) == 0)
        def _():
            for i in range(2):
                j = 2 * i + core
                cols[:, i * block : (i + 1) * block] = g_ref[:, j * block : (j + 1) * block]

        left = jnp.concatenate([a[...] for a in a_refs], axis=0)
        piece = tn(left, cols[...]).astype(jnp.bfloat16)
        yl = lax.axis_index("yl")
        for i in range(2):
            out[yl + i - 2 * yl * i] = piece[:, i * block : (i + 1) * block]

    return pl.pallas_call(
        body,
        grid=(groups,),
        out_shape=jax.ShapeDtypeStruct((2, groups, block, block), jnp.bfloat16),
        in_specs=[pl.BlockSpec((pl.squeezed, tok, block), lambda n: (n, 0, 0))] * X
        + [pl.BlockSpec(grads.shape, lambda n: (0, 0))],
        out_specs=pl.BlockSpec((2, pl.squeezed, block, block), lambda n: (0, n, 0, 0)),
        scratch_shapes=[pltpu.VMEM((rows, 2 * block), jnp.bfloat16)],
        compiler_params=params(24),
        cost_estimate=cost(4 * rows * groups * block * block, 5 * MIB),
        name="weight_parts",
    )(*attended, grads)


def project(attended, weights):
    groups, tok, block = attended[0].shape
    rows, feat = X * tok, groups * block

    def body(*refs):
        a_refs, w_ref, outs, left = refs[:X], refs[X], refs[X + 1 : 2 * X + 1], refs[2 * X + 1]

        @pl.when(pl.program_id(0) == 0)
        def _():
            for s in range(X):
                for n in range(groups):
                    left[s * tok : (s + 1) * tok, n * block : (n + 1) * block] = a_refs[s][n]

        out = jnp.dot(left[...], w_ref[...], preferred_element_type=jnp.float32)
        out = out.astype(jnp.bfloat16)
        for s in range(X):
            outs[s][...] = out[s * tok : (s + 1) * tok]

    return pl.pallas_call(
        body,
        grid=(4,),
        out_shape=[jax.ShapeDtypeStruct((tok, 4 * block), jnp.bfloat16)] * X,
        in_specs=[pl.BlockSpec((groups, tok, block), lambda j: (0, 0, 0))] * X
        + [pl.BlockSpec((pl.squeezed, feat, block), lambda j: (j, 0, 0))],
        out_specs=[pl.BlockSpec((tok, block), lambda j: (0, j))] * X,
        scratch_shapes=[pltpu.VMEM((rows, feat), jnp.bfloat16)],
        compiler_params=params(24),
        cost_estimate=cost(8 * rows * feat * block, 7 * MIB),
        name="project",
    )(*attended, weights)


def shift_x(array, shift):
    return lax.ppermute(array, "x", [(i, (i + shift) % X) for i in range(X)])


def swap(array, axis):
    return lax.ppermute(array, axis, [(0, 1), (1, 0)])


def exchange(array, axes=SEQ):
    return lax.all_to_all(array, axes, 0, 0, tiled=False)


def after(arrays, *others):
    return lax.optimization_barrier((arrays, others))[0]


def f32_sum(*arrays):
    total = arrays[0].astype(jnp.float32)
    for array in arrays[1:]:
        total = total + array.astype(jnp.float32)
    return total


def shards(query_input, key_input, value_input, out_weight, grad_out):
    cols = grad_out.shape[2]
    half = out_weight.shape[0] // 2

    lower, upper = lax.optimization_barrier((out_weight[:half], out_weight[half:]))
    query, key, value = after((query_input[0], key_input[0], value_input[0]), lower, upper)
    lower = swap(lower, "yl")
    upper = lax.ppermute(upper, ("yl", "yh"), [(i, 3 - i) for i in range(4)])
    qkv = exchange(pack_qkv(query, key, value))
    mine = pack_grad(grad_out[0])
    grads = [mine[0]] + [shift_x(mine[s], s) for s in range(1, X)]
    grads = jnp.concatenate(grads, axis=0)
    weights = [out_weight, swap(out_weight, "core")]
    weights.append(jnp.concatenate([lower, upper], axis=0))
    weights.append(jnp.concatenate([swap(lower, "core"), swap(upper, "core")], axis=0))
    weights = jnp.stack(weights)
    parts = grad_attended_parts(grads, weights)

    attended, lse = attend(after(qkv, *parts))
    parts = [parts[0]] + [shift_x(parts[s], -s) for s in range(1, X)]
    attended = after(exchange(attended), *parts)
    rows = [attended] + [shift_x(attended, s) for s in range(1, X)]
    grad_attended = exchange(f32_sum(*parts).astype(jnp.bfloat16))

    grads = after(grads, grad_attended)
    far = swap(weight_parts(rows, grads, 1), "core")
    near = weight_parts(rows, grads, 0)
    total = f32_sum(near, far).astype(jnp.bfloat16)
    total = exchange(total.reshape(-1, BLOCK, BLOCK), ("yl", *SEQ))
    grad_weight = jnp.sum(total.astype(jnp.float32), axis=0)

    projected = project(rows, weights)
    projected = [projected[0]] + [shift_x(projected[s], -s) for s in range(1, X)]
    projected = place_projected(projected, cols)[None]

    grads_in = attend_back(qkv, lse, grad_attended)
    return (projected, *[g[None] for g in grads_in], grad_weight)


def solution(mesh):
    fine = Mesh(mesh.devices.reshape(-1, X, 2, X, 2), DP + SEQ)
    return jax.shard_map(
        shards,
        mesh=fine,
        in_specs=(P(DP, SEQ, None), P(DP, SEQ, None), P(DP, SEQ, None), P(None, DP), P(DP, SEQ, None)),
        out_specs=(P(DP, SEQ, None), P(DP, None, SEQ), P(DP, None, SEQ), P(DP, None, SEQ), P(SEQ, DP)),
        check_vma=False,
    )
```

time: 313 us -> 158 us (0.50)
  Pallas kernels: 153 us -> 32.8 us
  waiting for transfers between devices: 93.6 us -> 40.5 us
  blocking collectives: 0 us -> 16.4 us
  other arithmetic: 5.79 us -> 9.46 us
    ppermute x17 -> x18, waiting for transfers between devices: 93.5 us -> 16 us  [the longest x12 14.8 us: shift_x(): return lax.ppermute(array, 'x', [(i, (i + shift) % X) for i in range(X)])]
    pallas_call x1, Pallas kernels: 49 us -> 1.28 us  [pack_qkv(): pl.pallas_call(body, out_shape=jax.ShapeDtypeStruct((groups, 3, tok, BLOC...]
    pallas_call x1, Pallas kernels: 33 us -> 0.85 us  [pack_grad(): pl.pallas_call(body, out_shape=[jax.ShapeDtypeStruct((tok, 4 * BLOCK), gr...]
    pallas_call x1, Pallas kernels: 33 us -> 1.09 us  [place_projected(): pl.pallas_call(body, out_shape=jax.ShapeDtypeStruct((tok, cols), parts[0]...]
    all_to_all x4 -> x3, waiting for transfers between devices: 0.01 us -> 24.6 us  [exchange(): return lax.all_to_all(array, axes, 0, 0, tiled=False)]
    all_to_all x0 -> x1, blocking collectives: none -> 16.4 us  [exchange(): return lax.all_to_all(array, axes, 0, 0, tiled=False)]
    pallas_call x1 -> x3, Pallas kernels: 16.5 us -> 9.09 us  [the longest x2 5.89 us: weight_parts(): pl.pallas_call(body, grid=(groups,), out_shape=jax.ShapeDtypeStruct((2, g...]
    unnamed x26 -> x25, local copies, waits for them, and re-layouts: 8.51 us -> 5.02 us
  transfers between devices with their start and end apart: 21 -> 21, of which waited for: 10 -> 10; matrix products, arithmetic and copies ran while one was open for 1% -> 4% of each run, Pallas kernels for 28% -> 19%
where the time goes in v1:
time: 158 us; the launch traced here: 157 us
  starting transfers between devices  49.5 us (31%)
  waiting for transfers between devices  40.5 us (26%)
  Pallas kernels  32.8 us (21%)
  blocking collectives  16.4 us (10%)
  other arithmetic  9.46 us (6%)
  local copies, waits for them, and re-layouts  7.43 us (5%)
    all_to_all x3, starting transfers between devices, exchange(): return lax.all_to_all(array, axes, 0, 0, tiled=False)  29.4 us
    all_to_all x3, waiting for transfers between devices, exchange(): return lax.all_to_all(array, axes, 0, 0, tiled=False)  24.6 us
    all_to_all x1, blocking collectives, exchange(): return lax.all_to_all(array, axes, 0, 0, tiled=False)  16.4 us
    ppermute x12, starting transfers between devices, shift_x(): return lax.ppermute(array, 'x', [(i, (i + shift) % X) for i in range(X)])  15.5 us
    ppermute x12, waiting for transfers between devices, shift_x(): return lax.ppermute(array, 'x', [(i, (i + shift) % X) for i in range(X)])  14.8 us
    pallas_call x1, Pallas kernels, attend_back(): pl.pallas_call(body, grid=(heads,), out_shape=[out] * 3, in_specs=[head_s...  8.3 us
    pallas_call x1, Pallas kernels, attend(): pl.pallas_call(body, grid=(heads,), out_shape=[jax.ShapeDtypeStruct((grou...  6.86 us
    pallas_call x2, Pallas kernels, weight_parts(): pl.pallas_call(body, grid=(groups,), out_shape=jax.ShapeDtypeStruct((2, g...  5.89 us
  transfers between devices with their start and end apart: 21, of which 10 were waited for; matrix products, arithmetic and copies ran while one was open for 4% of the time, Pallas kernels for 19%

profile of v1, /device:TPU:0, one launch (start us, length us, event | category | flops | bytes accessed | tf_op | source)
XLA Modules:
  0.0 157.0 jit_solution(17607553766041897146)
XLA Ops:
  0.7 2.4 %fusion = (bf16[1024,256]{1,0:T(8,128)(2,1)}, bf16[1024,256]{1,0:T(8,128)(2,1)}) fusion(bf16[2048,256]{1,0:T(8,128)(2,1)} %param.8), kind=kLoop, calls=%fused_computation.10 | loop fusion | bytes 2097152 | tf_op jit(solution)/shard_map/slice | solution.py:315
  3.1 1.7 %collective-permute-start.4 = (bf16[1024,256]{1,0:T(8,128)(2,1)}, bf16[1024,256]{1,0:T(8,128)(2,1)}, u32[]{:S(2)}, u32[]{:S(2)}) collective-permute-start(bf16[1024,256]{1,0:T(8,128)(2,1)} %get-tuple-element.30), channel_id=1, source_target_pairs={{0,64},{64,0},{1,65},{65,1},{2,66},{66,2},{3,67},{67,3},{4,68},{68... | collective-permute-start | bytes 1572872 | tf_op jit(solution)/shard_map/ppermute | solution.py:293
  4.7 2.2 %collective-permute-start.5 = (bf16[1024,256]{1,0:T(8,128)(2,1)}, bf16[1024,256]{1,0:T(8,128)(2,1)}, u32[]{:S(2)}, u32[]{:S(2)}) collective-permute-start(bf16[1024,256]{1,0:T(8,128)(2,1)} %get-tuple-element.31), channel_id=1, source_target_pairs={{0,65},{1,64},{64,1},{65,0},{2,67},{3,66},{66,3},{67,2},{4,69},{5,... | collective-permute-start | bytes 1572872 | tf_op jit(solution)/shard_map/ppermute | solution.py:318
  6.9 0.9 pack_grad.1
  7.8 1.5 collective-permute-start
  9.2 2.7 %collective-permute-start.1 = (bf16[128,1024]{1,0:T(8,128)(2,1)S(1)}, bf16[128,1024]{1,0:T(8,128)(2,1)}, u32[]{:S(2)}, u32[]{:S(2)}) collective-permute-start(bf16[128,1024]{1,0:T(8,128)(2,1)S(1)} %get-tuple-element.37), channel_id=1, source_target_pairs={{0,32},{16,48},{32,0},{48,16},{1,33},{17,49},{33,1},{49,17},{2,34}... | collective-permute-start | bytes 786440 | tf_op jit(solution)/shard_map/ppermute | solution.py:289
  12.0 1.3 pack_qkv.1
  13.3 5.5 %all-to-all-start = ((bf16[8,3,128,256]{3,2,1,0:T(8,128)(2,1)}), bf16[8,3,128,256]{3,2,1,0:T(8,128)(2,1)S(1)}, u32[]{:S(2)}, u32[]{:S(2)}) async-start(bf16[8,3,128,256]{3,2,1,0:T(8,128)(2,1)} %pack_qkv.1), calls=%async_computation | async-start | bytes 3145728 | tf_op jit(solution)/shard_map/all_to_all | solution.py:297
  18.7 1.5 collective-permute-start.2
  20.3 0.1 collective-permute-start.6
  20.4 0.5 collective-permute-start.7
  20.9 1.0 constant_dynamic-update-slice_fusion.2
  21.8 1.5 collective-permute-done.1
  23.4 1.0 constant_dynamic-update-slice_fusion.1
  24.3 2.6 %collective-permute-done.2 = bf16[128,1024]{1,0:T(8,128)(2,1)S(1)} collective-permute-done((bf16[128,1024]{1,0:T(8,128)(2,1)S(1)}, bf16[128,1024]{1,0:T(8,128)(2,1)S(1)}, u32[]{:S(2)}, u32[]{:S(2)}) %collective-permute-start.2) | collective-permute-done | bytes 262176 | tf_op jit(solution)/shard_map/ppermute | solution.py:289
  27.0 1.4 maximum_bitcast_fusion
  28.5 1.6 %pad_maximum_fusion.w_ref.refs_4_ = bf16[4,2048,256]{2,1,0:T(8,128)(2,1)S(1)} fusion(bf16[1,2048,256]{2,1,0:T(8,128)(2,1)S(1)} %maximum_bitcast_fusion.1, bf16[1,2048,256]{2,1,0:T(8,128)(2,1)S(1)} %maximum_bitcast_fusion, bf16[1,2048,256]{2,1,0:T(8,128)(2,1)} %bitcast.5, bf16[1,2048,256]{2,1,0:T(8,128)(2,1)S(1)} %bitcast.20), kind=kLoop, calls=%fused_computation | loop fusion | flops 6291456 | bytes 8388608 | tf_op jit(solution)/shard_map/stack | solution.py:326
  30.2 5.4 %grad_attended.1 = (bf16[8,128,256]{2,1,0:T(8,128)(2,1)S(1)}, bf16[8,128,256]{2,1,0:T(8,128)(2,1)}, bf16[8,128,256]{2,1,0:T(8,128)(2,1)}, bf16[8,128,256]{2,1,0:T(8,128)(2,1)S(1)}) custom-call(bf16[512,1024]{1,0:T(8,128)(2,1)S(1)} %constant_dynamic-update-slice_fusion.g_ref.refs_4_, bf16[4,2048,256]{2,1,0:T(8,128)(2,1)S(1)} %pad_maximum_fusion.w_ref.refs_4_), custom_call_target="tpu_custom_call" | custom-call | flops 2147483648 | bytes 6291456 | tf_op jit(solution)/shard_map/grad_attended/pallas_call | solution.py:208
  35.5 0.8 copy-done.5
  36.3 2.7 %collective-permute-start.8 = (bf16[8,128,256]{2,1,0:T(8,128)(2,1)}, bf16[8,128,256]{2,1,0:T(8,128)(2,1)}, u32[]{:S(2)}, u32[]{:S(2)}) collective-permute-start(bf16[8,128,256]{2,1,0:T(8,128)(2,1)} %get-tuple-element.40), channel_id=1, source_target_pairs={{0,48},{16,0},{32,16},{48,32},{1,49},{17,1},{33,17},{49,33},{2,50}... | collective-permute-start | bytes 1572872 | tf_op jit(solution)/shard_map/ppermute | solution.py:289
  39.0 0.9 collective-permute-start.10
  39.8 2.2 %all-to-all-done.q_ref.k_ref.v_ref = bf16[8,3,128,256]{3,2,1,0:T(8,128)(2,1)S(1)} async-done(((bf16[8,3,128,256]{3,2,1,0:T(8,128)(2,1)}), bf16[8,3,128,256]{3,2,1,0:T(8,128)(2,1)S(1)}, u32[]{:S(2)}, u32[]{:S(2)}) %all-to-all-start) | async-done | bytes 1572896 | tf_op jit(solution)/shard_map/all_to_all | solution.py:297
  42.0 6.9 %attend.1 = (bf16[8,128,256]{2,1,0:T(8,128)(2,1)}, f32[2,1,1024]{2,1,0:T(1,128)S(1)}) custom-call(bf16[8,3,128,256]{3,2,1,0:T(8,128)(2,1)S(1)} %all-to-all-done.q_ref.k_ref.v_ref, bf16[8,3,128,256]{3,2,1,0:T(8,128)(2,1)S(1)} %all-to-all-done.q_ref.k_ref.v_ref, bf16[8,3,128,256]{3,2,1,0:T(8,128)(2,1)S(1)} %all-to-all-done.q_ref.k_ref.v_ref), custom_call_target="tpu_custom_call" | custom-call | flops 2147483648 | bytes 2097152 | tf_op jit(solution)/shard_map/attend/pallas_call | solution.py:127
  48.9 16.7 %all-to-all-start.1 = ((bf16[8,128,256]{2,1,0:T(8,128)(2,1)}), bf16[8,128,256]{2,1,0:T(8,128)(2,1)S(1)}, u32[]{:S(2)}, u32[]{:S(2)}) async-start(bf16[8,128,256]{2,1,0:T(8,128)(2,1)} %get-tuple-element.44), calls=%async_computation.1 | async-start | bytes 1048576 | tf_op jit(solution)/shard_map/all_to_all | solution.py:297
  65.6 11.4 %all-to-all-done.1.refs_0_ = bf16[8,128,256]{2,1,0:T(8,128)(2,1)S(1)} async-done(((bf16[8,128,256]{2,1,0:T(8,128)(2,1)}), bf16[8,128,256]{2,1,0:T(8,128)(2,1)S(1)}, u32[]{:S(2)}, u32[]{:S(2)}) %all-to-all-start.1) | async-done | bytes 524320 | tf_op jit(solution)/shard_map/all_to_all | solution.py:297
  77.0 2.3 %collective-permute-start.13 = (bf16[8,128,256]{2,1,0:T(8,128)(2,1)S(1)}, bf16[8,128,256]{2,1,0:T(8,128)(2,1)S(1)}, u32[]{:S(2)}, u32[]{:S(2)}) collective-permute-start(bf16[8,128,256]{2,1,0:T(8,128)(2,1)S(1)} %all-to-all-done.1.refs_0_), channel_id=1, source_target_pairs={{0,48},{16,0},{32,16},{48,32},{1,49},{17,1},{33,17},{49,33},{2,50}... | collective-permute-start | bytes 1572872 | tf_op jit(solution)/shard_map/ppermute | solution.py:289
  79.4 1.5 collective-permute-start.12
  80.8 1.8 %add_convert_fusion.1 = bf16[8,128,256]{2,1,0:T(8,128)(2,1)S(1)} fusion(bf16[8,128,256]{2,1,0:T(8,128)(2,1)} %collective-permute-done.10, bf16[8,128,256]{2,1,0:T(8,128)(2,1)} %collective-permute-done.9, bf16[8,128,256]{2,1,0:T(8,128)(2,1)} %collective-permute-done.8, bf16[8,128,256]{2,1,0:T(8,128)(2,1)} %copy-done.5), kind=kLoop, calls=%fused_computation.5 | loop fusion | flops 2097152 | bytes 2621440 | tf_op jit(solution)/shard_map/convert_element_type | solution.py:333
  82.6 16.4 %all_to_all.20.g_ref = bf16[8,128,256]{2,1,0:T(8,128)(2,1)} all-to-all(bf16[8,128,256]{2,1,0:T(8,128)(2,1)S(1)} %add_convert_fusion.1), channel_id=1, replica_groups=mesh['yl'=2,'x'=4,'core'=2,'z'=4,'yh'=2] {'z','yh'}, dimensions={0} | all-to-all | bytes 1048576 | tf_op jit(solution)/shard_map/all_to_all | solution.py:297
  99.0 1.4 collective-permute-done.13.refs_3_
  100.4 3.7 %collective-permute-done.11.refs_1_ = bf16[8,128,256]{2,1,0:T(8,128)(2,1)S(1)} collective-permute-done((bf16[8,128,256]{2,1,0:T(8,128)(2,1)S(1)}, bf16[8,128,256]{2,1,0:T(8,128)(2,1)S(1)}, u32[]{:S(2)}, u32[]{:S(2)}) %collective-permute-start.11) | collective-permute-done | bytes 524320 | tf_op jit(solution)/shard_map/ppermute | solution.py:289
  104.1 2.9 %weight_parts.3 = bf16[2,8,256,256]{3,2,1,0:T(8,128)(2,1)S(1)} custom-call(bf16[8,128,256]{2,1,0:T(8,128)(2,1)S(1)} %all-to-all-done.1.refs_0_, bf16[8,128,256]{2,1,0:T(8,128)(2,1)S(1)} %collective-permute-done.11.refs_1_, bf16[8,128,256]{2,1,0:T(8,128)(2,1)S(1)} %collective-permute-done.12.refs_2_, ...), custom_call_target="tpu_custom_call" | custom-call | flops 1073741824 | bytes 5242880 | tf_op jit(solution)/shard_map/weight_parts/pallas_call | solution.py:242
  107.0 0.1 collective-permute-start.17
  107.1 3.0 %weight_parts.2 = bf16[2,8,256,256]{3,2,1,0:T(8,128)(2,1)S(1)} custom-call(bf16[8,128,256]{2,1,0:T(8,128)(2,1)S(1)} %all-to-all-done.1.refs_0_, bf16[8,128,256]{2,1,0:T(8,128)(2,1)S(1)} %collective-permute-done.11.refs_1_, bf16[8,128,256]{2,1,0:T(8,128)(2,1)S(1)} %collective-permute-done.12.refs_2_, ...), custom_call_target="tpu_custom_call" | custom-call | flops 1073741824 | bytes 5242880 | tf_op jit(solution)/shard_map/weight_parts/pallas_call | solution.py:242
  110.1 1.2 collective-permute-done.17
  111.3 2.0 %add_convert_fusion = bf16[2,8,256,256]{3,2,1,0:T(8,128)(2,1)} fusion(bf16[2,8,256,256]{3,2,1,0:T(8,128)(2,1)S(1)} %collective-permute-done.17, bf16[2,8,256,256]{3,2,1,0:T(8,128)(2,1)S(1)} %weight_parts.2), kind=kLoop, calls=%fused_computation.2 | loop fusion | flops 4194304 | bytes 6291456 | tf_op jit(solution)/shard_map/convert_element_type | solution.py:338
  113.3 7.3 %all-to-all-start.3 = ((bf16[16,256,256]{2,1,0:T(8,128)(2,1)}), bf16[16,256,256]{2,1,0:T(8,128)(2,1)}, u32[]{:S(2)}, u32[]{:S(2)}) async-start(bf16[16,256,256]{2,1,0:T(8,128)(2,1)} %bitcast.19), calls=%async_computation.3 | async-start | bytes 4194304 | tf_op jit(solution)/shard_map/all_to_all | solution.py:297
  120.6 2.2 %copy-done.1 = bf16[4,2048,256]{2,1,0:T(8,128)(2,1)S(1)} copy-done((bf16[4,2048,256]{2,1,0:T(8,128)(2,1)S(1)}, bf16[4,2048,256]{2,1,0:T(8,128)(2,1)}, u32[]{:S(2)}) %copy-start.1) | copy-done | bytes 4194328
  122.8 3.2 %project.1 = (bf16[128,1024]{1,0:T(8,128)(2,1)S(1)}, bf16[128,1024]{1,0:T(8,128)(2,1)S(1)}, bf16[128,1024]{1,0:T(8,128)(2,1)S(1)}, bf16[128,1024]{1,0:T(8,128)(2,1)S(1)}) custom-call(bf16[8,128,256]{2,1,0:T(8,128)(2,1)S(1)} %all-to-all-done.1.refs_0_, bf16[8,128,256]{2,1,0:T(8,128)(2,1)S(1)} %collective-permute-done.11.refs_1_, ...), custom_call_target="tpu_custom_call" | custom-call | flops 2147483648 | bytes 7340032 | tf_op jit(solution)/shard_map/project/pallas_call | solution.py:274
  126.0 1.4 collective-permute-start.14
  127.4 0.2 collective-permute-start.15
  127.6 0.8 collective-permute-start.16
  128.5 8.3 %attend_back.1 = (bf16[1024,256]{1,0:T(8,128)(2,1)}, bf16[1024,256]{1,0:T(8,128)(2,1)}, bf16[1024,256]{1,0:T(8,128)(2,1)}) custom-call(bf16[8,3,128,256]{3,2,1,0:T(8,128)(2,1)S(1)} %copy-done.3, bf16[8,3,128,256]{3,2,1,0:T(8,128)(2,1)S(1)} %copy-done.3, bf16[8,3,128,256]{3,2,1,0:T(8,128)(2,1)S(1)} %copy-done.3, f32[2,1,1024]{2,1,0:T(1,128)S(1)} %get-tuple-element.50.lse_ref, ...), custom_call_target="tpu_custom_call" | custom-call | flops 5368709120 | bytes 3670016 | tf_op jit(solution)/shard_map/attend_back/pallas_call | solution.py:176
  136.8 1.4 collective-permute-done.15.refs_2_
  138.2 4.1 %collective-permute-done.16.refs_3_ = bf16[128,1024]{1,0:T(8,128)(2,1)S(1)} collective-permute-done((bf16[128,1024]{1,0:T(8,128)(2,1)S(1)}, bf16[128,1024]{1,0:T(8,128)(2,1)S(1)}, u32[]{:S(2)}, u32[]{:S(2)}) %collective-permute-start.16) | collective-permute-done | bytes 262176 | tf_op jit(solution)/shard_map/ppermute | solution.py:289
  142.3 1.1 place_projected.1
  143.4 11.0 %all-to-all-done.3 = bf16[16,256,256]{2,1,0:T(8,128)(2,1)} async-done(((bf16[16,256,256]{2,1,0:T(8,128)(2,1)}), bf16[16,256,256]{2,1,0:T(8,128)(2,1)}, u32[]{:S(2)}, u32[]{:S(2)}) %all-to-all-start.3) | async-done | bytes 2097184 | tf_op jit(solution)/shard_map/all_to_all | solution.py:297
  154.4 2.6 %convert_reduce_fusion = f32[256,256]{1,0:T(8,128)} fusion(bf16[16,256,256]{2,1,0:T(8,128)(2,1)} %all-to-all-done.3), kind=kLoop, calls=%fused_computation.1 | loop fusion | flops 2031616 | bytes 2359296 | tf_op jit(solution)/shard_map/reduce_sum | solution.py:340
  (37 shorter events, 0.2 us)
Async XLA Ops:
  0.6 6.3 %copy-start.4 = (bf16[1,128,4096]{2,1,0:T(8,128)(2,1)S(1)}, bf16[1,128,4096]{2,1,0:T(8,128)(2,1)}, u32[]{:S(2)}) copy-start(bf16[1,128,4096]{2,1,0:T(8,128)(2,1)} %param.9) | copy-start | bytes 3145732
  0.6 11.3 %copy-start.9 = (bf16[1,128,2048]{2,1,0:T(8,128)(2,1)S(1)}, bf16[1,128,2048]{2,1,0:T(8,128)(2,1)}, u32[]{:S(2)}) copy-start(bf16[1,128,2048]{2,1,0:T(8,128)(2,1)} %param.7) | copy-start | bytes 1572868
  0.7 11.3 %copy-start.8 = (bf16[1,128,2048]{2,1,0:T(8,128)(2,1)S(1)}, bf16[1,128,2048]{2,1,0:T(8,128)(2,1)}, u32[]{:S(2)}) copy-start(bf16[1,128,2048]{2,1,0:T(8,128)(2,1)} %param.6) | copy-start | bytes 1572868
  0.7 11.3 %copy-start.7 = (bf16[1,128,2048]{2,1,0:T(8,128)(2,1)S(1)}, bf16[1,128,2048]{2,1,0:T(8,128)(2,1)}, u32[]{:S(2)}) copy-start(bf16[1,128,2048]{2,1,0:T(8,128)(2,1)} %param.5) | copy-start | bytes 1572868
  3.1 17.2 %collective-permute-start.4 = (bf16[1024,256]{1,0:T(8,128)(2,1)}, bf16[1024,256]{1,0:T(8,128)(2,1)}, u32[]{:S(2)}, u32[]{:S(2)}) collective-permute-start(bf16[1024,256]{1,0:T(8,128)(2,1)} %get-tuple-element.30), channel_id=1, source_target_pairs={{0,64},{64,0},{1,65},{65,1},{2,66},{66,2},{3,67},{67,3},{4,68},{68... | collective-permute-start | bytes 1572872 | tf_op jit(solution)/shard_map/ppermute | solution.py:293
  4.7 15.7 %collective-permute-start.5 = (bf16[1024,256]{1,0:T(8,128)(2,1)}, bf16[1024,256]{1,0:T(8,128)(2,1)}, u32[]{:S(2)}, u32[]{:S(2)}) collective-permute-start(bf16[1024,256]{1,0:T(8,128)(2,1)} %get-tuple-element.31), channel_id=1, source_target_pairs={{0,65},{1,64},{64,1},{65,0},{2,67},{3,66},{66,3},{67,2},{4,69},{5,... | collective-permute-start | bytes 1572872 | tf_op jit(solution)/shard_map/ppermute | solution.py:318
  7.8 11.0 %collective-permute-start = (bf16[128,1024]{1,0:T(8,128)(2,1)}, bf16[128,1024]{1,0:T(8,128)(2,1)}, u32[]{:S(2)}, u32[]{:S(2)}) collective-permute-start(bf16[128,1024]{1,0:T(8,128)(2,1)} %get-tuple-element.36), channel_id=1, source_target_pairs={{0,16},{16,32},{32,48},{48,0},{1,17},{17,33},{33,49},{49,1},{2,18}... | collective-permute-start | bytes 786440 | tf_op jit(solution)/shard_map/ppermute | solution.py:289
  9.2 19.2 %collective-permute-start.3 = (bf16[2048,256]{1,0:T(8,128)(2,1)}, bf16[2048,256]{1,0:T(8,128)(2,1)}, u32[]{:S(2)}, u32[]{:S(2)}) collective-permute-start(bf16[2048,256]{1,0:T(8,128)(2,1)} %param.8), channel_id=1, source_target_pairs={{0,8},{8,0},{1,9},{9,1},{2,10},{10,2},{3,11},{11,3},{4,12},{12,4},... | collective-permute-start | bytes 3145736 | tf_op jit(solution)/shard_map/ppermute | solution.py:293
  9.2 14.1 %collective-permute-start.1 = (bf16[128,1024]{1,0:T(8,128)(2,1)S(1)}, bf16[128,1024]{1,0:T(8,128)(2,1)}, u32[]{:S(2)}, u32[]{:S(2)}) collective-permute-start(bf16[128,1024]{1,0:T(8,128)(2,1)S(1)} %get-tuple-element.37), channel_id=1, source_target_pairs={{0,32},{16,48},{32,0},{48,16},{1,33},{17,49},{33,1},{49,17},{2,34}... | collective-permute-start | bytes 786440 | tf_op jit(solution)/shard_map/ppermute | solution.py:289
  13.3 28.7 %all-to-all-start = ((bf16[8,3,128,256]{3,2,1,0:T(8,128)(2,1)}), bf16[8,3,128,256]{3,2,1,0:T(8,128)(2,1)S(1)}, u32[]{:S(2)}, u32[]{:S(2)}) async-start(bf16[8,3,128,256]{3,2,1,0:T(8,128)(2,1)} %pack_qkv.1), calls=%async_computation | async-start | bytes 3145728 | tf_op jit(solution)/shard_map/all_to_all | solution.py:297
  18.7 8.2 %collective-permute-start.2 = (bf16[128,1024]{1,0:T(8,128)(2,1)S(1)}, bf16[128,1024]{1,0:T(8,128)(2,1)S(1)}, u32[]{:S(2)}, u32[]{:S(2)}) collective-permute-start(bf16[128,1024]{1,0:T(8,128)(2,1)S(1)} %get-tuple-element.38), channel_id=1, source_target_pairs={{0,48},{16,0},{32,16},{48,32},{1,49},{17,1},{33,17},{49,33},{2,50}... | collective-permute-start | bytes 786440 | tf_op jit(solution)/shard_map/ppermute | solution.py:289
  20.3 8.1 %collective-permute-start.6 = (bf16[1024,256]{1,0:T(8,128)(2,1)}, bf16[1024,256]{1,0:T(8,128)(2,1)S(1)}, u32[]{:S(2)}, u32[]{:S(2)}) collective-permute-start(bf16[1024,256]{1,0:T(8,128)(2,1)} %collective-permute-done.4), channel_id=1, source_target_pairs={{0,8},{8,0},{1,9},{9,1},{2,10},{10,2},{3,11},{11,3},{4,12},{12,4},... | collective-permute-start | bytes 1572872 | tf_op jit(solution)/shard_map/ppermute | solution.py:293
  20.4 8.0 %collective-permute-start.7 = (bf16[1024,256]{1,0:T(8,128)(2,1)}, bf16[1024,256]{1,0:T(8,128)(2,1)S(1)}, u32[]{:S(2)}, u32[]{:S(2)}) collective-permute-start(bf16[1024,256]{1,0:T(8,128)(2,1)} %collective-permute-done.5), channel_id=1, source_target_pairs={{0,8},{8,0},{1,9},{9,1},{2,10},{10,2},{3,11},{11,3},{4,12},{12,4},... | collective-permute-start | bytes 1572872 | tf_op jit(solution)/shard_map/ppermute | solution.py:293
  27.0 1.5 copy-start.10
  30.1 5.4 %copy-start = (bf16[4,2048,256]{2,1,0:T(8,128)(2,1)}, bf16[4,2048,256]{2,1,0:T(8,128)(2,1)S(1)}, u32[]{:S(2)}) copy-start(bf16[4,2048,256]{2,1,0:T(8,128)(2,1)S(1)} %pad_maximum_fusion.w_ref.refs_4_) | copy-start | bytes 12582916
  35.5 0.8 copy-start.5
  36.3 29.2 %collective-permute-start.8 = (bf16[8,128,256]{2,1,0:T(8,128)(2,1)}, bf16[8,128,256]{2,1,0:T(8,128)(2,1)}, u32[]{:S(2)}, u32[]{:S(2)}) collective-permute-start(bf16[8,128,256]{2,1,0:T(8,128)(2,1)} %get-tuple-element.40), channel_id=1, source_target_pairs={{0,48},{16,0},{32,16},{48,32},{1,49},{17,1},{33,17},{49,33},{2,50}... | collective-permute-start | bytes 1572872 | tf_op jit(solution)/shard_map/ppermute | solution.py:289
  39.0 26.6 %collective-permute-start.9 = (bf16[8,128,256]{2,1,0:T(8,128)(2,1)}, bf16[8,128,256]{2,1,0:T(8,128)(2,1)}, u32[]{:S(2)}, u32[]{:S(2)}) collective-permute-start(bf16[8,128,256]{2,1,0:T(8,128)(2,1)} %get-tuple-element.41), channel_id=1, source_target_pairs={{0,32},{16,48},{32,0},{48,16},{1,33},{17,49},{33,1},{49,17},{2,34}... | collective-permute-start | bytes 1572872 | tf_op jit(solution)/shard_map/ppermute | solution.py:289
  39.0 26.6 %collective-permute-start.10 = (bf16[8,128,256]{2,1,0:T(8,128)(2,1)S(1)}, bf16[8,128,256]{2,1,0:T(8,128)(2,1)}, u32[]{:S(2)}, u32[]{:S(2)}) collective-permute-start(bf16[8,128,256]{2,1,0:T(8,128)(2,1)S(1)} %get-tuple-element.42), channel_id=1, source_target_pairs={{0,16},{16,32},{32,48},{48,0},{1,17},{17,33},{33,49},{49,1},{2,18}... | collective-permute-start | bytes 1572872 | tf_op jit(solution)/shard_map/ppermute | solution.py:289
  42.0 6.9 %copy-start.2 = (bf16[8,3,128,256]{3,2,1,0:T(8,128)(2,1)}, bf16[8,3,128,256]{3,2,1,0:T(8,128)(2,1)S(1)}, u32[]{:S(2)}) copy-start(bf16[8,3,128,256]{3,2,1,0:T(8,128)(2,1)S(1)} %all-to-all-done.q_ref.k_ref.v_ref) | copy-start | bytes 4718596
  48.9 28.2 %all-to-all-start.1 = ((bf16[8,128,256]{2,1,0:T(8,128)(2,1)}), bf16[8,128,256]{2,1,0:T(8,128)(2,1)S(1)}, u32[]{:S(2)}, u32[]{:S(2)}) async-start(bf16[8,128,256]{2,1,0:T(8,128)(2,1)} %get-tuple-element.44), calls=%async_computation.1 | async-start | bytes 1048576 | tf_op jit(solution)/shard_map/all_to_all | solution.py:297
  77.0 23.4 %collective-permute-start.13 = (bf16[8,128,256]{2,1,0:T(8,128)(2,1)S(1)}, bf16[8,128,256]{2,1,0:T(8,128)(2,1)S(1)}, u32[]{:S(2)}, u32[]{:S(2)}) collective-permute-start(bf16[8,128,256]{2,1,0:T(8,128)(2,1)S(1)} %all-to-all-done.1.refs_0_), channel_id=1, source_target_pairs={{0,48},{16,0},{32,16},{48,32},{1,49},{17,1},{33,17},{49,33},{2,50}... | collective-permute-start | bytes 1572872 | tf_op jit(solution)/shard_map/ppermute | solution.py:289
  79.4 21.1 %collective-permute-start.12 = (bf16[8,128,256]{2,1,0:T(8,128)(2,1)S(1)}, bf16[8,128,256]{2,1,0:T(8,128)(2,1)S(1)}, u32[]{:S(2)}, u32[]{:S(2)}) collective-permute-start(bf16[8,128,256]{2,1,0:T(8,128)(2,1)S(1)} %all-to-all-done.1.refs_0_), channel_id=1, source_target_pairs={{0,32},{16,48},{32,0},{48,16},{1,33},{17,49},{33,1},{49,17},{2,34}... | collective-permute-start | bytes 1572872 | tf_op jit(solution)/shard_map/ppermute | solution.py:289
  80.8 23.3 %collective-permute-start.11 = (bf16[8,128,256]{2,1,0:T(8,128)(2,1)S(1)}, bf16[8,128,256]{2,1,0:T(8,128)(2,1)S(1)}, u32[]{:S(2)}, u32[]{:S(2)}) collective-permute-start(bf16[8,128,256]{2,1,0:T(8,128)(2,1)S(1)} %all-to-all-done.1.refs_0_), channel_id=1, source_target_pairs={{0,16},{16,32},{32,48},{48,0},{1,17},{17,33},{33,49},{49,1},{2,18}... | collective-permute-start | bytes 1572872 | tf_op jit(solution)/shard_map/ppermute | solution.py:289
  107.0 4.2 %collective-permute-start.17 = (bf16[2,8,256,256]{3,2,1,0:T(8,128)(2,1)S(1)}, bf16[2,8,256,256]{3,2,1,0:T(8,128)(2,1)S(1)}, u32[]{:S(2)}, u32[]{:S(2)}) collective-permute-start(bf16[2,8,256,256]{3,2,1,0:T(8,128)(2,1)S(1)} %weight_parts.3), channel_id=1, source_target_pairs={{0,8},{8,0},{1,9},{9,1},{2,10},{10,2},{3,11},{11,3},{4,12},{12,4},... | collective-permute-start | bytes 6291464 | tf_op jit(solution)/shard_map/ppermute | solution.py:293
  113.3 41.1 %all-to-all-start.3 = ((bf16[16,256,256]{2,1,0:T(8,128)(2,1)}), bf16[16,256,256]{2,1,0:T(8,128)(2,1)}, u32[]{:S(2)}, u32[]{:S(2)}) async-start(bf16[16,256,256]{2,1,0:T(8,128)(2,1)} %bitcast.19), calls=%async_computation.3 | async-start | bytes 4194304 | tf_op jit(solution)/shard_map/all_to_all | solution.py:297
  120.6 2.2 %copy-start.1 = (bf16[4,2048,256]{2,1,0:T(8,128)(2,1)S(1)}, bf16[4,2048,256]{2,1,0:T(8,128)(2,1)}, u32[]{:S(2)}) copy-start(bf16[4,2048,256]{2,1,0:T(8,128)(2,1)} %copy-done) | copy-start | bytes 12582916
  122.8 5.7 %copy-start.3 = (bf16[8,3,128,256]{3,2,1,0:T(8,128)(2,1)S(1)}, bf16[8,3,128,256]{3,2,1,0:T(8,128)(2,1)}, u32[]{:S(2)}) copy-start(bf16[8,3,128,256]{3,2,1,0:T(8,128)(2,1)} %copy-done.2) | copy-start | bytes 4718596
  122.8 5.7 %copy-start.6 = (bf16[8,128,256]{2,1,0:T(8,128)(2,1)S(1)}, bf16[8,128,256]{2,1,0:T(8,128)(2,1)}, u32[]{:S(2)}) copy-start(bf16[8,128,256]{2,1,0:T(8,128)(2,1)} %all_to_all.20.g_ref) | copy-start | bytes 1572868
  126.0 10.8 %collective-permute-start.14 = (bf16[128,1024]{1,0:T(8,128)(2,1)S(1)}, bf16[128,1024]{1,0:T(8,128)(2,1)S(1)}, u32[]{:S(2)}, u32[]{:S(2)}) collective-permute-start(bf16[128,1024]{1,0:T(8,128)(2,1)S(1)} %get-tuple-element.47), channel_id=1, source_target_pairs={{0,48},{16,0},{32,16},{48,32},{1,49},{17,1},{33,17},{49,33},{2,50}... | collective-permute-start | bytes 786440 | tf_op jit(solution)/shard_map/ppermute | solution.py:289
  127.4 10.8 %collective-permute-start.15 = (bf16[128,1024]{1,0:T(8,128)(2,1)S(1)}, bf16[128,1024]{1,0:T(8,128)(2,1)S(1)}, u32[]{:S(2)}, u32[]{:S(2)}) collective-permute-start(bf16[128,1024]{1,0:T(8,128)(2,1)S(1)} %get-tuple-element.48), channel_id=1, source_target_pairs={{0,32},{16,48},{32,0},{48,16},{1,33},{17,49},{33,1},{49,17},{2,34}... | collective-permute-start | bytes 786440 | tf_op jit(solution)/shard_map/ppermute | solution.py:289
  127.6 14.7 %collective-permute-start.16 = (bf16[128,1024]{1,0:T(8,128)(2,1)S(1)}, bf16[128,1024]{1,0:T(8,128)(2,1)S(1)}, u32[]{:S(2)}, u32[]{:S(2)}) collective-permute-start(bf16[128,1024]{1,0:T(8,128)(2,1)S(1)} %get-tuple-element.49), channel_id=1, source_target_pairs={{0,16},{16,32},{32,48},{48,0},{1,17},{17,33},{33,49},{49,1},{2,18}... | collective-permute-start | bytes 786440 | tf_op jit(solution)/shard_map/ppermute | solution.py:289

commit v2 on v1

--- a/solution.py
+++ b/solution.py
@@ -12,6 +12,7 @@
 SEQ = ("z", "yh")
 BLOCK = 256
 SCALE = HEAD ** (-0.5)
+LOG2E = 1.4426950408889634
 MIB = 1 << 20
 
 
@@ -108,36 +109,38 @@
 def attend(qkv):
     groups, _, tok, width = qkv.shape
     heads, length = width // HEAD, groups * tok
-    rows = 256
 
     def body(q_ref, k_ref, v_ref, o_ref, lse_ref):
-        keys = k_ref[...].reshape(length, HEAD)
-        values = v_ref[...].reshape(length, HEAD)
-        for b in range(length // rows):
-            per = rows // tok
-            query = q_ref[b * per : (b + 1) * per].reshape(rows, HEAD)
-            scores = nt(keys, query) * SCALE
-            peak = jnp.max(scores, axis=0, keepdims=True)
-            shifted = jnp.exp(scores - peak)
-            total = jnp.sum(shifted, axis=0, keepdims=True)
-            out = tn(values, shifted.astype(jnp.bfloat16)) / total
-            o_ref[b * per : (b + 1) * per] = out.T.astype(jnp.bfloat16).reshape(per, tok, HEAD)
-            lse_ref[:, b * rows : (b + 1) * rows] = peak + jnp.log(total)
-
-    return pl.pallas_call(
-        body,
-        grid=(heads,),
+        for h in range(heads):
+            cols = slice(h * HEAD, (h + 1) * HEAD)
+            keys = k_ref[:, :, cols].reshape(length, HEAD)
+            values = v_ref[:, :, cols].reshape(length, HEAD)
+            for b in range(groups):
+                scores = nt(keys, q_ref[b, :, cols]) * (SCALE * LOG2E)
+                peak = jnp.max(scores, axis=0, keepdims=True)
+                shifted = jnp.exp2(scores - peak)
+                total = jnp.sum(shifted, axis=0, keepdims=True)
+                out = tn(values, shifted.astype(jnp.bfloat16)) / total
+                o_ref[b, :, cols] = out.T.astype(jnp.bfloat16)
+                lse_ref[h, :, b * tok : (b + 1) * tok] = peak + jnp.log2(total)
+
+    return pl.pallas_call(
+        body,
+        grid=(1,),
         out_shape=[
             jax.ShapeDtypeStruct((groups, tok, width), jnp.bfloat16),
             jax.ShapeDtypeStruct((heads, 1, length), jnp.float32),
         ],
-        in_specs=[head_spec(groups, tok, i) for i in range(3)],
+        in_specs=[
+            pl.BlockSpec((groups, pl.squeezed, tok, width), lambda n, i=i: (0, i, 0, 0))
+            for i in range(3)
+        ],
         out_specs=[
-            pl.BlockSpec((groups, tok, HEAD), lambda h: (0, 0, h)),
-            pl.BlockSpec((pl.squeezed, 1, length), lambda h: (h, 0, 0)),
+            pl.BlockSpec((groups, tok, width), lambda n: (0, 0, 0)),
+            pl.BlockSpec((heads, 1, length), lambda n: (0, 0, 0)),
         ],
         compiler_params=params(32),
-        cost_estimate=cost(8 * heads * length * length * HEAD, 8 * length * width, heads * length * length),
+        cost_estimate=cost(4 * heads * length * length * HEAD, 8 * length * width, heads * length * length),
         name="attend",
     )(qkv, qkv, qkv)
 
@@ -154,8 +157,8 @@
             per = rows // tok
             query = q_ref[b * per : (b + 1) * per].reshape(rows, HEAD)
             grad_rows = g_ref[b * per : (b + 1) * per].reshape(rows, HEAD)
-            scores = nt(keys, query) * SCALE
-            probs = jnp.exp(scores - lse_ref[:, b * rows : (b + 1) * rows])
+            scores = nt(keys, query) * (SCALE * LOG2E)
+            probs = jnp.exp2(scores - lse_ref[:, b * rows : (b + 1) * rows])
             grad_probs = nt(values, grad_rows)
             delta = jnp.sum(probs * grad_probs, axis=0, keepdims=True)
             grad_scores = (probs * (grad_probs - delta)).astype(jnp.bfloat16)
@@ -220,12 +223,14 @@
     )(grads, weights)
 
 
-def weight_parts(attended, grads, core):
+def weight_parts(attended, grads, core, other=None):
     groups, tok, block = attended[0].shape
-    rows = X * tok
+    rows, step = X * tok, 4
+
+    extra = [] if other is None else [other]
 
     def body(*refs):
-        a_refs, g_ref, out, cols = refs[:X], refs[X], refs[X + 1], refs[X + 2]
+        a_refs, g_ref, out, cols = refs[:X], refs[X], refs[-2], refs[-1]
 
         @pl.when(pl.program_id(0) == 0)
         def _():
@@ -233,24 +238,32 @@
                 j = 2 * i + core
                 cols[:, i * block : (i + 1) * block] = g_ref[:, j * block : (j + 1) * block]
 
-        left = jnp.concatenate([a[...] for a in a_refs], axis=0)
-        piece = tn(left, cols[...]).astype(jnp.bfloat16)
+        left = jnp.concatenate(
+            [jnp.concatenate([a[i] for i in range(step)], axis=1) for a in a_refs], axis=0
+        )
+        piece = tn(left, cols[...])
         yl = lax.axis_index("yl")
-        for i in range(2):
-            out[yl + i - 2 * yl * i] = piece[:, i * block : (i + 1) * block]
-
-    return pl.pallas_call(
-        body,
-        grid=(groups,),
+        for g in range(step):
+            for i in range(2):
+                part = piece[g * block : (g + 1) * block, i * block : (i + 1) * block]
+                at = yl + i - 2 * yl * i
+                if other is not None:
+                    part = part + refs[X + 1][at, g].astype(jnp.float32)
+                out[at, g] = part.astype(jnp.bfloat16)
+
+    return pl.pallas_call(
+        body,
+        grid=(groups // step,),
         out_shape=jax.ShapeDtypeStruct((2, groups, block, block), jnp.bfloat16),
-        in_specs=[pl.BlockSpec((pl.squeezed, tok, block), lambda n: (n, 0, 0))] * X
-        + [pl.BlockSpec(grads.shape, lambda n: (0, 0))],
-        out_specs=pl.BlockSpec((2, pl.squeezed, block, block), lambda n: (0, n, 0, 0)),
+        in_specs=[pl.BlockSpec((step, tok, block), lambda n: (n, 0, 0))] * X
+        + [pl.BlockSpec(grads.shape, lambda n: (0, 0))]
+        + [pl.BlockSpec((2, step, block, block), lambda n: (0, n, 0, 0))] * len(extra),
+        out_specs=pl.BlockSpec((2, step, block, block), lambda n: (0, n, 0, 0)),
         scratch_shapes=[pltpu.VMEM((rows, 2 * block), jnp.bfloat16)],
-        compiler_params=params(24),
+        compiler_params=params(32),
         cost_estimate=cost(4 * rows * groups * block * block, 5 * MIB),
         name="weight_parts",
-    )(*attended, grads)
+    )(*attended, grads, *extra)
 
 
 def project(attended, weights):
@@ -312,12 +325,11 @@
     cols = grad_out.shape[2]
     half = out_weight.shape[0] // 2
 
-    lower, upper = lax.optimization_barrier((out_weight[:half], out_weight[half:]))
-    query, key, value = after((query_input[0], key_input[0], value_input[0]), lower, upper)
-    lower = swap(lower, "yl")
-    upper = lax.ppermute(upper, ("yl", "yh"), [(i, 3 - i) for i in range(4)])
-    qkv = exchange(pack_qkv(query, key, value))
-    mine = pack_grad(grad_out[0])
+    lower = swap(out_weight[:half], "yl")
+    upper = lax.ppermute(out_weight[half:], ("yl", "yh"), [(i, 3 - i) for i in range(4)])
+    packed = pack_qkv(query_input[0], key_input[0], value_input[0])
+    qkv = exchange(after(packed, lower, upper))
+    mine = pack_grad(after(grad_out, packed)[0])
     grads = [mine[0]] + [shift_x(mine[s], s) for s in range(1, X)]
     grads = jnp.concatenate(grads, axis=0)
     weights = [out_weight, swap(out_weight, "core")]
@@ -334,16 +346,15 @@
 
     grads = after(grads, grad_attended)
     far = swap(weight_parts(rows, grads, 1), "core")
-    near = weight_parts(rows, grads, 0)
-    total = f32_sum(near, far).astype(jnp.bfloat16)
+    total = weight_parts(rows, grads, 0, far)
     total = exchange(total.reshape(-1, BLOCK, BLOCK), ("yl", *SEQ))
     grad_weight = jnp.sum(total.astype(jnp.float32), axis=0)
 
-    projected = project(rows, weights)
+    grads_in = attend_back(qkv, lse, grad_attended)
+    projected = project(rows, after(weights, grads_in[0]))
     projected = [projected[0]] + [shift_x(projected[s], -s) for s in range(1, X)]
     projected = place_projected(projected, cols)[None]
 
-    grads_in = attend_back(qkv, lse, grad_attended)
     return (projected, *[g[None] for g in grads_in], grad_weight)
 
 

time: 158 us -> 148 us (0.937)
  starting transfers between devices: 49.5 us -> 36.8 us
  waiting for transfers between devices: 40.5 us -> 49.7 us
  Pallas kernels: 32.8 us -> 26.7 us
  other arithmetic: 9.46 us -> 7.53 us
    ppermute x12, waiting for transfers between devices: 14.8 us -> 29.4 us  [shift_x(): return lax.ppermute(array, 'x', [(i, (i + shift) % X) for i in range(X)])]
    all_to_all x3, waiting for transfers between devices: 24.6 us -> 10.2 us  [exchange(): return lax.all_to_all(array, axes, 0, 0, tiled=False)]
    all_to_all x3, starting transfers between devices: 29.4 us -> 18.5 us  [exchange(): return lax.all_to_all(array, axes, 0, 0, tiled=False)]
    ppermute x1, waiting for transfers between devices: 0.01 us -> 6.04 us  [shards(): lax.ppermute(out_weight[half:], ('yl', 'yh'), [(i, 3 - i) for i in range(...]
    pallas_call x3, Pallas kernels: 12.7 us -> 7.11 us  [the longest x2 3.59 us: weight_parts(): pl.pallas_call(body, grid=(groups // step,), out_shape=jax.ShapeDtypeStru...]
    ppermute x5, waiting for transfers between devices: 1.19 us -> 4.15 us  [swap(): return lax.ppermute(array, axis, [(0, 1), (1, 0)])]
    convert_element_type x1 -> x0, other arithmetic: 2.05 us -> none  [shards(): total = f32_sum(near, far).astype(jnp.bfloat16)]
    ppermute x5, starting transfers between devices: 2.33 us -> 0.74 us  [swap(): return lax.ppermute(array, axis, [(0, 1), (1, 0)])]
  transfers between devices with their start and end apart: 21 -> 21, of which waited for: 10 -> 10; matrix products, arithmetic and copies ran while one was open for 4% -> 5% of each run, Pallas kernels for 19% -> 16%
where the time goes in v2:
time: 148 us
  waiting for transfers between devices  49.7 us (34%)
  starting transfers between devices  36.8 us (25%)
  Pallas kernels  26.7 us (18%)
  blocking collectives  17.6 us (12%)
  local copies, waits for them, and re-layouts  8.42 us (6%)
  other arithmetic  7.53 us (5%)
    ppermute x12, waiting for transfers between devices, shift_x(): return lax.ppermute(array, 'x', [(i, (i + shift) % X) for i in range(X)])  29.4 us
    all_to_all x3, starting transfers between devices, exchange(): return lax.all_to_all(array, axes, 0, 0, tiled=False)  18.5 us
    all_to_all x1, blocking collectives, exchange(): return lax.all_to_all(array, axes, 0, 0, tiled=False)  17.6 us
    ppermute x12, starting transfers between devices, shift_x(): return lax.ppermute(array, 'x', [(i, (i + shift) % X) for i in range(X)])  14.4 us
    all_to_all x3, waiting for transfers between devices, exchange(): return lax.all_to_all(array, axes, 0, 0, tiled=False)  10.2 us
    pallas_call x1, Pallas kernels, attend_back(): pl.pallas_call(body, grid=(heads,), out_shape=[out] * 3, in_specs=[head_s...  8.31 us
    unnamed x37, local copies, waits for them, and re-layouts  6.07 us
    ppermute x1, waiting for transfers between devices, shards(): lax.ppermute(out_weight[half:], ('yl', 'yh'), [(i, 3 - i) for i in range(...  6.04 us
  transfers between devices with their start and end apart: 21, of which 10 were waited for; matrix products, arithmetic and copies ran while one was open for 5% of the time, Pallas kernels for 16%

profile of v2, /device:TPU:0, one launch (start us, length us, event | category | flops | bytes accessed | tf_op | source)
XLA Modules:
  0.0 147.8 jit_solution(14288802611514130306)
XLA Ops:
  0.7 1.4 fusion
  2.1 3.2 %collective-permute-start.1 = (bf16[1024,256]{1,0:T(8,128)(2,1)S(1)}, bf16[1024,256]{1,0:T(8,128)(2,1)S(1)}, u32[]{:S(2)}, u32[]{:S(2)}) collective-permute-start(bf16[1024,256]{1,0:T(8,128)(2,1)S(1)} %get-tuple-element.51), channel_id=1, source_target_pairs={{0,65},{1,64},{64,1},{65,0},{2,67},{3,66},{66,3},{67,2},{4,69},{5,... | collective-permute-start | bytes 1572872 | tf_op jit(solution)/shard_map/ppermute | solution.py:329
  5.4 1.3 pack_qkv.1
  6.7 0.1 pack_grad.1
  6.8 1.6 %collective-permute-start.2 = (bf16[128,1024]{1,0:T(8,128)(2,1)S(1)}, bf16[128,1024]{1,0:T(8,128)(2,1)}, u32[]{:S(2)}, u32[]{:S(2)}) collective-permute-start(bf16[128,1024]{1,0:T(8,128)(2,1)S(1)} %get-tuple-element.31), channel_id=1, source_target_pairs={{0,16},{16,32},{32,48},{48,0},{1,17},{17,33},{33,49},{49,1},{2,18}... | collective-permute-start | bytes 786440 | tf_op jit(solution)/shard_map/ppermute | solution.py:302
  8.4 2.7 %collective-permute-start.3 = (bf16[128,1024]{1,0:T(8,128)(2,1)S(1)}, bf16[128,1024]{1,0:T(8,128)(2,1)}, u32[]{:S(2)}, u32[]{:S(2)}) collective-permute-start(bf16[128,1024]{1,0:T(8,128)(2,1)S(1)} %get-tuple-element.32), channel_id=1, source_target_pairs={{0,32},{16,48},{32,0},{48,16},{1,33},{17,49},{33,1},{49,17},{2,34}... | collective-permute-start | bytes 786440 | tf_op jit(solution)/shard_map/ppermute | solution.py:302
  11.1 6.0 %collective-permute-done.1 = bf16[1024,256]{1,0:T(8,128)(2,1)S(1)} collective-permute-done((bf16[1024,256]{1,0:T(8,128)(2,1)S(1)}, bf16[1024,256]{1,0:T(8,128)(2,1)S(1)}, u32[]{:S(2)}, u32[]{:S(2)}) %collective-permute-start.1) | collective-permute-done | bytes 524320 | tf_op jit(solution)/shard_map/ppermute | solution.py:329
  17.2 2.8 %collective-permute-start.4 = (bf16[128,1024]{1,0:T(8,128)(2,1)S(1)}, bf16[128,1024]{1,0:T(8,128)(2,1)}, u32[]{:S(2)}, u32[]{:S(2)}) collective-permute-start(bf16[128,1024]{1,0:T(8,128)(2,1)S(1)} %get-tuple-element.33), channel_id=1, source_target_pairs={{0,48},{16,0},{32,16},{48,32},{1,49},{17,1},{33,17},{49,33},{2,50}... | collective-permute-start | bytes 786440 | tf_op jit(solution)/shard_map/ppermute | solution.py:302
  20.0 6.7 %all-to-all-start = ((bf16[8,3,128,256]{3,2,1,0:T(8,128)(2,1)}), bf16[8,3,128,256]{3,2,1,0:T(8,128)(2,1)S(1)}, u32[]{:S(2)}, u32[]{:S(2)}) async-start(bf16[8,3,128,256]{3,2,1,0:T(8,128)(2,1)} %pack_qkv.1), calls=%async_computation | async-start | bytes 3145728 | tf_op jit(solution)/shard_map/all_to_all | solution.py:310
  26.7 0.5 collective-permute-start.6
  27.2 1.0 constant_dynamic-update-slice_fusion.2
  28.1 1.0 constant_dynamic-update-slice_fusion.1
  29.1 1.0 constant_dynamic-update-slice_fusion.g_ref.refs_4_
  30.1 1.3 maximum_bitcast_fusion
  31.5 1.8 %pad_maximum_fusion.w_ref.refs_4_ = bf16[4,2048,256]{2,1,0:T(8,128)(2,1)S(1)} fusion(bf16[1,2048,256]{2,1,0:T(8,128)(2,1)S(1)} %maximum_bitcast_fusion.1, bf16[1,2048,256]{2,1,0:T(8,128)(2,1)S(1)} %maximum_bitcast_fusion, bf16[1,2048,256]{2,1,0:T(8,128)(2,1)} %bitcast.5, bf16[1,2048,256]{2,1,0:T(8,128)(2,1)} %bitcast.4), kind=kLoop, calls=%fused_computation | loop fusion | flops 6291456 | bytes 8388608 | tf_op jit(solution)/shard_map/stack | solution.py:338
  33.3 5.6 %grad_attended.1 = (bf16[8,128,256]{2,1,0:T(8,128)(2,1)S(1)}, bf16[8,128,256]{2,1,0:T(8,128)(2,1)}, bf16[8,128,256]{2,1,0:T(8,128)(2,1)}, bf16[8,128,256]{2,1,0:T(8,128)(2,1)}) custom-call(bf16[512,1024]{1,0:T(8,128)(2,1)S(1)} %constant_dynamic-update-slice_fusion.g_ref.refs_4_, bf16[4,2048,256]{2,1,0:T(8,128)(2,1)S(1)} %pad_maximum_fusion.w_ref.refs_4_), custom_call_target="tpu_custom_call" | custom-call | flops 2147483648 | bytes 6291456 | tf_op jit(solution)/shard_map/grad_attended/pallas_call | solution.py:211
  38.9 0.8 copy-done.10
  39.7 0.8 collective-permute-start.8
  40.5 0.7 collective-permute-start.9
  41.3 0.9 collective-permute-start.10
  42.1 6.3 %all-to-all-done.q_ref.k_ref.v_ref = bf16[8,3,128,256]{3,2,1,0:T(8,128)(2,1)S(1)} async-done(((bf16[8,3,128,256]{3,2,1,0:T(8,128)(2,1)}), bf16[8,3,128,256]{3,2,1,0:T(8,128)(2,1)S(1)}, u32[]{:S(2)}, u32[]{:S(2)}) %all-to-all-start) | async-done | bytes 1572896 | tf_op jit(solution)/shard_map/all_to_all | solution.py:310
  48.4 3.5 %attend.1 = (bf16[8,128,256]{2,1,0:T(8,128)(2,1)S(1)}, f32[2,1,1024]{2,1,0:T(1,128)S(1)}) custom-call(bf16[8,3,128,256]{3,2,1,0:T(8,128)(2,1)S(1)} %all-to-all-done.q_ref.k_ref.v_ref, bf16[8,3,128,256]{3,2,1,0:T(8,128)(2,1)S(1)} %all-to-all-done.q_ref.k_ref.v_ref, bf16[8,3,128,256]{3,2,1,0:T(8,128)(2,1)S(1)} %all-to-all-done.q_ref.k_ref.v_ref), custom_call_target="tpu_custom_call" | custom-call | flops 1073741824 | bytes 2097152 | tf_op jit(solution)/shard_map/attend/pallas_call | solution.py:127
  52.0 0.8 copy-done.12
  52.7 3.5 %all-to-all-start.1 = ((bf16[8,128,256]{2,1,0:T(8,128)(2,1)}), bf16[8,128,256]{2,1,0:T(8,128)(2,1)S(1)}, u32[]{:S(2)}, u32[]{:S(2)}) async-start(bf16[8,128,256]{2,1,0:T(8,128)(2,1)} %copy-done.12), calls=%async_computation.1 | async-start | bytes 1048576 | tf_op jit(solution)/shard_map/all_to_all | solution.py:310
  56.3 1.0 collective-permute-done.9
  57.2 10.0 %collective-permute-done.10 = bf16[8,128,256]{2,1,0:T(8,128)(2,1)} collective-permute-done((bf16[8,128,256]{2,1,0:T(8,128)(2,1)}, bf16[8,128,256]{2,1,0:T(8,128)(2,1)}, u32[]{:S(2)}, u32[]{:S(2)}) %collective-permute-start.10) | collective-permute-done | bytes 524320 | tf_op jit(solution)/shard_map/ppermute | solution.py:302
  67.3 0.9 collective-permute-start.13
  68.2 0.9 collective-permute-start.12
  69.1 0.9 collective-permute-start.11
  70.0 1.8 %add_convert_fusion = bf16[8,128,256]{2,1,0:T(8,128)(2,1)S(1)} fusion(bf16[8,128,256]{2,1,0:T(8,128)(2,1)} %collective-permute-done.10, bf16[8,128,256]{2,1,0:T(8,128)(2,1)} %collective-permute-done.9, bf16[8,128,256]{2,1,0:T(8,128)(2,1)} %collective-permute-done.8, bf16[8,128,256]{2,1,0:T(8,128)(2,1)} %copy-done.10), kind=kLoop, calls=%fused_computation.4 | loop fusion | flops 2097152 | bytes 2621440 | tf_op jit(solution)/shard_map/convert_element_type | solution.py:345
  71.7 17.6 %all_to_all.20.g_ref = bf16[8,128,256]{2,1,0:T(8,128)(2,1)} all-to-all(bf16[8,128,256]{2,1,0:T(8,128)(2,1)S(1)} %add_convert_fusion), channel_id=1, replica_groups=mesh['yl'=2,'x'=4,'core'=2,'z'=4,'yh'=2] {'z','yh'}, dimensions={0} | all-to-all | bytes 1048576 | tf_op jit(solution)/shard_map/all_to_all | solution.py:310
  89.4 4.5 %collective-permute-done.11.refs_1_ = bf16[8,128,256]{2,1,0:T(8,128)(2,1)S(1)} collective-permute-done((bf16[8,128,256]{2,1,0:T(8,128)(2,1)S(1)}, bf16[8,128,256]{2,1,0:T(8,128)(2,1)S(1)}, u32[]{:S(2)}, u32[]{:S(2)}) %collective-permute-start.11) | collective-permute-done | bytes 524320 | tf_op jit(solution)/shard_map/ppermute | solution.py:302
  93.9 1.7 %weight_parts.2 = bf16[2,8,256,256]{3,2,1,0:T(8,128)(2,1)S(1)} custom-call(bf16[8,128,256]{2,1,0:T(8,128)(2,1)S(1)} %all-to-all-done.1.refs_0_, bf16[8,128,256]{2,1,0:T(8,128)(2,1)S(1)} %collective-permute-done.11.refs_1_, bf16[8,128,256]{2,1,0:T(8,128)(2,1)S(1)} %collective-permute-done.12.refs_2_, ...), custom_call_target="tpu_custom_call" | custom-call | flops 1073741824 | bytes 5242880 | tf_op jit(solution)/shard_map/weight_parts/pallas_call | solution.py:254
  95.7 4.1 %collective-permute-done.17.refs_5_ = bf16[2,8,256,256]{3,2,1,0:T(8,128)(2,1)S(1)} collective-permute-done((bf16[2,8,256,256]{3,2,1,0:T(8,128)(2,1)S(1)}, bf16[2,8,256,256]{3,2,1,0:T(8,128)(2,1)S(1)}, u32[]{:S(2)}, u32[]{:S(2)}) %collective-permute-start.17) | collective-permute-done | bytes 2097184 | tf_op jit(solution)/shard_map/ppermute | solution.py:306
  99.8 1.9 %weight_parts.3 = bf16[2,8,256,256]{3,2,1,0:T(8,128)(2,1)S(1)} custom-call(bf16[8,128,256]{2,1,0:T(8,128)(2,1)S(1)} %all-to-all-done.1.refs_0_, bf16[8,128,256]{2,1,0:T(8,128)(2,1)S(1)} %collective-permute-done.11.refs_1_, bf16[8,128,256]{2,1,0:T(8,128)(2,1)S(1)} %collective-permute-done.12.refs_2_, ...), custom_call_target="tpu_custom_call" | custom-call | flops 1073741824 | bytes 5242880 | tf_op jit(solution)/shard_map/weight_parts/pallas_call | solution.py:254
  101.7 1.4 copy-done
  103.1 8.4 %all-to-all-start.3 = ((bf16[16,256,256]{2,1,0:T(8,128)(2,1)}), bf16[16,256,256]{2,1,0:T(8,128)(2,1)}, u32[]{:S(2)}, u32[]{:S(2)}) async-start(bf16[16,256,256]{2,1,0:T(8,128)(2,1)} %bitcast.15), calls=%async_computation.3 | async-start | bytes 4194304 | tf_op jit(solution)/shard_map/all_to_all | solution.py:310
  111.5 1.0 copy-done.11
  112.5 8.3 %attend_back.1 = (bf16[1024,256]{1,0:T(8,128)(2,1)}, bf16[1024,256]{1,0:T(8,128)(2,1)}, bf16[1024,256]{1,0:T(8,128)(2,1)}) custom-call(bf16[8,3,128,256]{3,2,1,0:T(8,128)(2,1)S(1)} %all-to-all-done.q_ref.k_ref.v_ref, bf16[8,3,128,256]{3,2,1,0:T(8,128)(2,1)S(1)} %all-to-all-done.q_ref.k_ref.v_ref, ...), custom_call_target="tpu_custom_call" | custom-call | flops 5368709120 | bytes 3670016 | tf_op jit(solution)/shard_map/attend_back/pallas_call | solution.py:179
  120.9 3.2 %project.1 = (bf16[128,1024]{1,0:T(8,128)(2,1)S(1)}, bf16[128,1024]{1,0:T(8,128)(2,1)S(1)}, bf16[128,1024]{1,0:T(8,128)(2,1)S(1)}, bf16[128,1024]{1,0:T(8,128)(2,1)S(1)}) custom-call(bf16[8,128,256]{2,1,0:T(8,128)(2,1)S(1)} %all-to-all-done.1.refs_0_, bf16[8,128,256]{2,1,0:T(8,128)(2,1)S(1)} %copy-done.8, bf16[8,128,256]{2,1,0:T(8,128)(2,1)S(1)} %copy-done.6, ...), custom_call_target="tpu_custom_call" | custom-call | flops 2147483648 | bytes 7340032 | tf_op jit(solution)/shard_map/project/pallas_call | solution.py:287
  124.1 1.3 collective-permute-start.14
  125.5 0.8 collective-permute-start.16
  126.3 7.1 %collective-permute-done.14.refs_1_ = bf16[128,1024]{1,0:T(8,128)(2,1)S(1)} collective-permute-done((bf16[128,1024]{1,0:T(8,128)(2,1)S(1)}, bf16[128,1024]{1,0:T(8,128)(2,1)S(1)}, u32[]{:S(2)}, u32[]{:S(2)}) %collective-permute-start.14) | collective-permute-done | bytes 262176 | tf_op jit(solution)/shard_map/ppermute | solution.py:302
  133.4 2.7 %collective-permute-done.15.refs_2_ = bf16[128,1024]{1,0:T(8,128)(2,1)S(1)} collective-permute-done((bf16[128,1024]{1,0:T(8,128)(2,1)S(1)}, bf16[128,1024]{1,0:T(8,128)(2,1)S(1)}, u32[]{:S(2)}, u32[]{:S(2)}) %collective-permute-start.15) | collective-permute-done | bytes 262176 | tf_op jit(solution)/shard_map/ppermute | solution.py:302
  136.1 4.1 %collective-permute-done.16.refs_3_ = bf16[128,1024]{1,0:T(8,128)(2,1)S(1)} collective-permute-done((bf16[128,1024]{1,0:T(8,128)(2,1)S(1)}, bf16[128,1024]{1,0:T(8,128)(2,1)S(1)}, u32[]{:S(2)}, u32[]{:S(2)}) %collective-permute-start.16) | collective-permute-done | bytes 262176 | tf_op jit(solution)/shard_map/ppermute | solution.py:302
  140.2 1.1 place_projected.1
  141.3 3.9 %all-to-all-done.3 = bf16[16,256,256]{2,1,0:T(8,128)(2,1)} async-done(((bf16[16,256,256]{2,1,0:T(8,128)(2,1)}), bf16[16,256,256]{2,1,0:T(8,128)(2,1)}, u32[]{:S(2)}, u32[]{:S(2)}) %all-to-all-start.3) | async-done | bytes 2097184 | tf_op jit(solution)/shard_map/all_to_all | solution.py:310
  145.2 2.6 %convert_reduce_fusion = f32[256,256]{1,0:T(8,128)} fusion(bf16[16,256,256]{2,1,0:T(8,128)(2,1)} %all-to-all-done.3), kind=kLoop, calls=%fused_computation.1 | loop fusion | flops 2031616 | bytes 2359296 | tf_op jit(solution)/shard_map/reduce_sum | solution.py:351
  (48 shorter events, 0.6 us)
Async XLA Ops:
  0.6 4.7 %copy-start.15 = (bf16[1,128,2048]{2,1,0:T(8,128)(2,1)S(1)}, bf16[1,128,2048]{2,1,0:T(8,128)(2,1)}, u32[]{:S(2)}) copy-start(bf16[1,128,2048]{2,1,0:T(8,128)(2,1)} %param.7) | copy-start | bytes 1572868
  0.6 4.7 %copy-start.14 = (bf16[1,128,2048]{2,1,0:T(8,128)(2,1)S(1)}, bf16[1,128,2048]{2,1,0:T(8,128)(2,1)}, u32[]{:S(2)}) copy-start(bf16[1,128,2048]{2,1,0:T(8,128)(2,1)} %param.6) | copy-start | bytes 1572868
  0.7 4.7 %copy-start.13 = (bf16[1,128,2048]{2,1,0:T(8,128)(2,1)S(1)}, bf16[1,128,2048]{2,1,0:T(8,128)(2,1)}, u32[]{:S(2)}) copy-start(bf16[1,128,2048]{2,1,0:T(8,128)(2,1)} %param.5) | copy-start | bytes 1572868
  2.0 4.6 %copy-start.9 = (bf16[1,128,4096]{2,1,0:T(8,128)(2,1)S(1)}, bf16[1,128,4096]{2,1,0:T(8,128)(2,1)}, u32[]{:S(2)}) copy-start(bf16[1,128,4096]{2,1,0:T(8,128)(2,1)} %param.9) | copy-start | bytes 3145732
  2.1 15.1 %collective-permute-start.1 = (bf16[1024,256]{1,0:T(8,128)(2,1)S(1)}, bf16[1024,256]{1,0:T(8,128)(2,1)S(1)}, u32[]{:S(2)}, u32[]{:S(2)}) collective-permute-start(bf16[1024,256]{1,0:T(8,128)(2,1)S(1)} %get-tuple-element.51), channel_id=1, source_target_pairs={{0,65},{1,64},{64,1},{65,0},{2,67},{3,66},{66,3},{67,2},{4,69},{5,... | collective-permute-start | bytes 1572872 | tf_op jit(solution)/shard_map/ppermute | solution.py:329
  5.2 14.7 %collective-permute-start = (bf16[1024,256]{1,0:T(8,128)(2,1)S(1)}, bf16[1024,256]{1,0:T(8,128)(2,1)}, u32[]{:S(2)}, u32[]{:S(2)}) collective-permute-start(bf16[1024,256]{1,0:T(8,128)(2,1)S(1)} %get-tuple-element.52), channel_id=1, source_target_pairs={{0,64},{64,0},{1,65},{65,1},{2,66},{66,2},{3,67},{67,3},{4,68},{68... | collective-permute-start | bytes 1572872 | tf_op jit(solution)/shard_map/ppermute | solution.py:306
  6.8 19.8 %collective-permute-start.2 = (bf16[128,1024]{1,0:T(8,128)(2,1)S(1)}, bf16[128,1024]{1,0:T(8,128)(2,1)}, u32[]{:S(2)}, u32[]{:S(2)}) collective-permute-start(bf16[128,1024]{1,0:T(8,128)(2,1)S(1)} %get-tuple-element.31), channel_id=1, source_target_pairs={{0,16},{16,32},{32,48},{48,0},{1,17},{17,33},{33,49},{49,1},{2,18}... | collective-permute-start | bytes 786440 | tf_op jit(solution)/shard_map/ppermute | solution.py:302
  8.4 23.1 %collective-permute-start.5 = (bf16[2048,256]{1,0:T(8,128)(2,1)}, bf16[2048,256]{1,0:T(8,128)(2,1)}, u32[]{:S(2)}, u32[]{:S(2)}) collective-permute-start(bf16[2048,256]{1,0:T(8,128)(2,1)} %param.8), channel_id=1, source_target_pairs={{0,8},{8,0},{1,9},{9,1},{2,10},{10,2},{3,11},{11,3},{4,12},{12,4},... | collective-permute-start | bytes 3145736 | tf_op jit(solution)/shard_map/ppermute | solution.py:306
  8.4 19.7 %collective-permute-start.3 = (bf16[128,1024]{1,0:T(8,128)(2,1)S(1)}, bf16[128,1024]{1,0:T(8,128)(2,1)}, u32[]{:S(2)}, u32[]{:S(2)}) collective-permute-start(bf16[128,1024]{1,0:T(8,128)(2,1)S(1)} %get-tuple-element.32), channel_id=1, source_target_pairs={{0,32},{16,48},{32,0},{48,16},{1,33},{17,49},{33,1},{49,17},{2,34}... | collective-permute-start | bytes 786440 | tf_op jit(solution)/shard_map/ppermute | solution.py:302
  17.2 2.8 %copy-start.16 = (bf16[1024,256]{1,0:T(8,128)(2,1)}, bf16[1024,256]{1,0:T(8,128)(2,1)S(1)}, u32[]{:S(2)}) copy-start(bf16[1024,256]{1,0:T(8,128)(2,1)S(1)} %collective-permute-done.1) | copy-start | bytes 1572868
  17.2 12.0 %collective-permute-start.4 = (bf16[128,1024]{1,0:T(8,128)(2,1)S(1)}, bf16[128,1024]{1,0:T(8,128)(2,1)}, u32[]{:S(2)}, u32[]{:S(2)}) collective-permute-start(bf16[128,1024]{1,0:T(8,128)(2,1)S(1)} %get-tuple-element.33), channel_id=1, source_target_pairs={{0,48},{16,0},{32,16},{48,32},{1,49},{17,1},{33,17},{49,33},{2,50}... | collective-permute-start | bytes 786440 | tf_op jit(solution)/shard_map/ppermute | solution.py:302
  20.0 28.5 %all-to-all-start = ((bf16[8,3,128,256]{3,2,1,0:T(8,128)(2,1)}), bf16[8,3,128,256]{3,2,1,0:T(8,128)(2,1)S(1)}, u32[]{:S(2)}, u32[]{:S(2)}) async-start(bf16[8,3,128,256]{3,2,1,0:T(8,128)(2,1)} %pack_qkv.1), calls=%async_computation | async-start | bytes 3145728 | tf_op jit(solution)/shard_map/all_to_all | solution.py:310
  26.6 4.7 %collective-permute-start.7 = (bf16[1024,256]{1,0:T(8,128)(2,1)}, bf16[1024,256]{1,0:T(8,128)(2,1)S(1)}, u32[]{:S(2)}, u32[]{:S(2)}) collective-permute-start(bf16[1024,256]{1,0:T(8,128)(2,1)} %copy-done.16), channel_id=1, source_target_pairs={{0,8},{8,0},{1,9},{9,1},{2,10},{10,2},{3,11},{11,3},{4,12},{12,4},... | collective-permute-start | bytes 1572872 | tf_op jit(solution)/shard_map/ppermute | solution.py:306
  26.7 4.7 %collective-permute-start.6 = (bf16[1024,256]{1,0:T(8,128)(2,1)}, bf16[1024,256]{1,0:T(8,128)(2,1)S(1)}, u32[]{:S(2)}, u32[]{:S(2)}) collective-permute-start(bf16[1024,256]{1,0:T(8,128)(2,1)} %collective-permute-done), channel_id=1, source_target_pairs={{0,8},{8,0},{1,9},{9,1},{2,10},{10,2},{3,11},{11,3},{4,12},{12,4},... | collective-permute-start | bytes 1572872 | tf_op jit(solution)/shard_map/ppermute | solution.py:306
  33.3 5.6 %copy-start.1 = (bf16[4,2048,256]{2,1,0:T(8,128)(2,1)}, bf16[4,2048,256]{2,1,0:T(8,128)(2,1)S(1)}, u32[]{:S(2)}) copy-start(bf16[4,2048,256]{2,1,0:T(8,128)(2,1)S(1)} %pad_maximum_fusion.w_ref.refs_4_) | copy-start | bytes 12582916
  38.9 0.8 copy-start.10
  39.7 16.5 %collective-permute-start.8 = (bf16[8,128,256]{2,1,0:T(8,128)(2,1)}, bf16[8,128,256]{2,1,0:T(8,128)(2,1)}, u32[]{:S(2)}, u32[]{:S(2)}) collective-permute-start(bf16[8,128,256]{2,1,0:T(8,128)(2,1)} %get-tuple-element.35), channel_id=1, source_target_pairs={{0,48},{16,0},{32,16},{48,32},{1,49},{17,1},{33,17},{49,33},{2,50}... | collective-permute-start | bytes 1572872 | tf_op jit(solution)/shard_map/ppermute | solution.py:302
  40.5 16.7 %collective-permute-start.9 = (bf16[8,128,256]{2,1,0:T(8,128)(2,1)}, bf16[8,128,256]{2,1,0:T(8,128)(2,1)}, u32[]{:S(2)}, u32[]{:S(2)}) collective-permute-start(bf16[8,128,256]{2,1,0:T(8,128)(2,1)} %get-tuple-element.36), channel_id=1, source_target_pairs={{0,32},{16,48},{32,0},{48,16},{1,33},{17,49},{33,1},{49,17},{2,34}... | collective-permute-start | bytes 1572872 | tf_op jit(solution)/shard_map/ppermute | solution.py:302
  41.3 26.0 %collective-permute-start.10 = (bf16[8,128,256]{2,1,0:T(8,128)(2,1)}, bf16[8,128,256]{2,1,0:T(8,128)(2,1)}, u32[]{:S(2)}, u32[]{:S(2)}) collective-permute-start(bf16[8,128,256]{2,1,0:T(8,128)(2,1)} %get-tuple-element.37), channel_id=1, source_target_pairs={{0,16},{16,32},{32,48},{48,0},{1,17},{17,33},{33,49},{49,1},{2,18}... | collective-permute-start | bytes 1572872 | tf_op jit(solution)/shard_map/ppermute | solution.py:302
  52.0 0.8 copy-start.12
  52.7 14.5 %all-to-all-start.1 = ((bf16[8,128,256]{2,1,0:T(8,128)(2,1)}), bf16[8,128,256]{2,1,0:T(8,128)(2,1)S(1)}, u32[]{:S(2)}, u32[]{:S(2)}) async-start(bf16[8,128,256]{2,1,0:T(8,128)(2,1)} %copy-done.12), calls=%async_computation.1 | async-start | bytes 1048576 | tf_op jit(solution)/shard_map/all_to_all | solution.py:310
  67.3 22.1 %collective-permute-start.13 = (bf16[8,128,256]{2,1,0:T(8,128)(2,1)S(1)}, bf16[8,128,256]{2,1,0:T(8,128)(2,1)S(1)}, u32[]{:S(2)}, u32[]{:S(2)}) collective-permute-start(bf16[8,128,256]{2,1,0:T(8,128)(2,1)S(1)} %all-to-all-done.1.refs_0_), channel_id=1, source_target_pairs={{0,48},{16,0},{32,16},{48,32},{1,49},{17,1},{33,17},{49,33},{2,50}... | collective-permute-start | bytes 1572872 | tf_op jit(solution)/shard_map/ppermute | solution.py:302
  68.2 21.2 %collective-permute-start.12 = (bf16[8,128,256]{2,1,0:T(8,128)(2,1)S(1)}, bf16[8,128,256]{2,1,0:T(8,128)(2,1)S(1)}, u32[]{:S(2)}, u32[]{:S(2)}) collective-permute-start(bf16[8,128,256]{2,1,0:T(8,128)(2,1)S(1)} %all-to-all-done.1.refs_0_), channel_id=1, source_target_pairs={{0,32},{16,48},{32,0},{48,16},{1,33},{17,49},{33,1},{49,17},{2,34}... | collective-permute-start | bytes 1572872 | tf_op jit(solution)/shard_map/ppermute | solution.py:302
  69.1 24.8 %collective-permute-start.11 = (bf16[8,128,256]{2,1,0:T(8,128)(2,1)S(1)}, bf16[8,128,256]{2,1,0:T(8,128)(2,1)S(1)}, u32[]{:S(2)}, u32[]{:S(2)}) collective-permute-start(bf16[8,128,256]{2,1,0:T(8,128)(2,1)S(1)} %all-to-all-done.1.refs_0_), channel_id=1, source_target_pairs={{0,16},{16,32},{32,48},{48,0},{1,17},{17,33},{33,49},{49,1},{2,18}... | collective-permute-start | bytes 1572872 | tf_op jit(solution)/shard_map/ppermute | solution.py:302
  89.4 10.4 %copy-start.3 = (bf16[8,128,256]{2,1,0:T(8,128)(2,1)}, bf16[8,128,256]{2,1,0:T(8,128)(2,1)S(1)}, u32[]{:S(2)}) copy-start(bf16[8,128,256]{2,1,0:T(8,128)(2,1)S(1)} %collective-permute-done.13.refs_3_) | copy-start | bytes 1572868
  89.4 10.4 %copy-start.5 = (bf16[8,128,256]{2,1,0:T(8,128)(2,1)}, bf16[8,128,256]{2,1,0:T(8,128)(2,1)S(1)}, u32[]{:S(2)}) copy-start(bf16[8,128,256]{2,1,0:T(8,128)(2,1)S(1)} %collective-permute-done.12.refs_2_) | copy-start | bytes 1572868
  93.8 6.0 %copy-start.7 = (bf16[8,128,256]{2,1,0:T(8,128)(2,1)}, bf16[8,128,256]{2,1,0:T(8,128)(2,1)S(1)}, u32[]{:S(2)}) copy-start(bf16[8,128,256]{2,1,0:T(8,128)(2,1)S(1)} %collective-permute-done.11.refs_1_) | copy-start | bytes 1572868
  95.6 4.2 %collective-permute-start.17 = (bf16[2,8,256,256]{3,2,1,0:T(8,128)(2,1)S(1)}, bf16[2,8,256,256]{3,2,1,0:T(8,128)(2,1)S(1)}, u32[]{:S(2)}, u32[]{:S(2)}) collective-permute-start(bf16[2,8,256,256]{3,2,1,0:T(8,128)(2,1)S(1)} %weight_parts.2), channel_id=1, source_target_pairs={{0,8},{8,0},{1,9},{9,1},{2,10},{10,2},{3,11},{11,3},{4,12},{12,4},... | collective-permute-start | bytes 6291464 | tf_op jit(solution)/shard_map/ppermute | solution.py:306
  101.7 1.4 copy-start
  103.1 42.1 %all-to-all-start.3 = ((bf16[16,256,256]{2,1,0:T(8,128)(2,1)}), bf16[16,256,256]{2,1,0:T(8,128)(2,1)}, u32[]{:S(2)}, u32[]{:S(2)}) async-start(bf16[16,256,256]{2,1,0:T(8,128)(2,1)} %bitcast.15), calls=%async_computation.3 | async-start | bytes 4194304 | tf_op jit(solution)/shard_map/all_to_all | solution.py:310
  111.5 1.0 copy-start.11
  112.5 8.3 %copy-start.2 = (bf16[4,2048,256]{2,1,0:T(8,128)(2,1)S(1)}, bf16[4,2048,256]{2,1,0:T(8,128)(2,1)}, u32[]{:S(2)}) copy-start(bf16[4,2048,256]{2,1,0:T(8,128)(2,1)} %copy-done.1) | copy-start | bytes 12582916
  112.5 8.3 %copy-start.4 = (bf16[8,128,256]{2,1,0:T(8,128)(2,1)S(1)}, bf16[8,128,256]{2,1,0:T(8,128)(2,1)}, u32[]{:S(2)}) copy-start(bf16[8,128,256]{2,1,0:T(8,128)(2,1)} %copy-done.3) | copy-start | bytes 1572868
  112.5 8.3 %copy-start.6 = (bf16[8,128,256]{2,1,0:T(8,128)(2,1)S(1)}, bf16[8,128,256]{2,1,0:T(8,128)(2,1)}, u32[]{:S(2)}) copy-start(bf16[8,128,256]{2,1,0:T(8,128)(2,1)} %copy-done.5) | copy-start | bytes 1572868
  112.5 8.3 %copy-start.8 = (bf16[8,128,256]{2,1,0:T(8,128)(2,1)S(1)}, bf16[8,128,256]{2,1,0:T(8,128)(2,1)}, u32[]{:S(2)}) copy-start(bf16[8,128,256]{2,1,0:T(8,128)(2,1)} %copy-done.7) | copy-start | bytes 1572868
  124.1 9.3 %collective-permute-start.14 = (bf16[128,1024]{1,0:T(8,128)(2,1)S(1)}, bf16[128,1024]{1,0:T(8,128)(2,1)S(1)}, u32[]{:S(2)}, u32[]{:S(2)}) collective-permute-start(bf16[128,1024]{1,0:T(8,128)(2,1)S(1)} %get-tuple-element.45), channel_id=1, source_target_pairs={{0,48},{16,0},{32,16},{48,32},{1,49},{17,1},{33,17},{49,33},{2,50}... | collective-permute-start | bytes 786440 | tf_op jit(solution)/shard_map/ppermute | solution.py:302
  125.4 10.7 %collective-permute-start.15 = (bf16[128,1024]{1,0:T(8,128)(2,1)S(1)}, bf16[128,1024]{1,0:T(8,128)(2,1)S(1)}, u32[]{:S(2)}, u32[]{:S(2)}) collective-permute-start(bf16[128,1024]{1,0:T(8,128)(2,1)S(1)} %get-tuple-element.46), channel_id=1, source_target_pairs={{0,32},{16,48},{32,0},{48,16},{1,33},{17,49},{33,1},{49,17},{2,34}... | collective-permute-start | bytes 786440 | tf_op jit(solution)/shard_map/ppermute | solution.py:302
  125.5 14.8 %collective-permute-start.16 = (bf16[128,1024]{1,0:T(8,128)(2,1)S(1)}, bf16[128,1024]{1,0:T(8,128)(2,1)S(1)}, u32[]{:S(2)}, u32[]{:S(2)}) collective-permute-start(bf16[128,1024]{1,0:T(8,128)(2,1)S(1)} %get-tuple-element.47), channel_id=1, source_target_pairs={{0,16},{16,32},{32,48},{48,0},{1,17},{17,33},{33,49},{49,1},{2,18}... | collective-permute-start | bytes 786440 | tf_op jit(solution)/shard_map/ppermute | solution.py:302

commit v3 on v2

--- a/solution.py
+++ b/solution.py
@@ -55,7 +55,7 @@
     return pl.pallas_call(
         body,
         out_shape=jax.ShapeDtypeStruct((groups, 3, tok, BLOCK), query.dtype),
-        compiler_params=params(16),
+        compiler_params=params(8),
         cost_estimate=cost(0, 3 * 2 * 2 * tok * feat),
         name="pack_qkv",
     )(query, key, value)
@@ -75,7 +75,7 @@
     return pl.pallas_call(
         body,
         out_shape=[jax.ShapeDtypeStruct((tok, 4 * BLOCK), grad.dtype)] * X,
-        compiler_params=params(16),
+        compiler_params=params(6),
         cost_estimate=cost(0, 4 * tok * cols),
         name="pack_grad",
     )(grad)
@@ -96,7 +96,7 @@
     return pl.pallas_call(
         body,
         out_shape=jax.ShapeDtypeStruct((tok, cols), parts[0].dtype),
-        compiler_params=params(16),
+        compiler_params=params(6),
         cost_estimate=cost(0, 4 * tok * cols),
         name="place_projected",
     )(*parts)
@@ -139,7 +139,7 @@
             pl.BlockSpec((groups, tok, width), lambda n: (0, 0, 0)),
             pl.BlockSpec((heads, 1, length), lambda n: (0, 0, 0)),
         ],
-        compiler_params=params(32),
+        compiler_params=params(14),
         cost_estimate=cost(4 * heads * length * length * HEAD, 8 * length * width, heads * length * length),
         name="attend",
     )(qkv, qkv, qkv)
@@ -187,7 +187,7 @@
         ],
         out_specs=[pl.BlockSpec((length, HEAD), lambda h: (0, h))] * 3,
         scratch_shapes=[pltpu.VMEM((length, HEAD), jnp.float32)] * 2,
-        compiler_params=params(40),
+        compiler_params=params(22),
         cost_estimate=cost(20 * heads * length * length * HEAD, 14 * length * width, heads * length * length),
         name="attend_back",
     )(qkv, qkv, qkv, lse, grad)
@@ -217,7 +217,7 @@
             pl.BlockSpec((4, BLOCK, block), lambda n: (0, n, 0)),
         ],
         out_specs=[pl.BlockSpec((pl.squeezed, tok, BLOCK), lambda n: (n, 0, 0))] * X,
-        compiler_params=params(32),
+        compiler_params=params(12),
         cost_estimate=cost(2 * rows * width * feat, 2 * feat * width + 4 * rows * width),
         name="grad_attended",
     )(grads, weights)
@@ -260,7 +260,7 @@
         + [pl.BlockSpec((2, step, block, block), lambda n: (0, n, 0, 0))] * len(extra),
         out_specs=pl.BlockSpec((2, step, block, block), lambda n: (0, n, 0, 0)),
         scratch_shapes=[pltpu.VMEM((rows, 2 * block), jnp.bfloat16)],
-        compiler_params=params(32),
+        compiler_params=params(18),
         cost_estimate=cost(4 * rows * groups * block * block, 5 * MIB),
         name="weight_parts",
     )(*attended, grads, *extra)
@@ -292,7 +292,7 @@
         + [pl.BlockSpec((pl.squeezed, feat, block), lambda j: (j, 0, 0))],
         out_specs=[pl.BlockSpec((tok, block), lambda j: (0, j))] * X,
         scratch_shapes=[pltpu.VMEM((rows, feat), jnp.bfloat16)],
-        compiler_params=params(24),
+        compiler_params=params(16),
         cost_estimate=cost(8 * rows * feat * block, 7 * MIB),
         name="project",
     )(*attended, weights)

time: 148 us -> 148 us (level)
  no operation moved by 1% of the time
where the time goes in v3:
time: 148 us
  waiting for transfers between devices  49.6 us (34%)
  starting transfers between devices  37 us (25%)
  Pallas kernels  26.7 us (18%)
  blocking collectives  17.6 us (12%)
  local copies, waits for them, and re-layouts  8.42 us (6%)
  other arithmetic  7.53 us (5%)
    ppermute x12, waiting for transfers between devices, shift_x(): return lax.ppermute(array, 'x', [(i, (i + shift) % X) for i in range(X)])  29.3 us
    all_to_all x3, starting transfers between devices, exchange(): return lax.all_to_all(array, axes, 0, 0, tiled=False)  18.5 us
    all_to_all x1, blocking collectives, exchange(): return lax.all_to_all(array, axes, 0, 0, tiled=False)  17.6 us
    ppermute x12, starting transfers between devices, shift_x(): return lax.ppermute(array, 'x', [(i, (i + shift) % X) for i in range(X)])  14.5 us
    all_to_all x3, waiting for transfers between devices, exchange(): return lax.all_to_all(array, axes, 0, 0, tiled=False)  10.1 us
    pallas_call x1, Pallas kernels, attend_back(): pl.pallas_call(body, grid=(heads,), out_shape=[out] * 3, in_specs=[head_s...  8.31 us
    unnamed x37, local copies, waits for them, and re-layouts  6.07 us
    ppermute x1, waiting for transfers between devices, shards(): lax.ppermute(out_weight[half:], ('yl', 'yh'), [(i, 3 - i) for i in range(...  6.04 us
  transfers between devices with their start and end apart: 21, of which 10 were waited for; matrix products, arithmetic and copies ran while one was open for 5% of the time, Pallas kernels for 16%

profile of v3, /device:TPU:0, one launch (start us, length us, event | category | flops | bytes accessed | tf_op | source)
XLA Modules:
  0.0 147.8 jit_solution(11170600787167665794)
XLA Ops:
  0.7 1.4 fusion
  2.1 3.2 %collective-permute-start.1 = (bf16[1024,256]{1,0:T(8,128)(2,1)S(1)}, bf16[1024,256]{1,0:T(8,128)(2,1)S(1)}, u32[]{:S(2)}, u32[]{:S(2)}) collective-permute-start(bf16[1024,256]{1,0:T(8,128)(2,1)S(1)} %get-tuple-element.51), channel_id=1, source_target_pairs={{0,65},{1,64},{64,1},{65,0},{2,67},{3,66},{66,3},{67,2},{4,69},{5,... | collective-permute-start | bytes 1572872 | tf_op jit(solution)/shard_map/ppermute | solution.py:329
  5.4 1.3 pack_qkv.1
  6.8 1.6 %collective-permute-start.2 = (bf16[128,1024]{1,0:T(8,128)(2,1)S(1)}, bf16[128,1024]{1,0:T(8,128)(2,1)}, u32[]{:S(2)}, u32[]{:S(2)}) collective-permute-start(bf16[128,1024]{1,0:T(8,128)(2,1)S(1)} %get-tuple-element.31), channel_id=1, source_target_pairs={{0,16},{16,32},{32,48},{48,0},{1,17},{17,33},{33,49},{49,1},{2,18}... | collective-permute-start | bytes 786440 | tf_op jit(solution)/shard_map/ppermute | solution.py:302
  8.4 2.7 %collective-permute-start.3 = (bf16[128,1024]{1,0:T(8,128)(2,1)S(1)}, bf16[128,1024]{1,0:T(8,128)(2,1)}, u32[]{:S(2)}, u32[]{:S(2)}) collective-permute-start(bf16[128,1024]{1,0:T(8,128)(2,1)S(1)} %get-tuple-element.32), channel_id=1, source_target_pairs={{0,32},{16,48},{32,0},{48,16},{1,33},{17,49},{33,1},{49,17},{2,34}... | collective-permute-start | bytes 786440 | tf_op jit(solution)/shard_map/ppermute | solution.py:302
  11.1 6.0 %collective-permute-done.1 = bf16[1024,256]{1,0:T(8,128)(2,1)S(1)} collective-permute-done((bf16[1024,256]{1,0:T(8,128)(2,1)S(1)}, bf16[1024,256]{1,0:T(8,128)(2,1)S(1)}, u32[]{:S(2)}, u32[]{:S(2)}) %collective-permute-start.1) | collective-permute-done | bytes 524320 | tf_op jit(solution)/shard_map/ppermute | solution.py:329
  17.2 2.8 %collective-permute-start.4 = (bf16[128,1024]{1,0:T(8,128)(2,1)S(1)}, bf16[128,1024]{1,0:T(8,128)(2,1)}, u32[]{:S(2)}, u32[]{:S(2)}) collective-permute-start(bf16[128,1024]{1,0:T(8,128)(2,1)S(1)} %get-tuple-element.33), channel_id=1, source_target_pairs={{0,48},{16,0},{32,16},{48,32},{1,49},{17,1},{33,17},{49,33},{2,50}... | collective-permute-start | bytes 786440 | tf_op jit(solution)/shard_map/ppermute | solution.py:302
  20.0 6.7 %all-to-all-start = ((bf16[8,3,128,256]{3,2,1,0:T(8,128)(2,1)}), bf16[8,3,128,256]{3,2,1,0:T(8,128)(2,1)S(1)}, u32[]{:S(2)}, u32[]{:S(2)}) async-start(bf16[8,3,128,256]{3,2,1,0:T(8,128)(2,1)} %pack_qkv.1), calls=%async_computation | async-start | bytes 3145728 | tf_op jit(solution)/shard_map/all_to_all | solution.py:310
  26.7 0.5 collective-permute-start.6
  27.2 1.0 constant_dynamic-update-slice_fusion.2
  28.1 1.0 constant_dynamic-update-slice_fusion.1
  29.1 1.0 constant_dynamic-update-slice_fusion.g_ref.refs_4_
  30.1 1.3 maximum_bitcast_fusion
  31.5 1.8 %pad_maximum_fusion.w_ref.refs_4_ = bf16[4,2048,256]{2,1,0:T(8,128)(2,1)S(1)} fusion(bf16[1,2048,256]{2,1,0:T(8,128)(2,1)S(1)} %maximum_bitcast_fusion.1, bf16[1,2048,256]{2,1,0:T(8,128)(2,1)S(1)} %maximum_bitcast_fusion, bf16[1,2048,256]{2,1,0:T(8,128)(2,1)} %bitcast.5, bf16[1,2048,256]{2,1,0:T(8,128)(2,1)} %bitcast.4), kind=kLoop, calls=%fused_computation | loop fusion | flops 6291456 | bytes 8388608 | tf_op jit(solution)/shard_map/stack | solution.py:338
  33.3 5.5 %grad_attended.1 = (bf16[8,128,256]{2,1,0:T(8,128)(2,1)S(1)}, bf16[8,128,256]{2,1,0:T(8,128)(2,1)}, bf16[8,128,256]{2,1,0:T(8,128)(2,1)}, bf16[8,128,256]{2,1,0:T(8,128)(2,1)}) custom-call(bf16[512,1024]{1,0:T(8,128)(2,1)S(1)} %constant_dynamic-update-slice_fusion.g_ref.refs_4_, bf16[4,2048,256]{2,1,0:T(8,128)(2,1)S(1)} %pad_maximum_fusion.w_ref.refs_4_), custom_call_target="tpu_custom_call" | custom-call | flops 2147483648 | bytes 6291456 | tf_op jit(solution)/shard_map/grad_attended/pallas_call | solution.py:211
  38.8 0.8 copy-done.10
  39.7 0.9 collective-permute-start.8
  40.6 0.8 collective-permute-start.9
  41.3 0.9 collective-permute-start.10
  42.2 6.2 %all-to-all-done.q_ref.k_ref.v_ref = bf16[8,3,128,256]{3,2,1,0:T(8,128)(2,1)S(1)} async-done(((bf16[8,3,128,256]{3,2,1,0:T(8,128)(2,1)}), bf16[8,3,128,256]{3,2,1,0:T(8,128)(2,1)S(1)}, u32[]{:S(2)}, u32[]{:S(2)}) %all-to-all-start) | async-done | bytes 1572896 | tf_op jit(solution)/shard_map/all_to_all | solution.py:310
  48.4 3.5 %attend.1 = (bf16[8,128,256]{2,1,0:T(8,128)(2,1)S(1)}, f32[2,1,1024]{2,1,0:T(1,128)S(1)}) custom-call(bf16[8,3,128,256]{3,2,1,0:T(8,128)(2,1)S(1)} %all-to-all-done.q_ref.k_ref.v_ref, bf16[8,3,128,256]{3,2,1,0:T(8,128)(2,1)S(1)} %all-to-all-done.q_ref.k_ref.v_ref, bf16[8,3,128,256]{3,2,1,0:T(8,128)(2,1)S(1)} %all-to-all-done.q_ref.k_ref.v_ref), custom_call_target="tpu_custom_call" | custom-call | flops 1073741824 | bytes 2097152 | tf_op jit(solution)/shard_map/attend/pallas_call | solution.py:127
  52.0 0.8 copy-done.12
  52.7 3.5 %all-to-all-start.1 = ((bf16[8,128,256]{2,1,0:T(8,128)(2,1)}), bf16[8,128,256]{2,1,0:T(8,128)(2,1)S(1)}, u32[]{:S(2)}, u32[]{:S(2)}) async-start(bf16[8,128,256]{2,1,0:T(8,128)(2,1)} %copy-done.12), calls=%async_computation.1 | async-start | bytes 1048576 | tf_op jit(solution)/shard_map/all_to_all | solution.py:310
  56.3 1.0 collective-permute-done.9
  57.2 10.0 %collective-permute-done.10 = bf16[8,128,256]{2,1,0:T(8,128)(2,1)} collective-permute-done((bf16[8,128,256]{2,1,0:T(8,128)(2,1)}, bf16[8,128,256]{2,1,0:T(8,128)(2,1)}, u32[]{:S(2)}, u32[]{:S(2)}) %collective-permute-start.10) | collective-permute-done | bytes 524320 | tf_op jit(solution)/shard_map/ppermute | solution.py:302
  67.2 1.0 collective-permute-start.13
  68.3 0.8 collective-permute-start.12
  69.1 0.9 collective-permute-start.11
  70.0 1.8 %add_convert_fusion = bf16[8,128,256]{2,1,0:T(8,128)(2,1)S(1)} fusion(bf16[8,128,256]{2,1,0:T(8,128)(2,1)} %collective-permute-done.10, bf16[8,128,256]{2,1,0:T(8,128)(2,1)} %collective-permute-done.9, bf16[8,128,256]{2,1,0:T(8,128)(2,1)} %collective-permute-done.8, bf16[8,128,256]{2,1,0:T(8,128)(2,1)} %copy-done.10), kind=kLoop, calls=%fused_computation.4 | loop fusion | flops 2097152 | bytes 2621440 | tf_op jit(solution)/shard_map/convert_element_type | solution.py:345
  71.8 17.6 %all_to_all.20.g_ref = bf16[8,128,256]{2,1,0:T(8,128)(2,1)} all-to-all(bf16[8,128,256]{2,1,0:T(8,128)(2,1)S(1)} %add_convert_fusion), channel_id=1, replica_groups=mesh['yl'=2,'x'=4,'core'=2,'z'=4,'yh'=2] {'z','yh'}, dimensions={0} | all-to-all | bytes 1048576 | tf_op jit(solution)/shard_map/all_to_all | solution.py:310
  89.4 4.4 %collective-permute-done.11.refs_1_ = bf16[8,128,256]{2,1,0:T(8,128)(2,1)S(1)} collective-permute-done((bf16[8,128,256]{2,1,0:T(8,128)(2,1)S(1)}, bf16[8,128,256]{2,1,0:T(8,128)(2,1)S(1)}, u32[]{:S(2)}, u32[]{:S(2)}) %collective-permute-start.11) | collective-permute-done | bytes 524320 | tf_op jit(solution)/shard_map/ppermute | solution.py:302
  93.8 1.7 %weight_parts.2 = bf16[2,8,256,256]{3,2,1,0:T(8,128)(2,1)S(1)} custom-call(bf16[8,128,256]{2,1,0:T(8,128)(2,1)S(1)} %all-to-all-done.1.refs_0_, bf16[8,128,256]{2,1,0:T(8,128)(2,1)S(1)} %collective-permute-done.11.refs_1_, bf16[8,128,256]{2,1,0:T(8,128)(2,1)S(1)} %collective-permute-done.12.refs_2_, ...), custom_call_target="tpu_custom_call" | custom-call | flops 1073741824 | bytes 5242880 | tf_op jit(solution)/shard_map/weight_parts/pallas_call | solution.py:254
  95.6 4.1 %collective-permute-done.17.refs_5_ = bf16[2,8,256,256]{3,2,1,0:T(8,128)(2,1)S(1)} collective-permute-done((bf16[2,8,256,256]{3,2,1,0:T(8,128)(2,1)S(1)}, bf16[2,8,256,256]{3,2,1,0:T(8,128)(2,1)S(1)}, u32[]{:S(2)}, u32[]{:S(2)}) %collective-permute-start.17) | collective-permute-done | bytes 2097184 | tf_op jit(solution)/shard_map/ppermute | solution.py:306
  99.8 1.9 %weight_parts.3 = bf16[2,8,256,256]{3,2,1,0:T(8,128)(2,1)S(1)} custom-call(bf16[8,128,256]{2,1,0:T(8,128)(2,1)S(1)} %all-to-all-done.1.refs_0_, bf16[8,128,256]{2,1,0:T(8,128)(2,1)S(1)} %collective-permute-done.11.refs_1_, bf16[8,128,256]{2,1,0:T(8,128)(2,1)S(1)} %collective-permute-done.12.refs_2_, ...), custom_call_target="tpu_custom_call" | custom-call | flops 1073741824 | bytes 5242880 | tf_op jit(solution)/shard_map/weight_parts/pallas_call | solution.py:254
  101.7 1.4 copy-done
  103.1 8.4 %all-to-all-start.3 = ((bf16[16,256,256]{2,1,0:T(8,128)(2,1)}), bf16[16,256,256]{2,1,0:T(8,128)(2,1)}, u32[]{:S(2)}, u32[]{:S(2)}) async-start(bf16[16,256,256]{2,1,0:T(8,128)(2,1)} %bitcast.15), calls=%async_computation.3 | async-start | bytes 4194304 | tf_op jit(solution)/shard_map/all_to_all | solution.py:310
  111.5 1.0 copy-done.11
  112.5 8.3 %attend_back.1 = (bf16[1024,256]{1,0:T(8,128)(2,1)}, bf16[1024,256]{1,0:T(8,128)(2,1)}, bf16[1024,256]{1,0:T(8,128)(2,1)}) custom-call(bf16[8,3,128,256]{3,2,1,0:T(8,128)(2,1)S(1)} %all-to-all-done.q_ref.k_ref.v_ref, bf16[8,3,128,256]{3,2,1,0:T(8,128)(2,1)S(1)} %all-to-all-done.q_ref.k_ref.v_ref, ...), custom_call_target="tpu_custom_call" | custom-call | flops 5368709120 | bytes 3670016 | tf_op jit(solution)/shard_map/attend_back/pallas_call | solution.py:179
  120.9 3.2 %project.1 = (bf16[128,1024]{1,0:T(8,128)(2,1)S(1)}, bf16[128,1024]{1,0:T(8,128)(2,1)S(1)}, bf16[128,1024]{1,0:T(8,128)(2,1)S(1)}, bf16[128,1024]{1,0:T(8,128)(2,1)S(1)}) custom-call(bf16[8,128,256]{2,1,0:T(8,128)(2,1)S(1)} %all-to-all-done.1.refs_0_, bf16[8,128,256]{2,1,0:T(8,128)(2,1)S(1)} %copy-done.8, bf16[8,128,256]{2,1,0:T(8,128)(2,1)S(1)} %copy-done.6, ...), custom_call_target="tpu_custom_call" | custom-call | flops 2147483648 | bytes 7340032 | tf_op jit(solution)/shard_map/project/pallas_call | solution.py:287
  124.1 1.3 collective-permute-start.14
  125.3 0.2 collective-permute-start.15
  125.5 0.8 collective-permute-start.16
  126.3 7.0 %collective-permute-done.14.refs_1_ = bf16[128,1024]{1,0:T(8,128)(2,1)S(1)} collective-permute-done((bf16[128,1024]{1,0:T(8,128)(2,1)S(1)}, bf16[128,1024]{1,0:T(8,128)(2,1)S(1)}, u32[]{:S(2)}, u32[]{:S(2)}) %collective-permute-start.14) | collective-permute-done | bytes 262176 | tf_op jit(solution)/shard_map/ppermute | solution.py:302
  133.4 2.7 %collective-permute-done.15.refs_2_ = bf16[128,1024]{1,0:T(8,128)(2,1)S(1)} collective-permute-done((bf16[128,1024]{1,0:T(8,128)(2,1)S(1)}, bf16[128,1024]{1,0:T(8,128)(2,1)S(1)}, u32[]{:S(2)}, u32[]{:S(2)}) %collective-permute-start.15) | collective-permute-done | bytes 262176 | tf_op jit(solution)/shard_map/ppermute | solution.py:302
  136.1 4.1 %collective-permute-done.16.refs_3_ = bf16[128,1024]{1,0:T(8,128)(2,1)S(1)} collective-permute-done((bf16[128,1024]{1,0:T(8,128)(2,1)S(1)}, bf16[128,1024]{1,0:T(8,128)(2,1)S(1)}, u32[]{:S(2)}, u32[]{:S(2)}) %collective-permute-start.16) | collective-permute-done | bytes 262176 | tf_op jit(solution)/shard_map/ppermute | solution.py:302
  140.2 1.1 place_projected.1
  141.3 3.9 %all-to-all-done.3 = bf16[16,256,256]{2,1,0:T(8,128)(2,1)} async-done(((bf16[16,256,256]{2,1,0:T(8,128)(2,1)}), bf16[16,256,256]{2,1,0:T(8,128)(2,1)}, u32[]{:S(2)}, u32[]{:S(2)}) %all-to-all-start.3) | async-done | bytes 2097184 | tf_op jit(solution)/shard_map/all_to_all | solution.py:310
  145.2 2.6 %convert_reduce_fusion = f32[256,256]{1,0:T(8,128)} fusion(bf16[16,256,256]{2,1,0:T(8,128)(2,1)} %all-to-all-done.3), kind=kLoop, calls=%fused_computation.1 | loop fusion | flops 2031616 | bytes 2359296 | tf_op jit(solution)/shard_map/reduce_sum | solution.py:351
  (48 shorter events, 0.6 us)
Async XLA Ops:
  0.6 4.7 %copy-start.15 = (bf16[1,128,2048]{2,1,0:T(8,128)(2,1)S(1)}, bf16[1,128,2048]{2,1,0:T(8,128)(2,1)}, u32[]{:S(2)}) copy-start(bf16[1,128,2048]{2,1,0:T(8,128)(2,1)} %param.7) | copy-start | bytes 1572868
  0.6 4.7 %copy-start.14 = (bf16[1,128,2048]{2,1,0:T(8,128)(2,1)S(1)}, bf16[1,128,2048]{2,1,0:T(8,128)(2,1)}, u32[]{:S(2)}) copy-start(bf16[1,128,2048]{2,1,0:T(8,128)(2,1)} %param.6) | copy-start | bytes 1572868
  0.7 4.7 %copy-start.13 = (bf16[1,128,2048]{2,1,0:T(8,128)(2,1)S(1)}, bf16[1,128,2048]{2,1,0:T(8,128)(2,1)}, u32[]{:S(2)}) copy-start(bf16[1,128,2048]{2,1,0:T(8,128)(2,1)} %param.5) | copy-start | bytes 1572868
  2.0 4.6 %copy-start.9 = (bf16[1,128,4096]{2,1,0:T(8,128)(2,1)S(1)}, bf16[1,128,4096]{2,1,0:T(8,128)(2,1)}, u32[]{:S(2)}) copy-start(bf16[1,128,4096]{2,1,0:T(8,128)(2,1)} %param.9) | copy-start | bytes 3145732
  2.1 15.1 %collective-permute-start.1 = (bf16[1024,256]{1,0:T(8,128)(2,1)S(1)}, bf16[1024,256]{1,0:T(8,128)(2,1)S(1)}, u32[]{:S(2)}, u32[]{:S(2)}) collective-permute-start(bf16[1024,256]{1,0:T(8,128)(2,1)S(1)} %get-tuple-element.51), channel_id=1, source_target_pairs={{0,65},{1,64},{64,1},{65,0},{2,67},{3,66},{66,3},{67,2},{4,69},{5,... | collective-permute-start | bytes 1572872 | tf_op jit(solution)/shard_map/ppermute | solution.py:329
  5.2 14.7 %collective-permute-start = (bf16[1024,256]{1,0:T(8,128)(2,1)S(1)}, bf16[1024,256]{1,0:T(8,128)(2,1)}, u32[]{:S(2)}, u32[]{:S(2)}) collective-permute-start(bf16[1024,256]{1,0:T(8,128)(2,1)S(1)} %get-tuple-element.52), channel_id=1, source_target_pairs={{0,64},{64,0},{1,65},{65,1},{2,66},{66,2},{3,67},{67,3},{4,68},{68... | collective-permute-start | bytes 1572872 | tf_op jit(solution)/shard_map/ppermute | solution.py:306
  6.8 19.8 %collective-permute-start.2 = (bf16[128,1024]{1,0:T(8,128)(2,1)S(1)}, bf16[128,1024]{1,0:T(8,128)(2,1)}, u32[]{:S(2)}, u32[]{:S(2)}) collective-permute-start(bf16[128,1024]{1,0:T(8,128)(2,1)S(1)} %get-tuple-element.31), channel_id=1, source_target_pairs={{0,16},{16,32},{32,48},{48,0},{1,17},{17,33},{33,49},{49,1},{2,18}... | collective-permute-start | bytes 786440 | tf_op jit(solution)/shard_map/ppermute | solution.py:302
  8.4 23.1 %collective-permute-start.5 = (bf16[2048,256]{1,0:T(8,128)(2,1)}, bf16[2048,256]{1,0:T(8,128)(2,1)}, u32[]{:S(2)}, u32[]{:S(2)}) collective-permute-start(bf16[2048,256]{1,0:T(8,128)(2,1)} %param.8), channel_id=1, source_target_pairs={{0,8},{8,0},{1,9},{9,1},{2,10},{10,2},{3,11},{11,3},{4,12},{12,4},... | collective-permute-start | bytes 3145736 | tf_op jit(solution)/shard_map/ppermute | solution.py:306
  8.4 19.7 %collective-permute-start.3 = (bf16[128,1024]{1,0:T(8,128)(2,1)S(1)}, bf16[128,1024]{1,0:T(8,128)(2,1)}, u32[]{:S(2)}, u32[]{:S(2)}) collective-permute-start(bf16[128,1024]{1,0:T(8,128)(2,1)S(1)} %get-tuple-element.32), channel_id=1, source_target_pairs={{0,32},{16,48},{32,0},{48,16},{1,33},{17,49},{33,1},{49,17},{2,34}... | collective-permute-start | bytes 786440 | tf_op jit(solution)/shard_map/ppermute | solution.py:302
  17.2 2.8 %copy-start.16 = (bf16[1024,256]{1,0:T(8,128)(2,1)}, bf16[1024,256]{1,0:T(8,128)(2,1)S(1)}, u32[]{:S(2)}) copy-start(bf16[1024,256]{1,0:T(8,128)(2,1)S(1)} %collective-permute-done.1) | copy-start | bytes 1572868
  17.2 11.9 %collective-permute-start.4 = (bf16[128,1024]{1,0:T(8,128)(2,1)S(1)}, bf16[128,1024]{1,0:T(8,128)(2,1)}, u32[]{:S(2)}, u32[]{:S(2)}) collective-permute-start(bf16[128,1024]{1,0:T(8,128)(2,1)S(1)} %get-tuple-element.33), channel_id=1, source_target_pairs={{0,48},{16,0},{32,16},{48,32},{1,49},{17,1},{33,17},{49,33},{2,50}... | collective-permute-start | bytes 786440 | tf_op jit(solution)/shard_map/ppermute | solution.py:302
  20.0 28.5 %all-to-all-start = ((bf16[8,3,128,256]{3,2,1,0:T(8,128)(2,1)}), bf16[8,3,128,256]{3,2,1,0:T(8,128)(2,1)S(1)}, u32[]{:S(2)}, u32[]{:S(2)}) async-start(bf16[8,3,128,256]{3,2,1,0:T(8,128)(2,1)} %pack_qkv.1), calls=%async_computation | async-start | bytes 3145728 | tf_op jit(solution)/shard_map/all_to_all | solution.py:310
  26.6 4.7 %collective-permute-start.7 = (bf16[1024,256]{1,0:T(8,128)(2,1)}, bf16[1024,256]{1,0:T(8,128)(2,1)S(1)}, u32[]{:S(2)}, u32[]{:S(2)}) collective-permute-start(bf16[1024,256]{1,0:T(8,128)(2,1)} %copy-done.16), channel_id=1, source_target_pairs={{0,8},{8,0},{1,9},{9,1},{2,10},{10,2},{3,11},{11,3},{4,12},{12,4},... | collective-permute-start | bytes 1572872 | tf_op jit(solution)/shard_map/ppermute | solution.py:306
  26.7 4.7 %collective-permute-start.6 = (bf16[1024,256]{1,0:T(8,128)(2,1)}, bf16[1024,256]{1,0:T(8,128)(2,1)S(1)}, u32[]{:S(2)}, u32[]{:S(2)}) collective-permute-start(bf16[1024,256]{1,0:T(8,128)(2,1)} %collective-permute-done), channel_id=1, source_target_pairs={{0,8},{8,0},{1,9},{9,1},{2,10},{10,2},{3,11},{11,3},{4,12},{12,4},... | collective-permute-start | bytes 1572872 | tf_op jit(solution)/shard_map/ppermute | solution.py:306
  33.3 5.6 %copy-start.1 = (bf16[4,2048,256]{2,1,0:T(8,128)(2,1)}, bf16[4,2048,256]{2,1,0:T(8,128)(2,1)S(1)}, u32[]{:S(2)}) copy-start(bf16[4,2048,256]{2,1,0:T(8,128)(2,1)S(1)} %pad_maximum_fusion.w_ref.refs_4_) | copy-start | bytes 12582916
  38.8 0.8 copy-start.10
  39.7 16.6 %collective-permute-start.8 = (bf16[8,128,256]{2,1,0:T(8,128)(2,1)}, bf16[8,128,256]{2,1,0:T(8,128)(2,1)}, u32[]{:S(2)}, u32[]{:S(2)}) collective-permute-start(bf16[8,128,256]{2,1,0:T(8,128)(2,1)} %get-tuple-element.35), channel_id=1, source_target_pairs={{0,48},{16,0},{32,16},{48,32},{1,49},{17,1},{33,17},{49,33},{2,50}... | collective-permute-start | bytes 1572872 | tf_op jit(solution)/shard_map/ppermute | solution.py:302
  40.6 16.7 %collective-permute-start.9 = (bf16[8,128,256]{2,1,0:T(8,128)(2,1)}, bf16[8,128,256]{2,1,0:T(8,128)(2,1)}, u32[]{:S(2)}, u32[]{:S(2)}) collective-permute-start(bf16[8,128,256]{2,1,0:T(8,128)(2,1)} %get-tuple-element.36), channel_id=1, source_target_pairs={{0,32},{16,48},{32,0},{48,16},{1,33},{17,49},{33,1},{49,17},{2,34}... | collective-permute-start | bytes 1572872 | tf_op jit(solution)/shard_map/ppermute | solution.py:302
  41.3 25.9 %collective-permute-start.10 = (bf16[8,128,256]{2,1,0:T(8,128)(2,1)}, bf16[8,128,256]{2,1,0:T(8,128)(2,1)}, u32[]{:S(2)}, u32[]{:S(2)}) collective-permute-start(bf16[8,128,256]{2,1,0:T(8,128)(2,1)} %get-tuple-element.37), channel_id=1, source_target_pairs={{0,16},{16,32},{32,48},{48,0},{1,17},{17,33},{33,49},{49,1},{2,18}... | collective-permute-start | bytes 1572872 | tf_op jit(solution)/shard_map/ppermute | solution.py:302
  51.9 0.8 copy-start.12
  52.7 14.5 %all-to-all-start.1 = ((bf16[8,128,256]{2,1,0:T(8,128)(2,1)}), bf16[8,128,256]{2,1,0:T(8,128)(2,1)S(1)}, u32[]{:S(2)}, u32[]{:S(2)}) async-start(bf16[8,128,256]{2,1,0:T(8,128)(2,1)} %copy-done.12), calls=%async_computation.1 | async-start | bytes 1048576 | tf_op jit(solution)/shard_map/all_to_all | solution.py:310
  67.2 22.1 %collective-permute-start.13 = (bf16[8,128,256]{2,1,0:T(8,128)(2,1)S(1)}, bf16[8,128,256]{2,1,0:T(8,128)(2,1)S(1)}, u32[]{:S(2)}, u32[]{:S(2)}) collective-permute-start(bf16[8,128,256]{2,1,0:T(8,128)(2,1)S(1)} %all-to-all-done.1.refs_0_), channel_id=1, source_target_pairs={{0,48},{16,0},{32,16},{48,32},{1,49},{17,1},{33,17},{49,33},{2,50}... | collective-permute-start | bytes 1572872 | tf_op jit(solution)/shard_map/ppermute | solution.py:302
  68.3 21.1 %collective-permute-start.12 = (bf16[8,128,256]{2,1,0:T(8,128)(2,1)S(1)}, bf16[8,128,256]{2,1,0:T(8,128)(2,1)S(1)}, u32[]{:S(2)}, u32[]{:S(2)}) collective-permute-start(bf16[8,128,256]{2,1,0:T(8,128)(2,1)S(1)} %all-to-all-done.1.refs_0_), channel_id=1, source_target_pairs={{0,32},{16,48},{32,0},{48,16},{1,33},{17,49},{33,1},{49,17},{2,34}... | collective-permute-start | bytes 1572872 | tf_op jit(solution)/shard_map/ppermute | solution.py:302
  69.1 24.7 %collective-permute-start.11 = (bf16[8,128,256]{2,1,0:T(8,128)(2,1)S(1)}, bf16[8,128,256]{2,1,0:T(8,128)(2,1)S(1)}, u32[]{:S(2)}, u32[]{:S(2)}) collective-permute-start(bf16[8,128,256]{2,1,0:T(8,128)(2,1)S(1)} %all-to-all-done.1.refs_0_), channel_id=1, source_target_pairs={{0,16},{16,32},{32,48},{48,0},{1,17},{17,33},{33,49},{49,1},{2,18}... | collective-permute-start | bytes 1572872 | tf_op jit(solution)/shard_map/ppermute | solution.py:302
  89.4 10.4 %copy-start.3 = (bf16[8,128,256]{2,1,0:T(8,128)(2,1)}, bf16[8,128,256]{2,1,0:T(8,128)(2,1)S(1)}, u32[]{:S(2)}) copy-start(bf16[8,128,256]{2,1,0:T(8,128)(2,1)S(1)} %collective-permute-done.13.refs_3_) | copy-start | bytes 1572868
  89.4 10.4 %copy-start.5 = (bf16[8,128,256]{2,1,0:T(8,128)(2,1)}, bf16[8,128,256]{2,1,0:T(8,128)(2,1)S(1)}, u32[]{:S(2)}) copy-start(bf16[8,128,256]{2,1,0:T(8,128)(2,1)S(1)} %collective-permute-done.12.refs_2_) | copy-start | bytes 1572868
  93.8 6.0 %copy-start.7 = (bf16[8,128,256]{2,1,0:T(8,128)(2,1)}, bf16[8,128,256]{2,1,0:T(8,128)(2,1)S(1)}, u32[]{:S(2)}) copy-start(bf16[8,128,256]{2,1,0:T(8,128)(2,1)S(1)} %collective-permute-done.11.refs_1_) | copy-start | bytes 1572868
  95.5 4.2 %collective-permute-start.17 = (bf16[2,8,256,256]{3,2,1,0:T(8,128)(2,1)S(1)}, bf16[2,8,256,256]{3,2,1,0:T(8,128)(2,1)S(1)}, u32[]{:S(2)}, u32[]{:S(2)}) collective-permute-start(bf16[2,8,256,256]{3,2,1,0:T(8,128)(2,1)S(1)} %weight_parts.2), channel_id=1, source_target_pairs={{0,8},{8,0},{1,9},{9,1},{2,10},{10,2},{3,11},{11,3},{4,12},{12,4},... | collective-permute-start | bytes 6291464 | tf_op jit(solution)/shard_map/ppermute | solution.py:306
  101.7 1.4 copy-start
  103.1 42.1 %all-to-all-start.3 = ((bf16[16,256,256]{2,1,0:T(8,128)(2,1)}), bf16[16,256,256]{2,1,0:T(8,128)(2,1)}, u32[]{:S(2)}, u32[]{:S(2)}) async-start(bf16[16,256,256]{2,1,0:T(8,128)(2,1)} %bitcast.15), calls=%async_computation.3 | async-start | bytes 4194304 | tf_op jit(solution)/shard_map/all_to_all | solution.py:310
  111.5 1.0 copy-start.11
  112.5 8.3 %copy-start.2 = (bf16[4,2048,256]{2,1,0:T(8,128)(2,1)S(1)}, bf16[4,2048,256]{2,1,0:T(8,128)(2,1)}, u32[]{:S(2)}) copy-start(bf16[4,2048,256]{2,1,0:T(8,128)(2,1)} %copy-done.1) | copy-start | bytes 12582916
  112.5 8.3 %copy-start.4 = (bf16[8,128,256]{2,1,0:T(8,128)(2,1)S(1)}, bf16[8,128,256]{2,1,0:T(8,128)(2,1)}, u32[]{:S(2)}) copy-start(bf16[8,128,256]{2,1,0:T(8,128)(2,1)} %copy-done.3) | copy-start | bytes 1572868
  112.5 8.3 %copy-start.6 = (bf16[8,128,256]{2,1,0:T(8,128)(2,1)S(1)}, bf16[8,128,256]{2,1,0:T(8,128)(2,1)}, u32[]{:S(2)}) copy-start(bf16[8,128,256]{2,1,0:T(8,128)(2,1)} %copy-done.5) | copy-start | bytes 1572868
  112.5 8.3 %copy-start.8 = (bf16[8,128,256]{2,1,0:T(8,128)(2,1)S(1)}, bf16[8,128,256]{2,1,0:T(8,128)(2,1)}, u32[]{:S(2)}) copy-start(bf16[8,128,256]{2,1,0:T(8,128)(2,1)} %copy-done.7) | copy-start | bytes 1572868
  124.1 9.3 %collective-permute-start.14 = (bf16[128,1024]{1,0:T(8,128)(2,1)S(1)}, bf16[128,1024]{1,0:T(8,128)(2,1)S(1)}, u32[]{:S(2)}, u32[]{:S(2)}) collective-permute-start(bf16[128,1024]{1,0:T(8,128)(2,1)S(1)} %get-tuple-element.45), channel_id=1, source_target_pairs={{0,48},{16,0},{32,16},{48,32},{1,49},{17,1},{33,17},{49,33},{2,50}... | collective-permute-start | bytes 786440 | tf_op jit(solution)/shard_map/ppermute | solution.py:302
  125.3 10.7 %collective-permute-start.15 = (bf16[128,1024]{1,0:T(8,128)(2,1)S(1)}, bf16[128,1024]{1,0:T(8,128)(2,1)S(1)}, u32[]{:S(2)}, u32[]{:S(2)}) collective-permute-start(bf16[128,1024]{1,0:T(8,128)(2,1)S(1)} %get-tuple-element.46), channel_id=1, source_target_pairs={{0,32},{16,48},{32,0},{48,16},{1,33},{17,49},{33,1},{49,17},{2,34}... | collective-permute-start | bytes 786440 | tf_op jit(solution)/shard_map/ppermute | solution.py:302
  125.5 14.7 %collective-permute-start.16 = (bf16[128,1024]{1,0:T(8,128)(2,1)S(1)}, bf16[128,1024]{1,0:T(8,128)(2,1)S(1)}, u32[]{:S(2)}, u32[]{:S(2)}) collective-permute-start(bf16[128,1024]{1,0:T(8,128)(2,1)S(1)} %get-tuple-element.47), channel_id=1, source_target_pairs={{0,16},{16,32},{32,48},{48,0},{1,17},{17,33},{33,49},{49,1},{2,18}... | collective-permute-start | bytes 786440 | tf_op jit(solution)/shard_map/ppermute | solution.py:302

commit v4 on v3

--- a/solution.py
+++ b/solution.py
@@ -340,7 +340,7 @@
 
     attended, lse = attend(after(qkv, *parts))
     parts = [parts[0]] + [shift_x(parts[s], -s) for s in range(1, X)]
-    attended = after(exchange(attended), *parts)
+    attended = after(exchange(attended), *parts[1:3])
     rows = [attended] + [shift_x(attended, s) for s in range(1, X)]
     grad_attended = exchange(f32_sum(*parts).astype(jnp.bfloat16))
 

time: 148 us -> 148 us (level)
    all_to_all x3, waiting for transfers between devices: 10.1 us -> 20.1 us  [exchange(): return lax.all_to_all(array, axes, 0, 0, tiled=False)]
    ppermute x12, waiting for transfers between devices: 29.3 us -> 19.8 us  [shift_x(): return lax.ppermute(array, 'x', [(i, (i + shift) % X) for i in range(X)])]
  transfers between devices with their start and end apart: 21 -> 21, of which waited for: 10 -> 11; matrix products, arithmetic and copies ran while one was open for 5% -> 5% of each run, Pallas kernels for 16% -> 16%
where the time goes in v4:
time: 148 us; the launch traced here: 147 us
  waiting for transfers between devices  50.1 us (34%)
  starting transfers between devices  37.2 us (25%)
  Pallas kernels  26.7 us (18%)
  blocking collectives  16.2 us (11%)
  local copies, waits for them, and re-layouts  8.42 us (6%)
  other arithmetic  7.53 us (5%)
    all_to_all x3, waiting for transfers between devices, exchange(): return lax.all_to_all(array, axes, 0, 0, tiled=False)  20.1 us
    ppermute x12, waiting for transfers between devices, shift_x(): return lax.ppermute(array, 'x', [(i, (i + shift) % X) for i in range(X)])  19.8 us
    all_to_all x3, starting transfers between devices, exchange(): return lax.all_to_all(array, axes, 0, 0, tiled=False)  18.6 us
    all_to_all x1, blocking collectives, exchange(): return lax.all_to_all(array, axes, 0, 0, tiled=False)  16.2 us
    ppermute x12, starting transfers between devices, shift_x(): return lax.ppermute(array, 'x', [(i, (i + shift) % X) for i in range(X)])  14.7 us
    pallas_call x1, Pallas kernels, attend_back(): pl.pallas_call(body, grid=(heads,), out_shape=[out] * 3, in_specs=[head_s...  8.31 us
    unnamed x37, local copies, waits for them, and re-layouts  6.07 us
    ppermute x1, waiting for transfers between devices, shards(): lax.ppermute(out_weight[half:], ('yl', 'yh'), [(i, 3 - i) for i in range(...  6.04 us
  transfers between devices with their start and end apart: 21, of which 11 were waited for; matrix products, arithmetic and copies ran while one was open for 5% of the time, Pallas kernels for 16%

profile of v4, /device:TPU:0, one launch (start us, length us, event | category | flops | bytes accessed | tf_op | source)
XLA Modules:
  0.0 147.1 jit_solution(15777417886310314754)
XLA Ops:
  0.7 1.4 fusion
  2.1 3.2 %collective-permute-start.1 = (bf16[1024,256]{1,0:T(8,128)(2,1)S(1)}, bf16[1024,256]{1,0:T(8,128)(2,1)S(1)}, u32[]{:S(2)}, u32[]{:S(2)}) collective-permute-start(bf16[1024,256]{1,0:T(8,128)(2,1)S(1)} %get-tuple-element.51), channel_id=1, source_target_pairs={{0,65},{1,64},{64,1},{65,0},{2,67},{3,66},{66,3},{67,2},{4,69},{5,... | collective-permute-start | bytes 1572872 | tf_op jit(solution)/shard_map/ppermute | solution.py:329
  5.4 1.3 pack_qkv.1
  6.8 1.6 %collective-permute-start.2 = (bf16[128,1024]{1,0:T(8,128)(2,1)S(1)}, bf16[128,1024]{1,0:T(8,128)(2,1)}, u32[]{:S(2)}, u32[]{:S(2)}) collective-permute-start(bf16[128,1024]{1,0:T(8,128)(2,1)S(1)} %get-tuple-element.31), channel_id=1, source_target_pairs={{0,16},{16,32},{32,48},{48,0},{1,17},{17,33},{33,49},{49,1},{2,18}... | collective-permute-start | bytes 786440 | tf_op jit(solution)/shard_map/ppermute | solution.py:302
  8.4 2.7 %collective-permute-start.3 = (bf16[128,1024]{1,0:T(8,128)(2,1)S(1)}, bf16[128,1024]{1,0:T(8,128)(2,1)}, u32[]{:S(2)}, u32[]{:S(2)}) collective-permute-start(bf16[128,1024]{1,0:T(8,128)(2,1)S(1)} %get-tuple-element.32), channel_id=1, source_target_pairs={{0,32},{16,48},{32,0},{48,16},{1,33},{17,49},{33,1},{49,17},{2,34}... | collective-permute-start | bytes 786440 | tf_op jit(solution)/shard_map/ppermute | solution.py:302
  11.1 6.0 %collective-permute-done.1 = bf16[1024,256]{1,0:T(8,128)(2,1)S(1)} collective-permute-done((bf16[1024,256]{1,0:T(8,128)(2,1)S(1)}, bf16[1024,256]{1,0:T(8,128)(2,1)S(1)}, u32[]{:S(2)}, u32[]{:S(2)}) %collective-permute-start.1) | collective-permute-done | bytes 524320 | tf_op jit(solution)/shard_map/ppermute | solution.py:329
  17.2 2.8 %collective-permute-start.4 = (bf16[128,1024]{1,0:T(8,128)(2,1)S(1)}, bf16[128,1024]{1,0:T(8,128)(2,1)}, u32[]{:S(2)}, u32[]{:S(2)}) collective-permute-start(bf16[128,1024]{1,0:T(8,128)(2,1)S(1)} %get-tuple-element.33), channel_id=1, source_target_pairs={{0,48},{16,0},{32,16},{48,32},{1,49},{17,1},{33,17},{49,33},{2,50}... | collective-permute-start | bytes 786440 | tf_op jit(solution)/shard_map/ppermute | solution.py:302
  20.0 6.7 %all-to-all-start = ((bf16[8,3,128,256]{3,2,1,0:T(8,128)(2,1)}), bf16[8,3,128,256]{3,2,1,0:T(8,128)(2,1)S(1)}, u32[]{:S(2)}, u32[]{:S(2)}) async-start(bf16[8,3,128,256]{3,2,1,0:T(8,128)(2,1)} %pack_qkv.1), calls=%async_computation | async-start | bytes 3145728 | tf_op jit(solution)/shard_map/all_to_all | solution.py:310
  26.7 0.5 collective-permute-start.6
  27.2 1.0 constant_dynamic-update-slice_fusion.2
  28.1 1.0 constant_dynamic-update-slice_fusion.1
  29.1 1.0 constant_dynamic-update-slice_fusion.g_ref.refs_4_
  30.1 1.3 maximum_bitcast_fusion
  31.5 1.8 %pad_maximum_fusion.w_ref.refs_4_ = bf16[4,2048,256]{2,1,0:T(8,128)(2,1)S(1)} fusion(bf16[1,2048,256]{2,1,0:T(8,128)(2,1)S(1)} %maximum_bitcast_fusion.1, bf16[1,2048,256]{2,1,0:T(8,128)(2,1)S(1)} %maximum_bitcast_fusion, bf16[1,2048,256]{2,1,0:T(8,128)(2,1)} %bitcast.5, bf16[1,2048,256]{2,1,0:T(8,128)(2,1)} %bitcast.4), kind=kLoop, calls=%fused_computation | loop fusion | flops 6291456 | bytes 8388608 | tf_op jit(solution)/shard_map/stack | solution.py:338
  33.3 5.5 %grad_attended.1 = (bf16[8,128,256]{2,1,0:T(8,128)(2,1)S(1)}, bf16[8,128,256]{2,1,0:T(8,128)(2,1)}, bf16[8,128,256]{2,1,0:T(8,128)(2,1)}, bf16[8,128,256]{2,1,0:T(8,128)(2,1)}) custom-call(bf16[512,1024]{1,0:T(8,128)(2,1)S(1)} %constant_dynamic-update-slice_fusion.g_ref.refs_4_, bf16[4,2048,256]{2,1,0:T(8,128)(2,1)S(1)} %pad_maximum_fusion.w_ref.refs_4_), custom_call_target="tpu_custom_call" | custom-call | flops 2147483648 | bytes 6291456 | tf_op jit(solution)/shard_map/grad_attended/pallas_call | solution.py:211
  38.8 0.8 copy-done.10
  39.7 0.9 collective-permute-start.8
  40.6 0.8 collective-permute-start.9
  41.3 0.9 collective-permute-start.13
  42.2 6.2 %all-to-all-done.q_ref.k_ref.v_ref = bf16[8,3,128,256]{3,2,1,0:T(8,128)(2,1)S(1)} async-done(((bf16[8,3,128,256]{3,2,1,0:T(8,128)(2,1)}), bf16[8,3,128,256]{3,2,1,0:T(8,128)(2,1)S(1)}, u32[]{:S(2)}, u32[]{:S(2)}) %all-to-all-start) | async-done | bytes 1572896 | tf_op jit(solution)/shard_map/all_to_all | solution.py:310
  48.4 3.5 %attend.1 = (bf16[8,128,256]{2,1,0:T(8,128)(2,1)S(1)}, f32[2,1,1024]{2,1,0:T(1,128)S(1)}) custom-call(bf16[8,3,128,256]{3,2,1,0:T(8,128)(2,1)S(1)} %all-to-all-done.q_ref.k_ref.v_ref, bf16[8,3,128,256]{3,2,1,0:T(8,128)(2,1)S(1)} %all-to-all-done.q_ref.k_ref.v_ref, bf16[8,3,128,256]{3,2,1,0:T(8,128)(2,1)S(1)} %all-to-all-done.q_ref.k_ref.v_ref), custom_call_target="tpu_custom_call" | custom-call | flops 1073741824 | bytes 2097152 | tf_op jit(solution)/shard_map/attend/pallas_call | solution.py:127
  52.0 0.8 copy-done.12
  52.7 3.5 %all-to-all-start.1 = ((bf16[8,128,256]{2,1,0:T(8,128)(2,1)}), bf16[8,128,256]{2,1,0:T(8,128)(2,1)S(1)}, u32[]{:S(2)}, u32[]{:S(2)}) async-start(bf16[8,128,256]{2,1,0:T(8,128)(2,1)} %copy-done.12), calls=%async_computation.1 | async-start | bytes 1048576 | tf_op jit(solution)/shard_map/all_to_all | solution.py:310
  56.3 1.0 collective-permute-done.9
  57.2 9.7 %all-to-all-done.1.refs_0_ = bf16[8,128,256]{2,1,0:T(8,128)(2,1)S(1)} async-done(((bf16[8,128,256]{2,1,0:T(8,128)(2,1)}), bf16[8,128,256]{2,1,0:T(8,128)(2,1)S(1)}, u32[]{:S(2)}, u32[]{:S(2)}) %all-to-all-start.1) | async-done | bytes 524320 | tf_op jit(solution)/shard_map/all_to_all | solution.py:310
  66.9 1.4 collective-permute-start.12
  68.3 0.8 collective-permute-start.11
  69.1 0.9 collective-permute-start.10
  70.0 1.8 %add_convert_fusion = bf16[8,128,256]{2,1,0:T(8,128)(2,1)S(1)} fusion(bf16[8,128,256]{2,1,0:T(8,128)(2,1)} %collective-permute-done.13, bf16[8,128,256]{2,1,0:T(8,128)(2,1)} %collective-permute-done.9, bf16[8,128,256]{2,1,0:T(8,128)(2,1)} %collective-permute-done.8, bf16[8,128,256]{2,1,0:T(8,128)(2,1)} %copy-done.10), kind=kLoop, calls=%fused_computation.4 | loop fusion | flops 2097152 | bytes 2621440 | tf_op jit(solution)/shard_map/convert_element_type | solution.py:345
  71.8 16.2 %all_to_all.20.g_ref = bf16[8,128,256]{2,1,0:T(8,128)(2,1)} all-to-all(bf16[8,128,256]{2,1,0:T(8,128)(2,1)S(1)} %add_convert_fusion), channel_id=1, replica_groups=mesh['yl'=2,'x'=4,'core'=2,'z'=4,'yh'=2] {'z','yh'}, dimensions={0} | all-to-all | bytes 1048576 | tf_op jit(solution)/shard_map/all_to_all | solution.py:310
  88.0 1.7 %collective-permute-done.12.refs_3_ = bf16[8,128,256]{2,1,0:T(8,128)(2,1)S(1)} collective-permute-done((bf16[8,128,256]{2,1,0:T(8,128)(2,1)S(1)}, bf16[8,128,256]{2,1,0:T(8,128)(2,1)S(1)}, u32[]{:S(2)}, u32[]{:S(2)}) %collective-permute-start.12) | collective-permute-done | bytes 524320 | tf_op jit(solution)/shard_map/ppermute | solution.py:302
  89.8 3.4 %collective-permute-done.10.refs_1_ = bf16[8,128,256]{2,1,0:T(8,128)(2,1)S(1)} collective-permute-done((bf16[8,128,256]{2,1,0:T(8,128)(2,1)S(1)}, bf16[8,128,256]{2,1,0:T(8,128)(2,1)S(1)}, u32[]{:S(2)}, u32[]{:S(2)}) %collective-permute-start.10) | collective-permute-done | bytes 524320 | tf_op jit(solution)/shard_map/ppermute | solution.py:302
  93.1 1.7 %weight_parts.2 = bf16[2,8,256,256]{3,2,1,0:T(8,128)(2,1)S(1)} custom-call(bf16[8,128,256]{2,1,0:T(8,128)(2,1)S(1)} %all-to-all-done.1.refs_0_, bf16[8,128,256]{2,1,0:T(8,128)(2,1)S(1)} %collective-permute-done.10.refs_1_, bf16[8,128,256]{2,1,0:T(8,128)(2,1)S(1)} %collective-permute-done.11.refs_2_, ...), custom_call_target="tpu_custom_call" | custom-call | flops 1073741824 | bytes 5242880 | tf_op jit(solution)/shard_map/weight_parts/pallas_call | solution.py:254
  94.9 4.1 %collective-permute-done.17.refs_5_ = bf16[2,8,256,256]{3,2,1,0:T(8,128)(2,1)S(1)} collective-permute-done((bf16[2,8,256,256]{3,2,1,0:T(8,128)(2,1)S(1)}, bf16[2,8,256,256]{3,2,1,0:T(8,128)(2,1)S(1)}, u32[]{:S(2)}, u32[]{:S(2)}) %collective-permute-start.17) | collective-permute-done | bytes 2097184 | tf_op jit(solution)/shard_map/ppermute | solution.py:306
  99.1 1.9 %weight_parts.3 = bf16[2,8,256,256]{3,2,1,0:T(8,128)(2,1)S(1)} custom-call(bf16[8,128,256]{2,1,0:T(8,128)(2,1)S(1)} %all-to-all-done.1.refs_0_, bf16[8,128,256]{2,1,0:T(8,128)(2,1)S(1)} %collective-permute-done.10.refs_1_, bf16[8,128,256]{2,1,0:T(8,128)(2,1)S(1)} %collective-permute-done.11.refs_2_, ...), custom_call_target="tpu_custom_call" | custom-call | flops 1073741824 | bytes 5242880 | tf_op jit(solution)/shard_map/weight_parts/pallas_call | solution.py:254
  101.0 1.4 copy-done
  102.4 8.4 %all-to-all-start.3 = ((bf16[16,256,256]{2,1,0:T(8,128)(2,1)}), bf16[16,256,256]{2,1,0:T(8,128)(2,1)}, u32[]{:S(2)}, u32[]{:S(2)}) async-start(bf16[16,256,256]{2,1,0:T(8,128)(2,1)} %bitcast.15), calls=%async_computation.3 | async-start | bytes 4194304 | tf_op jit(solution)/shard_map/all_to_all | solution.py:310
  110.8 1.0 copy-done.11
  111.8 8.3 %attend_back.1 = (bf16[1024,256]{1,0:T(8,128)(2,1)}, bf16[1024,256]{1,0:T(8,128)(2,1)}, bf16[1024,256]{1,0:T(8,128)(2,1)}) custom-call(bf16[8,3,128,256]{3,2,1,0:T(8,128)(2,1)S(1)} %all-to-all-done.q_ref.k_ref.v_ref, bf16[8,3,128,256]{3,2,1,0:T(8,128)(2,1)S(1)} %all-to-all-done.q_ref.k_ref.v_ref, ...), custom_call_target="tpu_custom_call" | custom-call | flops 5368709120 | bytes 3670016 | tf_op jit(solution)/shard_map/attend_back/pallas_call | solution.py:179
  120.2 3.2 %project.1 = (bf16[128,1024]{1,0:T(8,128)(2,1)S(1)}, bf16[128,1024]{1,0:T(8,128)(2,1)S(1)}, bf16[128,1024]{1,0:T(8,128)(2,1)S(1)}, bf16[128,1024]{1,0:T(8,128)(2,1)S(1)}) custom-call(bf16[8,128,256]{2,1,0:T(8,128)(2,1)S(1)} %all-to-all-done.1.refs_0_, bf16[8,128,256]{2,1,0:T(8,128)(2,1)S(1)} %copy-done.8, bf16[8,128,256]{2,1,0:T(8,128)(2,1)S(1)} %copy-done.6, ...), custom_call_target="tpu_custom_call" | custom-call | flops 2147483648 | bytes 7340032 | tf_op jit(solution)/shard_map/project/pallas_call | solution.py:287
  123.4 1.0 collective-permute-start.14
  124.6 0.8 collective-permute-start.16
  125.5 7.2 %collective-permute-done.14.refs_1_ = bf16[128,1024]{1,0:T(8,128)(2,1)S(1)} collective-permute-done((bf16[128,1024]{1,0:T(8,128)(2,1)S(1)}, bf16[128,1024]{1,0:T(8,128)(2,1)S(1)}, u32[]{:S(2)}, u32[]{:S(2)}) %collective-permute-start.14) | collective-permute-done | bytes 262176 | tf_op jit(solution)/shard_map/ppermute | solution.py:302
  132.7 2.5 %collective-permute-done.15.refs_2_ = bf16[128,1024]{1,0:T(8,128)(2,1)S(1)} collective-permute-done((bf16[128,1024]{1,0:T(8,128)(2,1)S(1)}, bf16[128,1024]{1,0:T(8,128)(2,1)S(1)}, u32[]{:S(2)}, u32[]{:S(2)}) %collective-permute-start.15) | collective-permute-done | bytes 262176 | tf_op jit(solution)/shard_map/ppermute | solution.py:302
  135.1 4.1 %collective-permute-done.16.refs_3_ = bf16[128,1024]{1,0:T(8,128)(2,1)S(1)} collective-permute-done((bf16[128,1024]{1,0:T(8,128)(2,1)S(1)}, bf16[128,1024]{1,0:T(8,128)(2,1)S(1)}, u32[]{:S(2)}, u32[]{:S(2)}) %collective-permute-start.16) | collective-permute-done | bytes 262176 | tf_op jit(solution)/shard_map/ppermute | solution.py:302
  139.3 1.1 place_projected.1
  140.4 4.1 %all-to-all-done.3 = bf16[16,256,256]{2,1,0:T(8,128)(2,1)} async-done(((bf16[16,256,256]{2,1,0:T(8,128)(2,1)}), bf16[16,256,256]{2,1,0:T(8,128)(2,1)}, u32[]{:S(2)}, u32[]{:S(2)}) %all-to-all-start.3) | async-done | bytes 2097184 | tf_op jit(solution)/shard_map/all_to_all | solution.py:310
  144.5 2.6 %convert_reduce_fusion = f32[256,256]{1,0:T(8,128)} fusion(bf16[16,256,256]{2,1,0:T(8,128)(2,1)} %all-to-all-done.3), kind=kLoop, calls=%fused_computation.1 | loop fusion | flops 2031616 | bytes 2359296 | tf_op jit(solution)/shard_map/reduce_sum | solution.py:351
  (48 shorter events, 0.8 us)
Async XLA Ops:
  0.6 4.7 %copy-start.15 = (bf16[1,128,2048]{2,1,0:T(8,128)(2,1)S(1)}, bf16[1,128,2048]{2,1,0:T(8,128)(2,1)}, u32[]{:S(2)}) copy-start(bf16[1,128,2048]{2,1,0:T(8,128)(2,1)} %param.7) | copy-start | bytes 1572868
  0.6 4.7 %copy-start.14 = (bf16[1,128,2048]{2,1,0:T(8,128)(2,1)S(1)}, bf16[1,128,2048]{2,1,0:T(8,128)(2,1)}, u32[]{:S(2)}) copy-start(bf16[1,128,2048]{2,1,0:T(8,128)(2,1)} %param.6) | copy-start | bytes 1572868
  0.7 4.7 %copy-start.13 = (bf16[1,128,2048]{2,1,0:T(8,128)(2,1)S(1)}, bf16[1,128,2048]{2,1,0:T(8,128)(2,1)}, u32[]{:S(2)}) copy-start(bf16[1,128,2048]{2,1,0:T(8,128)(2,1)} %param.5) | copy-start | bytes 1572868
  2.0 4.6 %copy-start.9 = (bf16[1,128,4096]{2,1,0:T(8,128)(2,1)S(1)}, bf16[1,128,4096]{2,1,0:T(8,128)(2,1)}, u32[]{:S(2)}) copy-start(bf16[1,128,4096]{2,1,0:T(8,128)(2,1)} %param.9) | copy-start | bytes 3145732
  2.1 15.1 %collective-permute-start.1 = (bf16[1024,256]{1,0:T(8,128)(2,1)S(1)}, bf16[1024,256]{1,0:T(8,128)(2,1)S(1)}, u32[]{:S(2)}, u32[]{:S(2)}) collective-permute-start(bf16[1024,256]{1,0:T(8,128)(2,1)S(1)} %get-tuple-element.51), channel_id=1, source_target_pairs={{0,65},{1,64},{64,1},{65,0},{2,67},{3,66},{66,3},{67,2},{4,69},{5,... | collective-permute-start | bytes 1572872 | tf_op jit(solution)/shard_map/ppermute | solution.py:329
  5.2 14.7 %collective-permute-start = (bf16[1024,256]{1,0:T(8,128)(2,1)S(1)}, bf16[1024,256]{1,0:T(8,128)(2,1)}, u32[]{:S(2)}, u32[]{:S(2)}) collective-permute-start(bf16[1024,256]{1,0:T(8,128)(2,1)S(1)} %get-tuple-element.52), channel_id=1, source_target_pairs={{0,64},{64,0},{1,65},{65,1},{2,66},{66,2},{3,67},{67,3},{4,68},{68... | collective-permute-start | bytes 1572872 | tf_op jit(solution)/shard_map/ppermute | solution.py:306
  6.8 19.8 %collective-permute-start.2 = (bf16[128,1024]{1,0:T(8,128)(2,1)S(1)}, bf16[128,1024]{1,0:T(8,128)(2,1)}, u32[]{:S(2)}, u32[]{:S(2)}) collective-permute-start(bf16[128,1024]{1,0:T(8,128)(2,1)S(1)} %get-tuple-element.31), channel_id=1, source_target_pairs={{0,16},{16,32},{32,48},{48,0},{1,17},{17,33},{33,49},{49,1},{2,18}... | collective-permute-start | bytes 786440 | tf_op jit(solution)/shard_map/ppermute | solution.py:302
  8.4 23.1 %collective-permute-start.5 = (bf16[2048,256]{1,0:T(8,128)(2,1)}, bf16[2048,256]{1,0:T(8,128)(2,1)}, u32[]{:S(2)}, u32[]{:S(2)}) collective-permute-start(bf16[2048,256]{1,0:T(8,128)(2,1)} %param.8), channel_id=1, source_target_pairs={{0,8},{8,0},{1,9},{9,1},{2,10},{10,2},{3,11},{11,3},{4,12},{12,4},... | collective-permute-start | bytes 3145736 | tf_op jit(solution)/shard_map/ppermute | solution.py:306
  8.4 19.7 %collective-permute-start.3 = (bf16[128,1024]{1,0:T(8,128)(2,1)S(1)}, bf16[128,1024]{1,0:T(8,128)(2,1)}, u32[]{:S(2)}, u32[]{:S(2)}) collective-permute-start(bf16[128,1024]{1,0:T(8,128)(2,1)S(1)} %get-tuple-element.32), channel_id=1, source_target_pairs={{0,32},{16,48},{32,0},{48,16},{1,33},{17,49},{33,1},{49,17},{2,34}... | collective-permute-start | bytes 786440 | tf_op jit(solution)/shard_map/ppermute | solution.py:302
  17.2 2.8 %copy-start.16 = (bf16[1024,256]{1,0:T(8,128)(2,1)}, bf16[1024,256]{1,0:T(8,128)(2,1)S(1)}, u32[]{:S(2)}) copy-start(bf16[1024,256]{1,0:T(8,128)(2,1)S(1)} %collective-permute-done.1) | copy-start | bytes 1572868
  17.2 11.9 %collective-permute-start.4 = (bf16[128,1024]{1,0:T(8,128)(2,1)S(1)}, bf16[128,1024]{1,0:T(8,128)(2,1)}, u32[]{:S(2)}, u32[]{:S(2)}) collective-permute-start(bf16[128,1024]{1,0:T(8,128)(2,1)S(1)} %get-tuple-element.33), channel_id=1, source_target_pairs={{0,48},{16,0},{32,16},{48,32},{1,49},{17,1},{33,17},{49,33},{2,50}... | collective-permute-start | bytes 786440 | tf_op jit(solution)/shard_map/ppermute | solution.py:302
  20.0 28.5 %all-to-all-start = ((bf16[8,3,128,256]{3,2,1,0:T(8,128)(2,1)}), bf16[8,3,128,256]{3,2,1,0:T(8,128)(2,1)S(1)}, u32[]{:S(2)}, u32[]{:S(2)}) async-start(bf16[8,3,128,256]{3,2,1,0:T(8,128)(2,1)} %pack_qkv.1), calls=%async_computation | async-start | bytes 3145728 | tf_op jit(solution)/shard_map/all_to_all | solution.py:310
  26.6 4.7 %collective-permute-start.7 = (bf16[1024,256]{1,0:T(8,128)(2,1)}, bf16[1024,256]{1,0:T(8,128)(2,1)S(1)}, u32[]{:S(2)}, u32[]{:S(2)}) collective-permute-start(bf16[1024,256]{1,0:T(8,128)(2,1)} %copy-done.16), channel_id=1, source_target_pairs={{0,8},{8,0},{1,9},{9,1},{2,10},{10,2},{3,11},{11,3},{4,12},{12,4},... | collective-permute-start | bytes 1572872 | tf_op jit(solution)/shard_map/ppermute | solution.py:306
  26.7 4.7 %collective-permute-start.6 = (bf16[1024,256]{1,0:T(8,128)(2,1)}, bf16[1024,256]{1,0:T(8,128)(2,1)S(1)}, u32[]{:S(2)}, u32[]{:S(2)}) collective-permute-start(bf16[1024,256]{1,0:T(8,128)(2,1)} %collective-permute-done), channel_id=1, source_target_pairs={{0,8},{8,0},{1,9},{9,1},{2,10},{10,2},{3,11},{11,3},{4,12},{12,4},... | collective-permute-start | bytes 1572872 | tf_op jit(solution)/shard_map/ppermute | solution.py:306
  33.3 5.6 %copy-start.1 = (bf16[4,2048,256]{2,1,0:T(8,128)(2,1)}, bf16[4,2048,256]{2,1,0:T(8,128)(2,1)S(1)}, u32[]{:S(2)}) copy-start(bf16[4,2048,256]{2,1,0:T(8,128)(2,1)S(1)} %pad_maximum_fusion.w_ref.refs_4_) | copy-start | bytes 12582916
  38.8 0.8 copy-start.10
  39.7 16.6 %collective-permute-start.8 = (bf16[8,128,256]{2,1,0:T(8,128)(2,1)}, bf16[8,128,256]{2,1,0:T(8,128)(2,1)}, u32[]{:S(2)}, u32[]{:S(2)}) collective-permute-start(bf16[8,128,256]{2,1,0:T(8,128)(2,1)} %get-tuple-element.35), channel_id=1, source_target_pairs={{0,48},{16,0},{32,16},{48,32},{1,49},{17,1},{33,17},{49,33},{2,50}... | collective-permute-start | bytes 1572872 | tf_op jit(solution)/shard_map/ppermute | solution.py:302
  40.6 16.7 %collective-permute-start.9 = (bf16[8,128,256]{2,1,0:T(8,128)(2,1)}, bf16[8,128,256]{2,1,0:T(8,128)(2,1)}, u32[]{:S(2)}, u32[]{:S(2)}) collective-permute-start(bf16[8,128,256]{2,1,0:T(8,128)(2,1)} %get-tuple-element.36), channel_id=1, source_target_pairs={{0,32},{16,48},{32,0},{48,16},{1,33},{17,49},{33,1},{49,17},{2,34}... | collective-permute-start | bytes 1572872 | tf_op jit(solution)/shard_map/ppermute | solution.py:302
  41.3 28.7 %collective-permute-start.13 = (bf16[8,128,256]{2,1,0:T(8,128)(2,1)}, bf16[8,128,256]{2,1,0:T(8,128)(2,1)}, u32[]{:S(2)}, u32[]{:S(2)}) collective-permute-start(bf16[8,128,256]{2,1,0:T(8,128)(2,1)} %get-tuple-element.37), channel_id=1, source_target_pairs={{0,16},{16,32},{32,48},{48,0},{1,17},{17,33},{33,49},{49,1},{2,18}... | collective-permute-start | bytes 1572872 | tf_op jit(solution)/shard_map/ppermute | solution.py:302
  51.9 0.8 copy-start.12
  52.7 14.2 %all-to-all-start.1 = ((bf16[8,128,256]{2,1,0:T(8,128)(2,1)}), bf16[8,128,256]{2,1,0:T(8,128)(2,1)S(1)}, u32[]{:S(2)}, u32[]{:S(2)}) async-start(bf16[8,128,256]{2,1,0:T(8,128)(2,1)} %copy-done.12), calls=%async_computation.1 | async-start | bytes 1048576 | tf_op jit(solution)/shard_map/all_to_all | solution.py:310
  66.9 22.8 %collective-permute-start.12 = (bf16[8,128,256]{2,1,0:T(8,128)(2,1)S(1)}, bf16[8,128,256]{2,1,0:T(8,128)(2,1)S(1)}, u32[]{:S(2)}, u32[]{:S(2)}) collective-permute-start(bf16[8,128,256]{2,1,0:T(8,128)(2,1)S(1)} %all-to-all-done.1.refs_0_), channel_id=1, source_target_pairs={{0,48},{16,0},{32,16},{48,32},{1,49},{17,1},{33,17},{49,33},{2,50}... | collective-permute-start | bytes 1572872 | tf_op jit(solution)/shard_map/ppermute | solution.py:302
  68.3 21.5 %collective-permute-start.11 = (bf16[8,128,256]{2,1,0:T(8,128)(2,1)S(1)}, bf16[8,128,256]{2,1,0:T(8,128)(2,1)S(1)}, u32[]{:S(2)}, u32[]{:S(2)}) collective-permute-start(bf16[8,128,256]{2,1,0:T(8,128)(2,1)S(1)} %all-to-all-done.1.refs_0_), channel_id=1, source_target_pairs={{0,32},{16,48},{32,0},{48,16},{1,33},{17,49},{33,1},{49,17},{2,34}... | collective-permute-start | bytes 1572872 | tf_op jit(solution)/shard_map/ppermute | solution.py:302
  69.1 24.0 %collective-permute-start.10 = (bf16[8,128,256]{2,1,0:T(8,128)(2,1)S(1)}, bf16[8,128,256]{2,1,0:T(8,128)(2,1)S(1)}, u32[]{:S(2)}, u32[]{:S(2)}) collective-permute-start(bf16[8,128,256]{2,1,0:T(8,128)(2,1)S(1)} %all-to-all-done.1.refs_0_), channel_id=1, source_target_pairs={{0,16},{16,32},{32,48},{48,0},{1,17},{17,33},{33,49},{49,1},{2,18}... | collective-permute-start | bytes 1572872 | tf_op jit(solution)/shard_map/ppermute | solution.py:302
  89.7 9.3 %copy-start.3 = (bf16[8,128,256]{2,1,0:T(8,128)(2,1)}, bf16[8,128,256]{2,1,0:T(8,128)(2,1)S(1)}, u32[]{:S(2)}) copy-start(bf16[8,128,256]{2,1,0:T(8,128)(2,1)S(1)} %collective-permute-done.12.refs_3_) | copy-start | bytes 1572868
  89.7 9.3 %copy-start.5 = (bf16[8,128,256]{2,1,0:T(8,128)(2,1)}, bf16[8,128,256]{2,1,0:T(8,128)(2,1)S(1)}, u32[]{:S(2)}) copy-start(bf16[8,128,256]{2,1,0:T(8,128)(2,1)S(1)} %collective-permute-done.11.refs_2_) | copy-start | bytes 1572868
  93.1 6.0 %copy-start.7 = (bf16[8,128,256]{2,1,0:T(8,128)(2,1)}, bf16[8,128,256]{2,1,0:T(8,128)(2,1)S(1)}, u32[]{:S(2)}) copy-start(bf16[8,128,256]{2,1,0:T(8,128)(2,1)S(1)} %collective-permute-done.10.refs_1_) | copy-start | bytes 1572868
  94.8 4.2 %collective-permute-start.17 = (bf16[2,8,256,256]{3,2,1,0:T(8,128)(2,1)S(1)}, bf16[2,8,256,256]{3,2,1,0:T(8,128)(2,1)S(1)}, u32[]{:S(2)}, u32[]{:S(2)}) collective-permute-start(bf16[2,8,256,256]{3,2,1,0:T(8,128)(2,1)S(1)} %weight_parts.2), channel_id=1, source_target_pairs={{0,8},{8,0},{1,9},{9,1},{2,10},{10,2},{3,11},{11,3},{4,12},{12,4},... | collective-permute-start | bytes 6291464 | tf_op jit(solution)/shard_map/ppermute | solution.py:306
  101.0 1.4 copy-start
  102.4 42.1 %all-to-all-start.3 = ((bf16[16,256,256]{2,1,0:T(8,128)(2,1)}), bf16[16,256,256]{2,1,0:T(8,128)(2,1)}, u32[]{:S(2)}, u32[]{:S(2)}) async-start(bf16[16,256,256]{2,1,0:T(8,128)(2,1)} %bitcast.15), calls=%async_computation.3 | async-start | bytes 4194304 | tf_op jit(solution)/shard_map/all_to_all | solution.py:310
  110.8 1.0 copy-start.11
  111.8 8.3 %copy-start.2 = (bf16[4,2048,256]{2,1,0:T(8,128)(2,1)S(1)}, bf16[4,2048,256]{2,1,0:T(8,128)(2,1)}, u32[]{:S(2)}) copy-start(bf16[4,2048,256]{2,1,0:T(8,128)(2,1)} %copy-done.1) | copy-start | bytes 12582916
  111.8 8.3 %copy-start.4 = (bf16[8,128,256]{2,1,0:T(8,128)(2,1)S(1)}, bf16[8,128,256]{2,1,0:T(8,128)(2,1)}, u32[]{:S(2)}) copy-start(bf16[8,128,256]{2,1,0:T(8,128)(2,1)} %copy-done.3) | copy-start | bytes 1572868
  111.8 8.3 %copy-start.6 = (bf16[8,128,256]{2,1,0:T(8,128)(2,1)S(1)}, bf16[8,128,256]{2,1,0:T(8,128)(2,1)}, u32[]{:S(2)}) copy-start(bf16[8,128,256]{2,1,0:T(8,128)(2,1)} %copy-done.5) | copy-start | bytes 1572868
  111.8 8.3 %copy-start.8 = (bf16[8,128,256]{2,1,0:T(8,128)(2,1)S(1)}, bf16[8,128,256]{2,1,0:T(8,128)(2,1)}, u32[]{:S(2)}) copy-start(bf16[8,128,256]{2,1,0:T(8,128)(2,1)} %copy-done.7) | copy-start | bytes 1572868
  123.4 9.3 %collective-permute-start.14 = (bf16[128,1024]{1,0:T(8,128)(2,1)S(1)}, bf16[128,1024]{1,0:T(8,128)(2,1)S(1)}, u32[]{:S(2)}, u32[]{:S(2)}) collective-permute-start(bf16[128,1024]{1,0:T(8,128)(2,1)S(1)} %get-tuple-element.45), channel_id=1, source_target_pairs={{0,48},{16,0},{32,16},{48,32},{1,49},{17,1},{33,17},{49,33},{2,50}... | collective-permute-start | bytes 786440 | tf_op jit(solution)/shard_map/ppermute | solution.py:302
  124.4 10.8 %collective-permute-start.15 = (bf16[128,1024]{1,0:T(8,128)(2,1)S(1)}, bf16[128,1024]{1,0:T(8,128)(2,1)S(1)}, u32[]{:S(2)}, u32[]{:S(2)}) collective-permute-start(bf16[128,1024]{1,0:T(8,128)(2,1)S(1)} %get-tuple-element.46), channel_id=1, source_target_pairs={{0,32},{16,48},{32,0},{48,16},{1,33},{17,49},{33,1},{49,17},{2,34}... | collective-permute-start | bytes 786440 | tf_op jit(solution)/shard_map/ppermute | solution.py:302
  124.6 14.6 %collective-permute-start.16 = (bf16[128,1024]{1,0:T(8,128)(2,1)S(1)}, bf16[128,1024]{1,0:T(8,128)(2,1)S(1)}, u32[]{:S(2)}, u32[]{:S(2)}) collective-permute-start(bf16[128,1024]{1,0:T(8,128)(2,1)S(1)} %get-tuple-element.47), channel_id=1, source_target_pairs={{0,16},{16,32},{32,48},{48,0},{1,17},{17,33},{33,49},{49,1},{2,18}... | collective-permute-start | bytes 786440 | tf_op jit(solution)/shard_map/ppermute | solution.py:302
